TPU v7x, 32 devices: a whole 2x2x4 slice. The times are simulated.
32 devices in a mesh: grp: 8 (over z, x), tp: 4 (over y, core).
Axes of the slice: x: 2, y: 2, z: 4, core: 2. Of those that a mesh axis runs over, the one named last changes fastest.
Arguments:
- enc_in: bfloat16 [8, 1024, 1536], P('grp', 'tp'), may hold values from -36 to 36
- dec_in: bfloat16 [8, 576, 1536], P('grp', 'tp'), may hold values from -36 to 36
- dec_cot: bfloat16 [8, 576, 1536], P('grp', 'tp'), may hold values from -6 to 6
- enc_seg: int32 [8, 1, 1024], P('grp'), may hold values from 0 to 3, as said below
- dec_seg: int32 [8, 3, 192], P('grp'), may hold values from 0 to 3, as said below
- enc_norm1: bfloat16 [1536], P('grp'), may hold values from 0.25 to 1.75
- enc_wq: bfloat16 [1536, 768], P('grp', 'tp'), may hold values from -0.0625 to 0.0625
- enc_wk: bfloat16 [1536, 768], P('grp', 'tp'), may hold values from -0.0625 to 0.0625
- enc_wv: bfloat16 [1536, 768], P('grp', 'tp'), may hold values from -0.15625 to 0.15625
- enc_wo: bfloat16 [768, 1536], P('tp', 'grp'), may hold values from -1.75 to 1.75
- enc_table: bfloat16 [32, 12], P(None, 'tp'), may hold values from -4 to 4
- enc_norm2: bfloat16 [1536], P('grp'), may hold values from 0.25 to 1.75
- enc_wgate: bfloat16 [1536, 3968], P('grp', 'tp'), may hold values from -0.15625 to 0.15625
- enc_wup: bfloat16 [1536, 3968], P('grp', 'tp'), may hold values from -0.15625 to 0.15625
- enc_wdown: bfloat16 [3968, 1536], P('tp', 'grp'), may hold values from -0.09375 to 0.09375
- enc_normf: bfloat16 [1536], P('grp'), may hold values from 0.25 to 1.75
- dec_norm1: bfloat16 [1536], P('grp'), may hold values from 0.25 to 1.75
- dec_wq: bfloat16 [1536, 768], P('grp', 'tp'), may hold values from -0.0625 to 0.0625
- dec_wk: bfloat16 [1536, 768], P('grp', 'tp'), may hold values from -0.0625 to 0.0625
- dec_wv: bfloat16 [1536, 768], P('grp', 'tp'), may hold values from -0.15625 to 0.15625
- dec_wo: bfloat16 [768, 1536], P('tp', 'grp'), may hold values from -0.875 to 0.875
- dec_table: bfloat16 [32, 12], P(None, 'tp'), may hold values from -4 to 4
- dec_norm2: bfloat16 [1536], P('grp'), may hold values from 0.25 to 1.75
- cross_wq: bfloat16 [1536, 768], P('grp', 'tp'), may hold values from -0.0625 to 0.0625
- cross_wk: bfloat16 [1536, 768], P('grp', 'tp'), may hold values from -0.0625 to 0.0625
- cross_wv: bfloat16 [1536, 768], P('grp', 'tp'), may hold values from -0.15625 to 0.15625
- cross_wo: bfloat16 [768, 1536], P('tp', 'grp'), may hold values from -1.75 to 1.75
- dec_norm3: bfloat16 [1536], P('grp'), may hold values from 0.25 to 1.75
- dec_wgate: bfloat16 [1536, 3968], P('grp', 'tp'), may hold values from -0.15625 to 0.15625
- dec_wup: bfloat16 [1536, 3968], P('grp', 'tp'), may hold values from -0.15625 to 0.15625
- dec_wdown: bfloat16 [3968, 1536], P('tp', 'grp'), may hold values from -0.09375 to 0.09375
Outputs:
- dec_out: bfloat16 [8, 576, 1536], P('grp', 'tp')
- enc_grad: bfloat16 [8, 1024, 1536], P('grp', 'tp')
- dec_grad: bfloat16 [8, 576, 1536], P('grp', 'tp')
- grad_enc_norm1: float32 [1536], P('grp')
- grad_enc_wq: float32 [1536, 768], P('grp', 'tp')
- grad_enc_wk: float32 [1536, 768], P('grp', 'tp')
- grad_enc_wv: float32 [1536, 768], P('grp', 'tp')
- grad_enc_wo: float32 [768, 1536], P('tp', 'grp')
- grad_enc_table: float32 [32, 12], P(None, 'tp')
- grad_enc_norm2: float32 [1536], P('grp')
- grad_enc_wgate: float32 [1536, 3968], P('grp', 'tp')
- grad_enc_wup: float32 [1536, 3968], P('grp', 'tp')
- grad_enc_wdown: float32 [3968, 1536], P('tp', 'grp')
- grad_enc_normf: float32 [1536], P('grp')
- grad_dec_norm1: float32 [1536], P('grp')
- grad_dec_wq: float32 [1536, 768], P('grp', 'tp')
- grad_dec_wk: float32 [1536, 768], P('grp', 'tp')
- grad_dec_wv: float32 [1536, 768], P('grp', 'tp')
- grad_dec_wo: float32 [768, 1536], P('tp', 'grp')
- grad_dec_table: float32 [32, 12], P(None, 'tp')
- grad_dec_norm2: float32 [1536], P('grp')
- grad_cross_wq: float32 [1536, 768], P('grp', 'tp')
- grad_cross_wk: float32 [1536, 768], P('grp', 'tp')
- grad_cross_wv: float32 [1536, 768], P('grp', 'tp')
- grad_cross_wo: float32 [768, 1536], P('tp', 'grp')
- grad_dec_norm3: float32 [1536], P('grp')
- grad_dec_wgate: float32 [1536, 3968], P('grp', 'tp')
- grad_dec_wup: float32 [1536, 3968], P('grp', 'tp')
- grad_dec_wdown: float32 [3968, 1536], P('tp', 'grp')
Inputs may be any that keep to these rules, and one draw needn't show every extreme that they name: `enc_seg`: in each row the ids never fall, and each of 0 to 3 occurs. `dec_seg`: in each row the ids never fall, and each of 0 to 3 occurs.
All inputs are finite; a program needn't handle non-finite values.
Results may differ from a plain program's by a relative error of at most 0.04.
Values may be sent and summed in bfloat16 or wider, within the bound.
No kernel may reach another device: no remote copies, remote signals or barrier semaphores. Data moves between devices by JAX's collectives and lax.ppermute only.
A program may use at most 640 MiB of HBM per device.

v0:
```python
from functools import partial

import jax
import jax.numpy as jnp
import numpy as np
from jax import lax
from jax.sharding import PartitionSpec as P

HEAD_DIM = 64
BUCKETS = 32
MAX_DIST = 128
ENC_LEN = 1024
DEC_LEN = 192
ROWS = 1


EPSILON = 1e-06
NEG_FILL = -1e30
PRECISE = lax.Precision.HIGHEST


def for_sending(shard):
    return jax.tree.map(lambda a: a.astype(jnp.bfloat16) if a.dtype == jnp.float32 else a, shard)


def from_behind(value, axis, steps):
    count = lax.axis_size(axis)
    initial, last = (max(0, -steps), min(count, count - steps))
    return lax.ppermute(value, axis, [(source, source + steps) for source in range(initial, last)])


def bucket_of(relative, two_sided):
    bucket_count = BUCKETS
    shifted = relative * 0
    if two_sided:
        bucket_count = bucket_count // 2
        shifted = shifted + (relative > 0) * bucket_count
        distance = np.abs(relative)
    else:
        distance = np.maximum(-relative, 0)
    exact_span = bucket_count // 2
    log_ratio = np.log(np.maximum(distance, 1) / exact_span) / np.log(MAX_DIST / exact_span)
    farther = np.minimum(
        exact_span + np.floor(log_ratio * (bucket_count - exact_span) + 1e-09).astype(np.int32),
        bucket_count - 1,
    )
    return (shifted + np.where(distance < exact_span, distance, farther)).astype(np.int32)


def offset_table(length, two_sided):
    relative = np.arange(2 * length - 1) - (length - 1)
    return np.eye(BUCKETS, dtype=np.float32)[bucket_of(relative, two_sided)]


def skew(vectors, rows_count, cols_count):
    diag_count = rows_count + cols_count - 1
    repeated = jnp.tile(vectors, (1, rows_count))[
        :, rows_count - 1 : rows_count - 1 + rows_count * (diag_count - 1)
    ]
    return repeated.reshape(vectors.shape[0], rows_count, diag_count - 1)[:, :, :cols_count]


def unskew(grid, rows_count, cols_count):
    diag_count = rows_count + cols_count - 1
    padded = jnp.pad(grid, ((0, 0), (0, 0), (0, diag_count - 1 - cols_count)))
    flattened = jnp.pad(padded.reshape(grid.shape[0], -1), ((0, 0), (rows_count - 1, 1)))
    return jnp.sum(flattened.reshape(grid.shape[0], rows_count, diag_count), axis=1)


def rms_scale(hidden, gain_vec):
    return (
        hidden * lax.rsqrt(jnp.mean(hidden * hidden, axis=-1, keepdims=True) + EPSILON) * gain_vec
    )


def norm_backward(hidden, gain_vec, grad_out):
    normed, pullback = jax.vjp(rms_scale, hidden, gain_vec)
    return pullback(grad_out)


def only_when(flag, func, *operands):

    def skipped(*inner):
        return jax.tree.map(jnp.zeros_like, func(*inner))

    return lax.cond(flag, func, skipped, *operands)


def gather_tokens(values):
    return lax.all_gather(values, "tp", axis=0, tiled=True)


def reduce_tokens(values):
    return jax.tree.map(
        lambda part: part.astype(jnp.float32),
        lax.psum_scatter(for_sending(values), "tp", scatter_dimension=0, tiled=True),
    )


def owner_rows(grad, split_axis, groups):
    if split_axis == 0:
        return grad.reshape(groups, -1)
    return grad.reshape(grad.shape[0], groups, -1).transpose(1, 0, 2).reshape(groups, -1)


def shard_shape(grad, split_axis, groups):
    if split_axis == 0:
        return (grad.shape[0] // groups, grad.shape[1])
    return (grad.shape[0], grad.shape[1] // groups)


def pack_owned(grads, axes_list, groups):
    return jnp.concatenate(
        [owner_rows(grad, split_axis, groups) for grad, split_axis in zip(grads, axes_list)], axis=1
    )


def unpack_owned(flat_vec, grads, axes_list, groups):
    results = []
    offset = 0
    for grad, split_axis in zip(grads, axes_list):
        shape_here = shard_shape(grad, split_axis, groups)
        count = shape_here[0] * shape_here[1]
        results.append(flat_vec[offset : offset + count].reshape(shape_here))
        offset = offset + count
    return tuple(results)


def project(token_rows, weight):
    mixed = jnp.einsum(
        "bld,de->ble", token_rows, weight, preferred_element_type=jnp.float32
    ).astype(jnp.bfloat16)
    return mixed.reshape(token_rows.shape[0], token_rows.shape[1], -1, HEAD_DIM)


def block_scores(queries, key_rows, offsets, query_ids, key_ids, causal, row_start, block_len):
    key_len = key_rows.shape[1]
    scores = jnp.einsum(
        "bqhd,bkhd->bhqk",
        queries[:, row_start : row_start + block_len],
        key_rows,
        preferred_element_type=jnp.float32,
    )
    if offsets is not None:
        lowest = key_len - row_start - block_len
        scores = (
            scores
            + skew(offsets[:, lowest : lowest + block_len + key_len - 1], block_len, key_len)[None]
        )
    allowed = query_ids[:, row_start : row_start + block_len, None].astype(jnp.float32) == key_ids[
        :, None, :
    ].astype(jnp.float32)
    if causal:
        query_pos = row_start + jnp.arange(block_len)[:, None]
        key_pos = jnp.arange(key_len)[None, :]
        allowed = allowed & (key_pos <= query_pos)[None]
    return jnp.where(allowed[:, None], scores, NEG_FILL)


def attend_forward(queries, key_rows, value_rows, offsets, query_ids, key_ids, causal):
    query_len = queries.shape[1]
    block_len = min(query_len, 512)
    pieces, maxima, totals = ([], [], [])
    for row_start in range(0, query_len, block_len):
        scores = block_scores(
            queries, key_rows, offsets, query_ids, key_ids, causal, row_start, block_len
        )
        row_peak = jnp.max(scores, axis=-1, keepdims=True)
        exponent = jnp.exp(scores - row_peak)
        row_total = jnp.sum(exponent, axis=-1, keepdims=True)
        weights_bf = (exponent / row_total).astype(jnp.bfloat16)
        pieces.append(
            jnp.einsum(
                "bhqk,bkhd->bqhd", weights_bf, value_rows, preferred_element_type=jnp.float32
            ).astype(jnp.bfloat16)
        )
        maxima.append(row_peak)
        totals.append(row_total)
    return (
        jnp.concatenate(pieces, axis=1),
        jnp.concatenate(maxima, axis=2),
        jnp.concatenate(totals, axis=2),
    )


def attend_backward(
    queries, key_rows, value_rows, offsets, query_ids, key_ids, causal, maxima, totals, grad_out
):
    query_len = queries.shape[1]
    key_len = key_rows.shape[1]
    block_len = min(query_len, 512)
    grad_keys = jnp.zeros(key_rows.shape, jnp.float32)
    grad_values = jnp.zeros(value_rows.shape, jnp.float32)
    grad_offsets = None if offsets is None else jnp.zeros(offsets.shape, jnp.float32)
    pieces = []
    for row_start in range(0, query_len, block_len):
        row_end = row_start + block_len
        scores = block_scores(
            queries, key_rows, offsets, query_ids, key_ids, causal, row_start, block_len
        )
        weights_f = (
            jnp.exp(scores - maxima[:, :, row_start:row_end]) / totals[:, :, row_start:row_end]
        )
        grad_block = grad_out[:, row_start:row_end]
        grad_values = grad_values + jnp.einsum(
            "bhqk,bqhd->bkhd",
            weights_f.astype(jnp.bfloat16),
            grad_block,
            preferred_element_type=jnp.float32,
        )
        grad_weights = jnp.einsum(
            "bqhd,bkhd->bhqk", grad_block, value_rows, preferred_element_type=jnp.float32
        )
        grad_scores = weights_f * (
            grad_weights - jnp.sum(grad_weights * weights_f, axis=-1, keepdims=True)
        )
        if offsets is not None:
            lowest = key_len - row_start - block_len
            grad_offsets = grad_offsets.at[:, lowest : lowest + block_len + key_len - 1].add(
                unskew(jnp.sum(grad_scores, axis=0), block_len, key_len)
            )
        scores_bf = grad_scores.astype(jnp.bfloat16)
        pieces.append(
            jnp.einsum("bhqk,bkhd->bqhd", scores_bf, key_rows, preferred_element_type=jnp.float32)
        )
        grad_keys = grad_keys + jnp.einsum(
            "bhqk,bqhd->bkhd",
            scores_bf,
            queries[:, row_start:row_end],
            preferred_element_type=jnp.float32,
        )
    return (jnp.concatenate(pieces, axis=1), grad_keys, grad_values, grad_offsets)


def input_grads(token_rows, head_grads, weights):
    flat_rows = token_rows.reshape(-1, token_rows.shape[-1])
    grad_in = jnp.zeros(flat_rows.shape, jnp.float32)
    weight_grads = []
    for grad_heads, weight in zip(head_grads, weights):
        grad_bf = grad_heads.astype(jnp.bfloat16).reshape(flat_rows.shape[0], -1)
        grad_in = grad_in + jnp.einsum(
            "te,de->td", grad_bf, weight, preferred_element_type=jnp.float32
        )
        weight_grads.append(
            jnp.einsum("td,te->de", flat_rows, grad_bf, preferred_element_type=jnp.float32)
        )
    return (grad_in, weight_grads)


def self_forward(token_rows, w_query, w_key, w_value, w_out, table, row_ids, two_sided):
    length = token_rows.shape[1]
    queries = project(token_rows, w_query)
    key_rows = project(token_rows, w_key)
    value_rows = project(token_rows, w_value)
    offsets = jnp.dot(
        offset_table(length, two_sided), table.astype(jnp.float32), precision=PRECISE
    ).T
    attended, maxima, totals = attend_forward(
        queries, key_rows, value_rows, offsets, row_ids, row_ids, not two_sided
    )
    flat_att = attended.reshape(-1, attended.shape[2] * HEAD_DIM)
    partial_out = jnp.dot(flat_att, w_out, preferred_element_type=jnp.float32)
    return (partial_out, (queries, key_rows, value_rows, attended, maxima, totals))


def self_backward(
    token_rows, w_query, w_key, w_value, w_out, table, row_ids, kept, grad_rows, two_sided
):
    queries, key_rows, value_rows, attended, maxima, totals = kept
    length = token_rows.shape[1]
    flat_att = attended.reshape(-1, attended.shape[2] * HEAD_DIM)
    grad_wo = jnp.einsum("te,td->ed", flat_att, grad_rows, preferred_element_type=jnp.float32)
    grad_att = (
        jnp.einsum("td,ed->te", grad_rows, w_out, preferred_element_type=jnp.float32)
        .astype(jnp.bfloat16)
        .reshape(attended.shape)
    )
    table_map = offset_table(length, two_sided)
    offsets = jnp.dot(table_map, table.astype(jnp.float32), precision=PRECISE).T
    grad_query, grad_key, grad_value, grad_offsets = attend_backward(
        queries,
        key_rows,
        value_rows,
        offsets,
        row_ids,
        row_ids,
        not two_sided,
        maxima,
        totals,
        grad_att,
    )
    grad_table = jnp.dot(table_map.T, grad_offsets.T, precision=PRECISE)
    grad_in, weight_grads = input_grads(
        token_rows, (grad_query, grad_key, grad_value), (w_query, w_key, w_value)
    )
    return (grad_in, weight_grads[0], weight_grads[1], weight_grads[2], grad_wo, grad_table)


def cross_forward(query_rows, memory_rows, w_query, w_key, w_value, w_out, query_ids, memory_ids):
    queries = project(query_rows, w_query)
    key_rows = project(memory_rows, w_key)
    value_rows = project(memory_rows, w_value)
    attended, maxima, totals = attend_forward(
        queries, key_rows, value_rows, None, query_ids, memory_ids, False
    )
    flat_att = attended.reshape(-1, attended.shape[2] * HEAD_DIM)
    partial_out = jnp.dot(flat_att, w_out, preferred_element_type=jnp.float32)
    return (partial_out, (queries, key_rows, value_rows, attended, maxima, totals))


def cross_backward(
    query_rows, memory_rows, w_query, w_key, w_value, w_out, query_ids, memory_ids, kept, grad_rows
):
    queries, key_rows, value_rows, attended, maxima, totals = kept
    flat_att = attended.reshape(-1, attended.shape[2] * HEAD_DIM)
    grad_wo = jnp.einsum("te,td->ed", flat_att, grad_rows, preferred_element_type=jnp.float32)
    grad_att = (
        jnp.einsum("td,ed->te", grad_rows, w_out, preferred_element_type=jnp.float32)
        .astype(jnp.bfloat16)
        .reshape(attended.shape)
    )
    grad_query, grad_key, grad_value, unused = attend_backward(
        queries, key_rows, value_rows, None, query_ids, memory_ids, False, maxima, totals, grad_att
    )
    grad_in, query_grads = input_grads(query_rows, (grad_query,), (w_query,))
    grad_memory, memory_grads = input_grads(memory_rows, (grad_key, grad_value), (w_key, w_value))
    return (grad_in, grad_memory, query_grads[0], memory_grads[0], memory_grads[1], grad_wo)


def feed_forward(token_flat, w_gate, w_up, w_down):
    gate_val = jnp.dot(token_flat, w_gate, preferred_element_type=jnp.float32)
    up_val = jnp.dot(token_flat, w_up, preferred_element_type=jnp.float32)
    hidden_bf = (jax.nn.gelu(gate_val, approximate=True) * up_val).astype(jnp.bfloat16)
    return (jnp.dot(hidden_bf, w_down, preferred_element_type=jnp.float32), (gate_val, up_val))


def feed_backward(token_flat, w_gate, w_up, w_down, kept, grad_rows):
    gate_val, up_val = kept
    activated, gelu_back = jax.vjp(partial(jax.nn.gelu, approximate=True), gate_val)
    hidden_bf = (activated * up_val).astype(jnp.bfloat16)
    grad_down = jnp.einsum("tf,td->fd", hidden_bf, grad_rows, preferred_element_type=jnp.float32)
    grad_hidden = jnp.einsum("td,fd->tf", grad_rows, w_down, preferred_element_type=jnp.float32)
    grad_gate = gelu_back(grad_hidden * up_val)[0].astype(jnp.bfloat16)
    grad_up = (grad_hidden * activated).astype(jnp.bfloat16)
    grad_in = jnp.einsum(
        "tf,df->td", grad_gate, w_gate, preferred_element_type=jnp.float32
    ) + jnp.einsum("tf,df->td", grad_up, w_up, preferred_element_type=jnp.float32)
    grad_wgate = jnp.einsum("td,tf->df", token_flat, grad_gate, preferred_element_type=jnp.float32)
    grad_wup = jnp.einsum("td,tf->df", token_flat, grad_up, preferred_element_type=jnp.float32)
    return (grad_in, grad_wgate, grad_wup, grad_down)


def body(
    enc_in,
    dec_in,
    dec_cot,
    enc_seg,
    dec_seg,
    enc_norm1,
    enc_wq,
    enc_wk,
    enc_wv,
    enc_wo,
    enc_table,
    enc_norm2,
    enc_wgate,
    enc_wup,
    enc_wdown,
    enc_normf,
    dec_norm1,
    dec_wq,
    dec_wk,
    dec_wv,
    dec_wo,
    dec_table,
    dec_norm2,
    cross_wq,
    cross_wk,
    cross_wv,
    cross_wo,
    dec_norm3,
    dec_wgate,
    dec_wup,
    dec_wdown,
):
    groups = lax.axis_size("grp")
    quarter = groups // 4
    where_grp = lax.axis_index("grp")
    is_encoder = where_grp < 3 * quarter
    is_decoder = jnp.logical_not(is_encoder)
    enc_flag = is_encoder.astype(jnp.float32)
    dec_flag = is_decoder.astype(jnp.float32)
    local_heads = enc_table.shape[1]
    head_start = lax.axis_index("tp") * local_heads
    (
        e_norm1,
        e_wq,
        e_wk,
        e_wv,
        e_wo,
        e_norm2,
        e_wgate,
        e_wup,
        e_wdown,
        e_normf,
        d_norm1,
        d_wq,
        d_wk,
        d_wv,
        d_wo,
        d_norm2,
        c_wq,
        c_wk,
        c_wv,
        c_wo,
        d_norm3,
        d_wgate,
        d_wup,
        d_wdown,
    ) = (
        lax.all_gather(enc_norm1, "grp", axis=0, tiled=True),
        lax.all_gather(enc_wq, "grp", axis=0, tiled=True),
        lax.all_gather(enc_wk, "grp", axis=0, tiled=True),
        lax.all_gather(enc_wv, "grp", axis=0, tiled=True),
        lax.all_gather(enc_wo, "grp", axis=1, tiled=True),
        lax.all_gather(enc_norm2, "grp", axis=0, tiled=True),
        lax.all_gather(enc_wgate, "grp", axis=0, tiled=True),
        lax.all_gather(enc_wup, "grp", axis=0, tiled=True),
        lax.all_gather(enc_wdown, "grp", axis=1, tiled=True),
        lax.all_gather(enc_normf, "grp", axis=0, tiled=True),
        lax.all_gather(dec_norm1, "grp", axis=0, tiled=True),
        lax.all_gather(dec_wq, "grp", axis=0, tiled=True),
        lax.all_gather(dec_wk, "grp", axis=0, tiled=True),
        lax.all_gather(dec_wv, "grp", axis=0, tiled=True),
        lax.all_gather(dec_wo, "grp", axis=1, tiled=True),
        lax.all_gather(dec_norm2, "grp", axis=0, tiled=True),
        lax.all_gather(cross_wq, "grp", axis=0, tiled=True),
        lax.all_gather(cross_wk, "grp", axis=0, tiled=True),
        lax.all_gather(cross_wv, "grp", axis=0, tiled=True),
        lax.all_gather(cross_wo, "grp", axis=1, tiled=True),
        lax.all_gather(dec_norm3, "grp", axis=0, tiled=True),
        lax.all_gather(dec_wgate, "grp", axis=0, tiled=True),
        lax.all_gather(dec_wup, "grp", axis=0, tiled=True),
        lax.all_gather(dec_wdown, "grp", axis=1, tiled=True),
    )
    gain_e1 = e_norm1.astype(jnp.float32)
    gain_e2 = e_norm2.astype(jnp.float32)
    gain_ef = e_normf.astype(jnp.float32)
    gain_d1 = d_norm1.astype(jnp.float32)
    gain_d2 = d_norm2.astype(jnp.float32)
    gain_d3 = d_norm3.astype(jnp.float32)
    enc_x = enc_in[0].astype(jnp.float32)
    dec_x = dec_in[0].astype(jnp.float32)
    enc_ids = enc_seg[0]
    dec_ids = dec_seg[0]
    route_hops = [3 * quarter, 2 * quarter, quarter]
    enc_self = partial(self_forward, two_sided=True)
    dec_self = partial(self_forward, two_sided=False)
    enc_self_back = partial(self_backward, two_sided=True)
    dec_self_back = partial(self_backward, two_sided=False)
    enc_n1 = rms_scale(enc_x, gain_e1).astype(jnp.bfloat16)
    dec_n1 = rms_scale(dec_x, gain_d1).astype(jnp.bfloat16)
    enc_full1, dec_full1 = (
        lax.all_gather(enc_n1, "tp", axis=0, tiled=True),
        lax.all_gather(dec_n1, "tp", axis=0, tiled=True),
    )
    enc_rows1 = enc_full1.reshape(ROWS, ENC_LEN, -1)
    dec_rows1 = dec_full1.reshape(3 * ROWS, DEC_LEN, -1)
    enc_part1, enc_kept1 = only_when(
        is_encoder, enc_self, enc_rows1, e_wq, e_wk, e_wv, e_wo, enc_table, enc_ids
    )
    dec_part1, dec_kept1 = only_when(
        is_decoder, dec_self, dec_rows1, d_wq, d_wk, d_wv, d_wo, dec_table, dec_ids
    )
    enc_sum1, dec_sum1 = (
        lax.psum_scatter(
            enc_part1.astype(jnp.bfloat16), "tp", scatter_dimension=0, tiled=True
        ).astype(jnp.float32),
        lax.psum_scatter(
            dec_part1.astype(jnp.bfloat16), "tp", scatter_dimension=0, tiled=True
        ).astype(jnp.float32),
    )
    enc_x1 = enc_x + enc_sum1
    dec_x1 = dec_x + dec_sum1
    enc_rows2 = gather_tokens(rms_scale(enc_x1, gain_e2).astype(jnp.bfloat16))
    enc_part2, enc_kept2 = only_when(is_encoder, feed_forward, enc_rows2, e_wgate, e_wup, e_wdown)
    enc_x2 = enc_x1 + reduce_tokens(enc_part2)
    enc_out = rms_scale(enc_x2, gain_ef).astype(jnp.bfloat16)
    id_code = enc_ids.astype(jnp.bfloat16)
    moved_rows, moved_ids = ([], [])
    for route in range(3):
        arrived, arrived_ids = from_behind((enc_out, id_code), "grp", route_hops[route])
        moved_rows.append(arrived)
        moved_ids.append(arrived_ids)
    memory_ids = jnp.concatenate(moved_ids, axis=0)
    dec_n2 = rms_scale(dec_x1, gain_d2).astype(jnp.bfloat16)
    dec_full2, memory_a, memory_b, memory_c = (
        lax.all_gather(dec_n2, "tp", axis=0, tiled=True),
        lax.all_gather(moved_rows[0], "tp", axis=0, tiled=True),
        lax.all_gather(moved_rows[1], "tp", axis=0, tiled=True),
        lax.all_gather(moved_rows[2], "tp", axis=0, tiled=True),
    )
    memory_rows = jnp.concatenate(
        [
            memory_a.reshape(ROWS, ENC_LEN, -1),
            memory_b.reshape(ROWS, ENC_LEN, -1),
            memory_c.reshape(ROWS, ENC_LEN, -1),
        ],
        axis=0,
    )
    dec_rows2 = dec_full2.reshape(3 * ROWS, DEC_LEN, -1)
    dec_part2, dec_kept2 = only_when(
        is_decoder,
        cross_forward,
        dec_rows2,
        memory_rows,
        c_wq,
        c_wk,
        c_wv,
        c_wo,
        dec_ids,
        memory_ids,
    )
    dec_x2 = dec_x1 + reduce_tokens(dec_part2)
    dec_rows3 = gather_tokens(rms_scale(dec_x2, gain_d3).astype(jnp.bfloat16))
    dec_part3, dec_kept3 = only_when(is_decoder, feed_forward, dec_rows3, d_wgate, d_wup, d_wdown)
    dec_x3 = dec_x2 + reduce_tokens(dec_part3)
    dec_result = jnp.where(is_decoder, dec_x3, 0.0).astype(jnp.bfloat16)[None]
    grad_x3 = dec_cot[0].astype(jnp.float32)
    grad_rows3 = gather_tokens(grad_x3.astype(jnp.bfloat16))
    dec_back3 = only_when(
        is_decoder, feed_backward, dec_rows3, d_wgate, d_wup, d_wdown, dec_kept3, grad_rows3
    )
    grad_hidden, grad_gain_d3 = norm_backward(dec_x2, gain_d3, reduce_tokens(dec_back3[0]))
    grad_x2 = grad_x3 + grad_hidden
    grad_rows2 = gather_tokens(grad_x2.astype(jnp.bfloat16))
    dec_back2 = only_when(
        is_decoder,
        cross_backward,
        dec_rows2,
        memory_rows,
        c_wq,
        c_wk,
        c_wv,
        c_wo,
        dec_ids,
        memory_ids,
        dec_kept2,
        grad_rows2,
    )
    grad_routes = dec_back2[1].reshape(3, ROWS * ENC_LEN, -1)
    grad_n2, back_route0, back_route1, back_route2 = (
        lax.psum_scatter(
            dec_back2[0].astype(jnp.bfloat16), "tp", scatter_dimension=0, tiled=True
        ).astype(jnp.float32),
        lax.psum_scatter(
            grad_routes[0].astype(jnp.bfloat16), "tp", scatter_dimension=0, tiled=True
        ).astype(jnp.float32),
        lax.psum_scatter(
            grad_routes[1].astype(jnp.bfloat16), "tp", scatter_dimension=0, tiled=True
        ).astype(jnp.float32),
        lax.psum_scatter(
            grad_routes[2].astype(jnp.bfloat16), "tp", scatter_dimension=0, tiled=True
        ).astype(jnp.float32),
    )
    grad_hidden, grad_gain_d2 = norm_backward(dec_x1, gain_d2, grad_n2)
    grad_x1 = grad_x2 + grad_hidden
    grad_rows1 = gather_tokens(grad_x1.astype(jnp.bfloat16))
    dec_back1 = only_when(
        is_decoder,
        dec_self_back,
        dec_rows1,
        d_wq,
        d_wk,
        d_wv,
        d_wo,
        dec_table,
        dec_ids,
        dec_kept1,
        grad_rows1,
    )
    grad_hidden, grad_gain_d1 = norm_backward(dec_x, gain_d1, reduce_tokens(dec_back1[0]))
    dec_grad_out = jnp.where(is_decoder, grad_x1 + grad_hidden, 0.0).astype(jnp.bfloat16)[None]
    dec_list = (
        dec_back1[1],
        dec_back1[2],
        dec_back1[3],
        dec_back1[4],
        dec_back2[2],
        dec_back2[3],
        dec_back2[4],
        dec_back2[5],
        dec_back3[1],
        dec_back3[2],
        dec_back3[3],
    )
    dec_axes = (0, 0, 0, 1, 0, 0, 0, 1, 0, 0, 1)
    returned = jnp.zeros(enc_x.shape, jnp.float32)
    for route, grad_piece in enumerate((back_route0, back_route1, back_route2)):
        arrived = from_behind(grad_piece.astype(jnp.bfloat16), "grp", -route_hops[route])
        returned = returned + arrived.astype(jnp.float32)
    grad_e2, grad_gain_ef = norm_backward(enc_x2, gain_ef, returned)
    grad_rows_e2 = gather_tokens(grad_e2.astype(jnp.bfloat16))
    enc_back2 = only_when(
        is_encoder, feed_backward, enc_rows2, e_wgate, e_wup, e_wdown, enc_kept2, grad_rows_e2
    )
    grad_hidden, grad_gain_e2 = norm_backward(enc_x1, gain_e2, reduce_tokens(enc_back2[0]))
    grad_e1 = grad_e2 + grad_hidden
    grad_rows_e1 = gather_tokens(grad_e1.astype(jnp.bfloat16))
    enc_back1 = only_when(
        is_encoder,
        enc_self_back,
        enc_rows1,
        e_wq,
        e_wk,
        e_wv,
        e_wo,
        enc_table,
        enc_ids,
        enc_kept1,
        grad_rows_e1,
    )
    grad_hidden, grad_gain_e1 = norm_backward(enc_x, gain_e1, reduce_tokens(enc_back1[0]))
    enc_grad_out = jnp.where(is_encoder, grad_e1 + grad_hidden, 0.0).astype(jnp.bfloat16)[None]
    enc_list = (
        enc_back1[1],
        enc_back1[2],
        enc_back1[3],
        enc_back1[4],
        enc_back2[1],
        enc_back2[2],
        enc_back2[3],
    )
    enc_axes = (0, 0, 0, 1, 0, 0, 1)
    enc_flat = pack_owned(enc_list, enc_axes, groups)
    dec_flat = pack_owned(dec_list, dec_axes, groups)
    enc_width = enc_flat.shape[1]
    dec_width = dec_flat.shape[1]
    common = max(enc_width, dec_width)
    enc_padded = jnp.pad(enc_flat, ((0, 0), (0, common - enc_width)))
    dec_padded = jnp.pad(dec_flat, ((0, 0), (0, common - dec_width)))
    outgoing = jnp.where(is_encoder, enc_padded, dec_padded)
    incoming = lax.all_to_all(
        for_sending(outgoing), "grp", split_axis=0, concat_axis=0, tiled=True
    ).astype(outgoing.dtype)
    enc_total = jnp.sum(incoming[: 3 * quarter, :enc_width], axis=0)
    dec_total = jnp.sum(incoming[3 * quarter :, :dec_width], axis=0)
    enc_shards = unpack_owned(enc_total, enc_list, enc_axes, groups)
    dec_shards = unpack_owned(dec_total, dec_list, dec_axes, groups)
    zero_table = jnp.zeros((BUCKETS, local_heads * lax.axis_size("tp")), jnp.float32)
    table_grad_e = lax.dynamic_update_slice(zero_table, enc_back1[5], (0, head_start))
    table_grad_d = lax.dynamic_update_slice(zero_table, dec_back1[5], (0, head_start))
    total_e1, total_e2, total_ef, total_d1, total_d2, total_d3, total_table_e, total_table_d = (
        lax.psum(
            (
                grad_gain_e1 * enc_flag,
                grad_gain_e2 * enc_flag,
                grad_gain_ef * enc_flag,
                grad_gain_d1 * dec_flag,
                grad_gain_d2 * dec_flag,
                grad_gain_d3 * dec_flag,
                table_grad_e,
                table_grad_d,
            ),
            ("grp", "tp"),
        )
    )
    share_len = total_e1.shape[0] // groups
    gain_start = where_grp * share_len

    def pick_share(full_grad):
        return lax.dynamic_slice_in_dim(full_grad, gain_start, share_len)

    def pick_heads(full_table):
        return lax.dynamic_slice_in_dim(full_table, head_start, local_heads, axis=1)

    return (
        dec_result,
        enc_grad_out,
        dec_grad_out,
        pick_share(total_e1),
        enc_shards[0],
        enc_shards[1],
        enc_shards[2],
        enc_shards[3],
        pick_heads(total_table_e),
        pick_share(total_e2),
        enc_shards[4],
        enc_shards[5],
        enc_shards[6],
        pick_share(total_ef),
        pick_share(total_d1),
        dec_shards[0],
        dec_shards[1],
        dec_shards[2],
        dec_shards[3],
        pick_heads(total_table_d),
        pick_share(total_d2),
        dec_shards[4],
        dec_shards[5],
        dec_shards[6],
        dec_shards[7],
        pick_share(total_d3),
        dec_shards[8],
        dec_shards[9],
        dec_shards[10],
    )


def solution(mesh):
    placed = (
        P("grp", "tp", None),
        P("grp", "tp", None),
        P("grp", "tp", None),
        P("grp", None, None),
        P("grp", None, None),
        P("grp"),
        P("grp", "tp"),
        P("grp", "tp"),
        P("grp", "tp"),
        P("tp", "grp"),
        P(None, "tp"),
        P("grp"),
        P("grp", "tp"),
        P("grp", "tp"),
        P("tp", "grp"),
        P("grp"),
        P("grp"),
        P("grp", "tp"),
        P("grp", "tp"),
        P("grp", "tp"),
        P("tp", "grp"),
        P(None, "tp"),
        P("grp"),
        P("grp", "tp"),
        P("grp", "tp"),
        P("grp", "tp"),
        P("tp", "grp"),
        P("grp"),
        P("grp", "tp"),
        P("grp", "tp"),
        P("tp", "grp"),
    )
    return jax.shard_map(
        body,
        mesh=mesh,
        in_specs=placed,
        out_specs=(
            P("grp", "tp", None),
            P("grp", "tp", None),
            P("grp", "tp", None),
            P("grp"),
            P("grp", "tp"),
            P("grp", "tp"),
            P("grp", "tp"),
            P("tp", "grp"),
            P(None, "tp"),
            P("grp"),
            P("grp", "tp"),
            P("grp", "tp"),
            P("tp", "grp"),
            P("grp"),
            P("grp"),
            P("grp", "tp"),
            P("grp", "tp"),
            P("grp", "tp"),
            P("tp", "grp"),
            P(None, "tp"),
            P("grp"),
            P("grp", "tp"),
            P("grp", "tp"),
            P("grp", "tp"),
            P("tp", "grp"),
            P("grp"),
            P("grp", "tp"),
            P("grp", "tp"),
            P("tp", "grp"),
        ),
        check_vma=False,
    )
```

profile of v0, /device:TPU:0, one launch (start us, length us, event | category | flops | bytes accessed | tf_op | source)
XLA Modules:
  0.0 2889.5 jit_solution(7130867904872864965)
XLA Ops:
  16.6 39.5 %all-reduce.15 = (bf16[1536]{0:T(1024)(128)(2,1)}, bf16[1536]{0:T(1024)(128)(2,1)}, bf16[1536]{0:T(1024)(128)(2,1)S(1)}, bf16[1536]{0:T(1024)(128)(2,1)S(1)}, bf...) all-reduce(bf16[1536]{0:T(1024)(128)(2,1)S(1)} %dynamic-update-slice.13, ...), channel_id=1, replica_groups=mesh['grp'=8,'tp'=4] {'grp'}, use_global_device_ids=true, to_apply=%add.13 | all-reduce | flops 9216 | bytes 36864
  59.2 34.4 %all_gather.122 = bf16[192,1536]{0,1:T(8,128)(2,1)} all-gather(bf16[192,192]{0,1:T(8,128)(2,1)S(1)} %copy.256), channel_id=1, replica_groups=mesh['grp'=8,'tp'=4] {'grp'}, dimensions={1}, use_global_device_ids=true | all-gather | bytes 663552 | tf_op jit(solution)/shard_map/all_gather | solution.py:425
  195.7 175.3 %conditional.11 = (bf16[1024,1536]{1,0:T(8,128)(2,1)}, bf16[1,1024,3,64]{1,3,2,0:T(8,128)(2,1)}, bf16[1,1024,3,64]{1,3,2,0:T(8,128)(2,1)}, bf16[1,1024,3,64]{1,3...) conditional(s32[]{:T(128)} %convert_element_type.528, ...), branch_computations={%region_8.9_spmd, %region_9.0_spmd} | conditional | flops 3251373056 | bytes 301338816 | solution.py:86
  431.5 61.3 %all-gather.29.cloned.1.call-done = bf16[1536,992]{1,0:T(8,128)(2,1)} async-done(((bf16[192,992]{1,0:T(8,128)(2,1)}), bf16[1536,992]{1,0:T(8,128)(2,1)}) %all-gather.29.cloned.1.call-update) | async-done | bytes 3047440 | tf_op jit(solution)/shard_map/all_gather | solution.py:428
  492.8 61.3 %all-gather.31.cloned.1.call-done = bf16[992,1536]{0,1:T(8,128)(2,1)} async-done(((bf16[992,192]{0,1:T(8,128)(2,1)}), bf16[992,1536]{0,1:T(8,128)(2,1)}) %all-gather.31.cloned.1.call-update) | async-done | bytes 3047440 | tf_op jit(solution)/shard_map/all_gather | solution.py:429
  642.6 34.4 %all_gather.114 = bf16[1536,192]{1,0:T(8,128)(2,1)} all-gather(bf16[192,192]{1,0:T(8,128)(2,1)S(1)} %copy-done.97), channel_id=1, replica_groups=mesh['grp'=8,'tp'=4] {'grp'}, dimensions={0}, use_global_device_ids=true | all-gather | bytes 663552 | tf_op jit(solution)/shard_map/all_gather | solution.py:432
  765.4 43.7 %collective-permute-start.1 = (bf16[256,1536]{1,0:T(8,128)(2,1)}, bf16[256,1536]{1,0:T(8,128)(2,1)S(1)}, u32[]{:S(2)}, u32[]{:S(2)}) collective-permute-start(bf16[256,1536]{1,0:T(8,128)(2,1)} %copy-done.68), channel_id=1, source_target_pairs={{0,16},{4,20},{8,24},{12,28},{1,17},{5,21},{9,25},{13,29},{2,18},{... | collective-permute-start | bytes 2359304 | tf_op jit(solution)/shard_map/ppermute | solution.py:29
  861.1 34.3 %all_gather.137 = bf16[192,1536]{0,1:T(8,128)(2,1)} all-gather(bf16[192,192]{0,1:T(8,128)(2,1)S(1)} %copy.259), channel_id=1, replica_groups=mesh['grp'=8,'tp'=4] {'grp'}, dimensions={1}, use_global_device_ids=true | all-gather | bytes 663552 | tf_op jit(solution)/shard_map/all_gather | solution.py:440
  895.4 34.4 %all_gather.135 = bf16[1536,192]{1,0:T(8,128)(2,1)} all-gather(bf16[192,192]{1,0:T(8,128)(2,1)S(1)} %copy-done.100), channel_id=1, replica_groups=mesh['grp'=8,'tp'=4] {'grp'}, dimensions={0}, use_global_device_ids=true | all-gather | bytes 663552 | tf_op jit(solution)/shard_map/all_gather | solution.py:437
  1015.7 48.5 %reduce-scatter.20.cloned.1.call-done = bf16[144,1536]{1,0:T(8,128)(2,1)} async-done(((bf16[576,1536]{1,0:T(8,128)(2,1)}), bf16[144,1536]{1,0:T(8,128)(2,1)}) %reduce-scatter.20.cloned.1.call-update) | async-done | bytes 442384 | tf_op jit(solution)/shard_map/reduce_scatter | solution.py:96
  1068.2 58.4 %all-gather.43.cloned.1.call-done = bf16[1536,992]{1,0:T(8,128)(2,1)} async-done(((bf16[192,992]{1,0:T(8,128)(2,1)}), bf16[1536,992]{1,0:T(8,128)(2,1)}) %all-gather.43.cloned.1.call-update) | async-done | bytes 3047440 | tf_op jit(solution)/shard_map/all_gather | solution.py:442
  1126.5 61.0 %all-gather.45.cloned.1.call-done = bf16[1536,992]{1,0:T(8,128)(2,1)} async-done(((bf16[192,992]{1,0:T(8,128)(2,1)}), bf16[1536,992]{1,0:T(8,128)(2,1)}) %all-gather.45.cloned.1.call-update) | async-done | bytes 3047440 | tf_op jit(solution)/shard_map/all_gather | solution.py:443
  1187.6 61.0 %all-gather.47.cloned.1.call-done = bf16[992,1536]{0,1:T(8,128)(2,1)} async-done(((bf16[992,192]{0,1:T(8,128)(2,1)}), bf16[992,1536]{0,1:T(8,128)(2,1)}) %all-gather.47.cloned.1.call-update) | async-done | bytes 3047440 | tf_op jit(solution)/shard_map/all_gather | solution.py:444
  1308.9 68.0 %reduce-scatter.24.cloned.1.call-done = bf16[144,1536]{1,0:T(8,128)(2,1)} async-done(((bf16[576,1536]{1,0:T(8,128)(2,1)}), bf16[144,1536]{1,0:T(8,128)(2,1)}) %reduce-scatter.24.cloned.1.call-update) | async-done | bytes 442384 | tf_op jit(solution)/shard_map/reduce_scatter | solution.py:96
  1418.6 90.5 %reduce-scatter.36.cloned.1.call-done = bf16[144,1536]{1,0:T(8,128)(2,1)} async-done(((bf16[576,1536]{1,0:T(8,128)(2,1)}), bf16[144,1536]{1,0:T(8,128)(2,1)}) %reduce-scatter.36.cloned.1.call-update) | async-done | bytes 442384 | tf_op jit(solution)/shard_map/reduce_scatter | solution.py:553
  1606.6 39.1 %reduce-scatter.28.cloned.1.call-done = bf16[256,1536]{1,0:T(8,128)(2,1)} async-done(((bf16[1024,1536]{1,0:T(8,128)(2,1)}), bf16[256,1536]{1,0:T(8,128)(2,1)}) %reduce-scatter.28.cloned.1.call-update) | async-done | bytes 786448 | tf_op jit(solution)/shard_map/reduce_scatter | solution.py:559
  1647.0 39.4 %reduce-scatter.26.cloned.1.call-done = bf16[256,1536]{1,0:T(8,128)(2,1)} async-done(((bf16[1024,1536]{1,0:T(8,128)(2,1)}), bf16[256,1536]{1,0:T(8,128)(2,1)}) %reduce-scatter.26.cloned.1.call-update) | async-done | bytes 786448 | tf_op jit(solution)/shard_map/reduce_scatter | solution.py:556
  1741.2 66.2 %conditional.17 = (bf16[1024,1536]{1,0:T(8,128)(2,1)}, bf16[992,1536]{1,0:T(8,128)(2,1)}, bf16[8,190464]{1,0:T(8,128)(2,1)}, bf16[8,190464]{1,0:T(8,128)(2,1)}) conditional(s32[]{:T(128)} %convert_element_type.528, () %tuple.143, (bf16[1024,1536]{1,0:T(8,128)(2,1)}, bf16[992,1536]{0,1:T(8,128)(2,1)}, f32[1024,992]{0,1:T(8,128)}, ...), branch_computations={%region_40.41_spmd, %region_41.42_spmd} | conditional | flops 18761056256 | bytes 173342944 | solution.py:86
  1879.9 383.0 %conditional.18 = (bf16[1024,1536]{1,0:T(8,128)(2,1)}, bf16[192,1536]{1,0:T(8,128)(2,1)}, f32[32,3]{0,1:T(4,128)}, bf16[8,36864]{1,0:T(8,128)(2,1)}, bf16[8,36864]{1,0:T(8,128)(2,1)}, /*index=5*/bf16[8,36864]{1,0:T(8,128)(2,1)}) conditional(s32[]{:T(128)} %convert_element_type.528, () %tuple.145, (s32[1,1024]{1,0:T(1,128)S(1)}, ...), branch_computations={%region_44.45_spmd, %region_45.51_spmd.clone} | conditional | flops 6897657856 | bytes 775753984 | solution.py:86
  2303.7 35.4 %reduce.26 = bf16[8,866304]{1,0:T(8,128)(2,1)} reduce(bf16[8,1,866304]{2,0,1:T(8,128)(2,1)} %fusion.170, bf16[]{:T(256)} %broadcast.763), dimensions={1}, to_apply=%copy.282.reduce_sub_computation | reduce | bytes 27721730 | tf_op jit(solution)/shard_map/all_to_all | solution.py:643
  2339.2 40.6 %reshape.1310 = bf16[8,2,433152]{2,1,0:T(2,128)(2,1)} reshape(bf16[8,866304]{1,0:T(8,128)(2,1)} %reduce.26) | data formatting | bytes 27721728
  2423.0 35.7 %reduce-scatter.34.cloned.1.call-done = bf16[256,1536]{1,0:T(8,128)(2,1)} async-done(((bf16[1024,1536]{1,0:T(8,128)(2,1)}), bf16[256,1536]{1,0:T(8,128)(2,1)}) %reduce-scatter.34.cloned.1.call-update) | async-done | bytes 786448 | tf_op jit(solution)/shard_map/reduce_scatter | solution.py:96
  2460.6 246.0 %all-reduce.14 = (f32[1536]{0:T(1024)S(1)}, f32[32,12]{0,1:T(8,128)S(1)}, f32[1536]{0:T(1024)S(1)}, f32[1536]{0:T(1024)S(1)}, f32[1536]{0:T(1024)S(1)}, /*index=...) all-reduce(f32[1536]{0:T(1024)S(1)} %broadcast_multiply_fusion.5, ...), channel_id=1, replica_groups=mesh['grp'=8,'tp'=4] {'grp','tp'}, use_global_device_ids=true, to_apply=%region_63.64 | all-reduce | flops 9984 | bytes 79872 | tf_op jit(solution)/shard_map/psum | solution.py:654
  2821.8 37.1 %slice_reduce_fusion.1 = f32[866304]{0:T(1024)S(1)} fusion(f32[8,1,866304]{2,1,0:T(1,128)} %convert_element_type.571), kind=kLoop, calls=%fused_computation.261 | loop fusion | flops 866304 | bytes 10395648 | tf_op jit(solution)/shard_map/reduce_sum | solution.py:647
  (658 shorter events, 1722.1 us)
Async XLA Ops:
  8.1 187.6 %all-gather.23.cloned.1.call-start = ((), (), s32[]{:S(2)}) async-start(), calls=%async_computation.16 | async-start | bytes 3932160 | tf_op jit(solution)/shard_map/all_gather | solution.py:464
  59.0 347.4 %reduce-scatter.16.cloned.1.call-start = ((), (), s32[]{:S(2)}) async-start(), calls=%async_computation.17 | async-start | bytes 3932160 | tf_op jit(solution)/shard_map/reduce_scatter | solution.py:476
  372.2 181.9 %all-gather.31.cloned.1.call-start = ((), (), s32[]{:S(2)}) async-start(), calls=%async_computation.21 | async-start | bytes 3538944 | tf_op jit(solution)/shard_map/all_gather | solution.py:429
  372.7 210.6 %all-gather.25.cloned.1.call-start = ((), (), s32[]{:S(2)}) async-start(), calls=%async_computation.18 | async-start | bytes 3932160 | tf_op jit(solution)/shard_map/all_gather | solution.py:90
  410.3 334.8 %all-gather.21.cloned.1.call-start = ((), (), s32[]{:S(2)}) async-start(), calls=%async_computation.14 | async-start | bytes 2211840 | tf_op jit(solution)/shard_map/all_gather | solution.py:465
  411.5 338.7 %reduce-scatter.18.cloned.1.call-start = ((), (), s32[]{:S(2)}) async-start(), calls=%async_computation.22 | async-start | bytes 3932160 | tf_op jit(solution)/shard_map/reduce_scatter | solution.py:96
  607.6 240.2 %reduce-scatter.14.cloned.1.call-start = ((), (), s32[]{:S(2)}) async-start(), calls=%async_computation.15 | async-start | bytes 2211840 | tf_op jit(solution)/shard_map/reduce_scatter | solution.py:479
  750.2 246.9 %all-gather.37.cloned.1.call-start = ((), (), s32[]{:S(2)}) async-start(), calls=%async_computation.25 | async-start | bytes 3932160 | tf_op jit(solution)/shard_map/all_gather | solution.py:501
  765.3 231.8 %all-gather.35.cloned.1.call-start = ((), (), s32[]{:S(2)}) async-start(), calls=%async_computation.24 | async-start | bytes 3932160 | tf_op jit(solution)/shard_map/all_gather | solution.py:500
  819.9 177.3 %all-gather.33.cloned.1.call-start = ((), (), s32[]{:S(2)}) async-start(), calls=%async_computation.23 | async-start | bytes 3932160 | tf_op jit(solution)/shard_map/all_gather | solution.py:499
  847.6 158.7 %all-gather.39.cloned.1.call-start = ((), (), s32[]{:S(2)}) async-start(), calls=%async_computation.26 | async-start | bytes 2211840 | tf_op jit(solution)/shard_map/all_gather | solution.py:498
  851.0 213.2 %reduce-scatter.20.cloned.1.call-start = ((), (), s32[]{:S(2)}) async-start(), calls=%async_computation.27 | async-start | bytes 2211840 | tf_op jit(solution)/shard_map/reduce_scatter | solution.py:96
  851.1 145.9 %collective-permute-start.5 = (bf16[1,1024]{1,0:T(2,128)(2,1)S(1)}, bf16[1,1024]{1,0:T(2,128)(2,1)S(1)}, u32[]{:S(2)}, u32[]{:S(2)}) collective-permute-start(bf16[1,1024]{1,0:T(2,128)(2,1)S(1)} %bitcast_convert_fusion), channel_id=1, source_target_pairs={{0,8},{4,12},{8,16},{12,20},{16,24},{20,28},{1,9},{5,13},{9,17},{1... | collective-permute-start | bytes 6152 | tf_op jit(solution)/shard_map/ppermute | solution.py:29
  852.4 144.6 %collective-permute-start.4 = (bf16[1,1024]{1,0:T(2,128)(2,1)S(1)}, bf16[1,1024]{1,0:T(2,128)(2,1)S(1)}, u32[]{:S(2)}, u32[]{:S(2)}) collective-permute-start(bf16[1,1024]{1,0:T(2,128)(2,1)S(1)} %bitcast_convert_fusion), channel_id=1, source_target_pairs={{0,16},{4,20},{8,24},{12,28},{1,17},{5,21},{9,25},{13,29},{2,18},{... | collective-permute-start | bytes 6152 | tf_op jit(solution)/shard_map/ppermute | solution.py:29
  859.7 137.3 %collective-permute-start.3 = (bf16[1,1024]{1,0:T(2,128)(2,1)S(1)}, bf16[1,1024]{1,0:T(2,128)(2,1)S(1)}, u32[]{:S(2)}, u32[]{:S(2)}) collective-permute-start(bf16[1,1024]{1,0:T(2,128)(2,1)S(1)} %bitcast_convert_fusion), channel_id=1, source_target_pairs={{0,24},{4,28},{1,25},{5,29},{2,26},{6,30},{3,27},{7,31}} | collective-permute-start | bytes 6152 | tf_op jit(solution)/shard_map/ppermute | solution.py:29
  1012.5 175.0 %all-gather.45.cloned.1.call-start = ((), (), s32[]{:S(2)}) async-start(), calls=%async_computation.30 | async-start | bytes 3538944 | tf_op jit(solution)/shard_map/all_gather | solution.py:443
  1013.1 235.5 %all-gather.47.cloned.1.call-start = ((), (), s32[]{:S(2)}) async-start(), calls=%async_computation.31 | async-start | bytes 3538944 | tf_op jit(solution)/shard_map/all_gather | solution.py:444
  1013.7 256.3 %all-gather.41.cloned.1.call-start = ((), (), s32[]{:S(2)}) async-start(), calls=%async_computation.28 | async-start | bytes 2211840 | tf_op jit(solution)/shard_map/all_gather | solution.py:90
  1067.5 224.6 %all-gather.57.cloned.1.call-start = ((), (), s32[]{:S(2)}) async-start(), calls=%async_computation.45 | async-start | bytes 2211840 | tf_op jit(solution)/shard_map/all_gather | solution.py:90
  1068.1 308.8 %reduce-scatter.24.cloned.1.call-start = ((), (), s32[]{:S(2)}) async-start(), calls=%async_computation.33 | async-start | bytes 2211840 | tf_op jit(solution)/shard_map/reduce_scatter | solution.py:96
  1418.6 153.1 %all-gather.55.cloned.1.call-start = ((), (), s32[]{:S(2)}) async-start(), calls=%async_computation.43 | async-start | bytes 2211840 | tf_op jit(solution)/shard_map/all_gather | solution.py:90
  1551.8 134.6 %reduce-scatter.26.cloned.1.call-start = ((), (), s32[]{:S(2)}) async-start(), calls=%async_computation.35 | async-start | bytes 3932160 | tf_op jit(solution)/shard_map/reduce_scatter | solution.py:556
  1571.6 169.6 %all-gather.51.cloned.1.call-start = ((), (), s32[]{:S(2)}) async-start(), calls=%async_computation.38 | async-start | bytes 3932160 | tf_op jit(solution)/shard_map/all_gather | solution.py:90
  2379.7 333.8 %all-to-all-start = ((bf16[8,2,433152]{2,1,0:T(2,128)(2,1)}), bf16[8,2,433152]{2,1,0:T(2,128)(2,1)}, u32[]{:S(2)}, u32[]{:S(2)}) async-start(bf16[8,2,433152]{2,1,0:T(2,128)(2,1)} %reshape.1310), calls=%async_computation.13 | async-start | bytes 27721728 | tf_op jit(solution)/shard_map/all_to_all | solution.py:643
  (148 other events, 8188.3 us)
Sparse Core Ops, SparseCore 0:
  59.1 25.8 all-gather.22
  371.1 35.2 reduce-scatter.15
  607.7 37.0 reduce-scatter.17
  750.3 51.4 reduce-scatter.13
  803.8 31.6 all-gather.36
  837.6 28.5 all-gather.34
  868.4 28.5 all-gather.32
  899.2 20.7 all-gather.38
  1308.9 67.8 reduce-scatter.23
  1381.4 20.7 all-gather.48
  1418.1 91.0 reduce-scatter.35
  1511.6 29.3 reduce-scatter.21
  1715.4 25.7 all-gather.50
  1807.5 36.9 reduce-scatter.31
  1851.4 28.5 all-gather.52
  2388.6 29.7 reduce-scatter.37
  2420.8 37.9 reduce-scatter.33
Sparse Core Ops, SparseCore 1:
  373.9 57.6 all-gather.26
  433.8 58.9 all-gather.28
  495.1 58.9 all-gather.30
  556.3 27.0 all-gather.24
  585.5 20.6 all-gather.20
  1012.0 52.1 reduce-scatter.19
  1066.3 60.2 all-gather.42
  1128.6 58.9 all-gather.44
  1189.6 58.9 all-gather.46
  1250.8 19.2 all-gather.40
  1271.5 20.6 all-gather.56
  1544.2 20.6 all-gather.54
  1567.4 37.8 reduce-scatter.29
  1607.8 37.8 reduce-scatter.27
  1648.4 37.9 reduce-scatter.25
where the time goes:
time: 2900 us; the launch traced here: 2890 us
  waiting for transfers between devices  961 us (33%)
  local copies, waits for them, and re-layouts  723 us (25%)
  blocking collectives  694 us (24%)
  other arithmetic  242 us (8%)
  matrix products  142 us (5%)
  starting transfers between devices  83.6 us (3%)
    reduce_scatter x7, waiting for transfers between devices, reduce_tokens(): lax.psum_scatter(for_sending(values), 'tp', scatter_dimension=0, tiled=True)  247 us
    psum x1, blocking collectives, body(): lax.psum((grad_gain_e1 * enc_flag, grad_gain_e2 * enc_flag, grad_gain_ef...  246 us
    cond x84, local copies, waits for them, and re-layouts  168 us
    unnamed x225, local copies, waits for them, and re-layouts  132 us
    all_gather x7, waiting for transfers between devices, gather_tokens(): return lax.all_gather(values, 'tp', axis=0, tiled=True)  121 us
    reduce_scatter x1, waiting for transfers between devices, body(): lax.psum_scatter(dec_back2[0].astype(jnp.bfloat16), 'tp', scatter_dimensi...  90.5 us
    ppermute x9, starting transfers between devices, from_behind(): lax.ppermute(value, axis, [(source, source + steps) for source in range(i...  75 us
    another operation x8, local copies, waits for them, and re-layouts, skew(): jnp.tile(vectors, (1, rows_count))  72.7 us
  transfers between devices with their start and end apart: 42, of which 27 were waited for; matrix products, arithmetic and copies ran while one was open for 5% of the time, Pallas kernels for 0%

commit v1 on v0

v1 whole, which is shorter than its diff:
```python
from functools import partial

import jax
import jax.numpy as jnp
import numpy as np
from jax import lax
from jax.experimental import pallas as pl
from jax.experimental.pallas import tpu as pltpu
from jax.sharding import PartitionSpec as P

HEAD_DIM = 64
BUCKETS = 32
MAX_DIST = 128
DEC_LEN = 192
EPSILON = 1e-06
NEG_FILL = -1e30
QB = 128
F32 = jnp.float32
BF16 = jnp.bfloat16


def bucket_of(relative, two_sided):
    bucket_count = BUCKETS
    shifted = relative * 0
    if two_sided:
        bucket_count = bucket_count // 2
        shifted = shifted + (relative > 0) * bucket_count
        distance = np.abs(relative)
    else:
        distance = np.maximum(-relative, 0)
    exact_span = bucket_count // 2
    log_ratio = np.log(np.maximum(distance, 1) / exact_span) / np.log(MAX_DIST / exact_span)
    farther = np.minimum(
        exact_span + np.floor(log_ratio * (bucket_count - exact_span) + 1e-09).astype(np.int32),
        bucket_count - 1,
    )
    return (shifted + np.where(distance < exact_span, distance, farther)).astype(np.int32)


def one_hot_blocks(relative, two_sided):
    return np.eye(BUCKETS, dtype=np.float32)[:, bucket_of(relative, two_sided).reshape(-1)]


def enc_relative():
    return np.arange(-2 * QB, 3 * QB)[:, None] - np.arange(QB)[None, :]


def dec_relative():
    return np.arange(DEC_LEN)[:, None] - np.arange(DEC_LEN)[None, :]


def dot(left, right, dims):
    return lax.dot_general(left, right, (dims, ((), ())), preferred_element_type=F32)


NN = ((1,), (0,))
NT = ((1,), (1,))
TN = ((0,), (0,))


def block_of(place, tp):
    wide = place // 2
    swapped = (wide % 2) * 2 + wide // 2
    return (swapped ^ tp) * 2 + place % 2


def scores_t(head, cfg, keys, queries, bias_ref, same, place, tp):
    lanes = slice(head * HEAD_DIM, (head + 1) * HEAD_DIM)
    scores = dot(keys[:, lanes], queries[:, lanes], NT)
    if cfg["bias"] == "blocks":
        mine = block_of(place, tp)
        parts = []
        for kb in range(keys.shape[0] // QB):
            step = jnp.clip(block_of(kb, tp) - mine, -2, 2) + 2
            parts.append(bias_ref[head, step])
        scores = scores + jnp.concatenate(parts, axis=0)
    elif cfg["bias"] == "full":
        scores = scores + bias_ref[head]
    return jnp.where(same, scores, NEG_FILL)


def allowed_t(cfg, idk_ref, idq_ref):
    same = idk_ref[...] == idq_ref[0]
    if cfg["causal"]:
        key_pos = lax.broadcasted_iota(jnp.int32, same.shape, 0)
        query_pos = lax.broadcasted_iota(jnp.int32, same.shape, 1)
        same = same & (key_pos <= query_pos)
    return same


def forward_kernel(cfg, tp_ref, q_ref, kv_ref, idk_ref, idq_ref, *rest):
    if cfg["bias"]:
        bias_ref, out_ref, lse_ref, vt_ref = rest
    else:
        bias_ref, (out_ref, lse_ref, vt_ref) = None, rest
    heads = cfg["heads"]
    width = heads * HEAD_DIM
    place = pl.program_id(0)
    keys = kv_ref[:, cfg["k"] : cfg["k"] + width]

    def fill():
        vt_ref[...] = kv_ref[:, cfg["v"] : cfg["v"] + width].T

    if cfg["follow"]:
        fill()
    else:
        pl.when(place == 0)(fill)
    queries = q_ref[:, :width]
    same = allowed_t(cfg, idk_ref, idq_ref)
    outs = []
    for head in range(heads):
        scores = scores_t(head, cfg, keys, queries, bias_ref, same, place, tp_ref[0])
        peak = jnp.max(scores, axis=0, keepdims=True)
        exponent = jnp.exp(scores - peak)
        total = jnp.sum(exponent, axis=0, keepdims=True)
        weights = (exponent * (1.0 / total)).astype(BF16)
        outs.append(dot(vt_ref[head * HEAD_DIM : (head + 1) * HEAD_DIM, :], weights, NN))
        lse_ref[0, head : head + 1, :] = peak + jnp.log(total)
    out_ref[...] = jnp.concatenate(outs, axis=0).T.astype(BF16)


def backward_kernel(cfg, tp_ref, q_ref, kv_ref, idk_ref, idq_ref, *rest):
    if cfg["bias"]:
        bias_ref, lse_ref, go_ref, gq_ref, gkv_ref, gb_ref, kt_ref, acc_ref = rest
    else:
        bias_ref, gb_ref = None, None
        lse_ref, go_ref, gq_ref, gkv_ref, kt_ref, acc_ref = rest
    heads = cfg["heads"]
    width = heads * HEAD_DIM
    place = pl.program_id(0)
    keys = kv_ref[:, cfg["k"] : cfg["k"] + width]
    values = kv_ref[:, cfg["v"] : cfg["v"] + width]

    def clear():
        kt_ref[...] = kv_ref[:, cfg["k"] : cfg["k"] + width].T
        acc_ref[...] = jnp.zeros_like(acc_ref)

    def clear_bias():
        if gb_ref is not None:
            gb_ref[...] = jnp.zeros_like(gb_ref)

    pl.when(place == 0)(clear_bias)
    if cfg["follow"]:
        clear()
    else:
        pl.when(place == 0)(clear)
    queries = q_ref[:, :width]
    grad_out = go_ref[...]
    same = allowed_t(cfg, idk_ref, idq_ref)
    grads = []
    for head in range(heads):
        lanes = slice(head * HEAD_DIM, (head + 1) * HEAD_DIM)
        scores = scores_t(head, cfg, keys, queries, bias_ref, same, place, tp_ref[0])
        weights = jnp.exp(scores - lse_ref[0, head : head + 1, :])
        grad_weights = dot(values[:, lanes], grad_out[:, lanes], NT)
        delta = jnp.sum(grad_weights * weights, axis=0, keepdims=True)
        grad_scores = weights * (grad_weights - delta)
        if cfg["bias"] == "blocks":
            mine = block_of(place, tp_ref[0])
            for kb in range(keys.shape[0] // QB):
                step = jnp.clip(block_of(kb, tp_ref[0]) - mine, -2, 2) + 2
                gb_ref[head, step] += grad_scores[kb * QB : (kb + 1) * QB]
        elif cfg["bias"] == "full":
            gb_ref[head] += grad_scores
        scores_bf = grad_scores.astype(BF16)
        acc_ref[head] += dot(scores_bf, queries[:, lanes], NN)
        acc_ref[heads + head] += dot(weights.astype(BF16), grad_out[:, lanes], NN)
        grads.append(dot(kt_ref[lanes, :], scores_bf, NN))
    gq_ref[...] = jnp.concatenate(grads, axis=0).T.astype(BF16)

    def finish():
        gkv_ref[...] = jnp.concatenate(
            [acc_ref[k].astype(BF16) for k in range(2 * heads)], axis=1
        )

    if cfg["follow"]:
        finish()
    else:
        pl.when(place == pl.num_programs(0) - 1)(finish)


def attention_specs(cfg, q_cols, kv_cols, bias):
    bq, bk = cfg["bq"], cfg["bk"]
    follow = cfg["follow"]
    specs = [
        pl.BlockSpec((bq, q_cols), lambda i, s: (i, 0)),
        pl.BlockSpec((bk, kv_cols), (lambda i, s: (i, 0)) if follow else (lambda i, s: (0, 0))),
        pl.BlockSpec((bk, bq), (lambda i, s: (i, 0)) if follow else (lambda i, s: (0, 0))),
        pl.BlockSpec((1, 1, bq), lambda i, s: (i, 0, 0)),
    ]
    if bias is not None:
        rank = bias.ndim
        specs.append(pl.BlockSpec(bias.shape, lambda i, s: (0,) * rank))
    return specs


def attention_forward(cfg, tp, q, kv, idk, idq, bias=None):
    heads, bq, bk, steps = cfg["heads"], cfg["bq"], cfg["bk"], cfg["steps"]
    width = heads * HEAD_DIM
    extra = () if bias is None else (bias,)
    return pl.pallas_call(
        partial(forward_kernel, cfg),
        out_shape=(
            jax.ShapeDtypeStruct((steps * bq, width), BF16),
            jax.ShapeDtypeStruct((steps, heads, bq), F32),
        ),
        grid_spec=pltpu.PrefetchScalarGridSpec(
            num_scalar_prefetch=1,
            grid=(steps,),
            in_specs=attention_specs(cfg, q.shape[1], kv.shape[1], bias),
            out_specs=(
                pl.BlockSpec((bq, width), lambda i, s: (i, 0)),
                pl.BlockSpec((1, heads, bq), lambda i, s: (i, 0, 0)),
            ),
            scratch_shapes=[pltpu.VMEM((width, bk), BF16)],
        ),
        compiler_params=pltpu.CompilerParams(vmem_limit_bytes=40 << 20),
        name=cfg["name"] + "_forward",
    )(tp, q, kv, idk, idq, *extra)


def attention_backward(cfg, tp, q, kv, idk, idq, lse, grad_out, bias=None):
    heads, bq, bk, steps = cfg["heads"], cfg["bq"], cfg["bk"], cfg["steps"]
    width = heads * HEAD_DIM
    follow = cfg["follow"]
    extra = () if bias is None else (bias,)
    out_shape = [
        jax.ShapeDtypeStruct((steps * bq, width), BF16),
        jax.ShapeDtypeStruct((steps * bk if follow else bk, 2 * width), BF16),
    ]
    out_specs = [
        pl.BlockSpec((bq, width), lambda i, s: (i, 0)),
        pl.BlockSpec((bk, 2 * width), (lambda i, s: (i, 0)) if follow else (lambda i, s: (0, 0))),
    ]
    if bias is not None:
        rank = bias.ndim
        out_shape.append(jax.ShapeDtypeStruct(bias.shape, F32))
        out_specs.append(pl.BlockSpec(bias.shape, lambda i, s: (0,) * rank))
    return pl.pallas_call(
        partial(backward_kernel, cfg),
        out_shape=tuple(out_shape),
        grid_spec=pltpu.PrefetchScalarGridSpec(
            num_scalar_prefetch=1,
            grid=(steps,),
            in_specs=attention_specs(cfg, q.shape[1], kv.shape[1], bias)
            + [
                pl.BlockSpec((1, heads, bq), lambda i, s: (i, 0, 0)),
                pl.BlockSpec((bq, width), lambda i, s: (i, 0)),
            ],
            out_specs=tuple(out_specs),
            scratch_shapes=[pltpu.VMEM((width, bk), BF16), pltpu.VMEM((2 * heads, bk, HEAD_DIM), F32)],
        ),
        compiler_params=pltpu.CompilerParams(vmem_limit_bytes=48 << 20),
        name=cfg["name"] + "_backward",
    )(tp, q, kv, idk, idq, *extra, lse, grad_out)


def rms_scale(hidden, gain_vec):
    return (
        hidden * lax.rsqrt(jnp.mean(hidden * hidden, axis=-1, keepdims=True) + EPSILON) * gain_vec
    )


def norm_backward(hidden, gain_vec, grad_out):
    rate = lax.rsqrt(jnp.mean(hidden * hidden, axis=-1, keepdims=True) + EPSILON)
    scaled = gain_vec * grad_out
    inner = jnp.mean(hidden * scaled, axis=-1, keepdims=True)
    grad_in = rate * scaled - hidden * (rate * rate * rate * inner)
    return grad_in, jnp.sum(grad_out * hidden * rate, axis=0)


def gelu(value):
    return jax.nn.gelu(value, approximate=True)


def gated(gate_val, up_val):
    return (gelu(gate_val) * up_val).astype(BF16)


def gated_back(gate_val, up_val, grad_hidden):
    activated, gelu_back = jax.vjp(gelu, gate_val)
    hidden_bf = (activated * up_val).astype(BF16)
    grad_gate = gelu_back(grad_hidden * up_val)[0].astype(BF16)
    grad_up = (grad_hidden * activated).astype(BF16)
    return hidden_bf, grad_gate, grad_up


SWAP_CORE = [(0, 1), (1, 0), (2, 3), (3, 2)]
SWAP_PAIR = [(0, 2), (2, 0), (1, 3), (3, 1)]


def core_swap(value):
    return lax.ppermute(value, "tp", SWAP_CORE)


def pair_swap(value):
    return lax.ppermute(value, "tp", SWAP_PAIR)


def gather_tokens(own):
    far = pair_swap(own)
    return jnp.concatenate([own, far, core_swap(own), core_swap(far)], axis=0)


def reduce_tokens(partial_bf):
    count = partial_bf.shape[0] // 4
    other = core_swap(partial_bf[2 * count :])
    half = partial_bf[: 2 * count].astype(F32) + other.astype(F32)
    far = pair_swap(half[count:].astype(BF16))
    return half[:count] + far.astype(F32)


class Groups:
    def __init__(self):
        self.count = lax.axis_size("grp")
        self.quarter = self.count // 4
        where = lax.axis_index("grp")
        self.where = where
        self.role = where // self.quarter
        self.place = where % self.quarter
        self.is_enc = self.role < 3
        self.peers = [
            [a * self.quarter + j for j in range(self.quarter)] for a in range(4)
        ]
        self.swap = [(i, i ^ 1) for i in range(self.count)]

    def shift(self, value, steps):
        hop = steps * self.quarter
        return lax.ppermute(
            value, "grp", [(i, (i + hop) % self.count) for i in range(self.count)]
        )

    def send(self, value, source, target):
        q = self.quarter
        return lax.ppermute(
            value, "grp", [(source * q + j, target * q + j) for j in range(q)]
        )

    def gather(self, enc, dec):
        own = jnp.where(self.is_enc, enc, dec)
        held = [own]
        for step in (1, 2, 3):
            target = (self.role + step) % 4
            held.append(self.shift(jnp.where(target < 3, enc, dec), step))
        full = jnp.zeros((4, self.quarter) + own.shape, own.dtype)
        for step, shard in enumerate(held):
            source = (self.role - step) % 4
            if self.quarter == 2:
                other = lax.ppermute(shard, "grp", self.swap)
                full = lax.dynamic_update_slice(
                    full, shard[None, None], (source, self.place, 0, 0)
                )
                full = lax.dynamic_update_slice(
                    full, other[None, None], (source, 1 - self.place, 0, 0)
                )
            else:
                group = lax.all_gather(shard, "grp", axis_index_groups=self.peers)
                full = lax.dynamic_update_slice(full, group[None], (source, 0, 0, 0))
        return full.reshape(-1, own.shape[1])

    def peer_sum(self, value):
        if self.quarter == 2:
            return value + lax.ppermute(value, "grp", self.swap)
        return lax.psum(value, "grp", axis_index_groups=self.peers)

    def role_sums(self, mine):
        enc_total, dec_total = 0.0, 0.0
        for step in range(4):
            target = (self.role + step) % 4
            block = lax.dynamic_index_in_dim(mine, target, 0, keepdims=False)
            if step:
                block = self.shift(block, step)
            block = block.astype(F32)
            source_enc = (self.role - step) % 4 < 3
            enc_total = enc_total + jnp.where(source_enc, block, 0.0)
            dec_total = dec_total + jnp.where(source_enc, 0.0, block)
        return enc_total, dec_total

    def scatter(self, grad_bf):
        rows = grad_bf.shape[0] // self.count
        blocks = grad_bf.reshape(4, self.quarter, rows, grad_bf.shape[1])
        if self.quarter == 2:
            away = lax.dynamic_index_in_dim(blocks, 1 - self.place, 1, keepdims=False)
            home = lax.dynamic_index_in_dim(blocks, self.place, 1, keepdims=False)
            arrived = lax.ppermute(away, "grp", self.swap)
            mine = (home.astype(F32) + arrived.astype(F32)).astype(BF16)
        else:
            mine = lax.psum_scatter(
                blocks, "grp", scatter_dimension=1, axis_index_groups=self.peers
            )
        return self.role_sums(mine)

    def all_role_sums(self, value):
        value = self.peer_sum(value)
        return self.role_sums(jnp.broadcast_to(value[None], (4,) + value.shape))


def pad_rows(value, count):
    return jnp.pad(value, ((0, count - value.shape[0]), (0, 0)))


class DecoderRows:
    def __init__(self, tp, count, stride):
        self.count, self.stride, self.tp = count, stride, tp

    @staticmethod
    def flip(index):
        return (index % 2) * 2 + index // 2

    def to_rows(self, value, stride):
        return jnp.concatenate(
            [
                lax.dynamic_slice_in_dim(
                    value, self.flip(i ^ self.tp) * stride, self.count, axis=0
                )
                for i in range(4)
            ],
            axis=0,
        )

    def to_relative(self, value, stride):
        return jnp.concatenate(
            [
                pad_rows(
                    lax.dynamic_slice_in_dim(
                        value, (self.flip(b) ^ self.tp) * self.count, self.count, axis=0
                    ),
                    stride,
                )
                for b in range(4)
            ],
            axis=0,
        )


def body(
    enc_in,
    dec_in,
    dec_cot,
    enc_seg,
    dec_seg,
    enc_norm1,
    enc_wq,
    enc_wk,
    enc_wv,
    enc_wo,
    enc_table,
    enc_norm2,
    enc_wgate,
    enc_wup,
    enc_wdown,
    enc_normf,
    dec_norm1,
    dec_wq,
    dec_wk,
    dec_wv,
    dec_wo,
    dec_table,
    dec_norm2,
    cross_wq,
    cross_wk,
    cross_wv,
    cross_wo,
    dec_norm3,
    dec_wgate,
    dec_wup,
    dec_wdown,
):
    groups = Groups()
    is_enc = groups.is_enc
    tp = lax.axis_index("tp")
    tp_arg = tp.astype(jnp.int32)[None]
    heads = enc_table.shape[1]
    width = heads * HEAD_DIM
    enc_count = enc_in.shape[1]
    dec_count = dec_in.shape[1]
    enc_len = enc_seg.shape[-1]
    rows = DecoderRows(tp, dec_count, enc_count)

    def columns(parts):
        return jnp.concatenate(parts, axis=1)

    x_own = jnp.where(is_enc, enc_in[0], pad_rows(dec_in[0], enc_count))
    x_all = gather_tokens(x_own)
    w_qkv = groups.gather(
        columns([enc_wq, enc_wk, enc_wv, enc_norm1[:, None], enc_norm2[:, None], enc_normf[:, None]]),
        columns([dec_wq, dec_wk, dec_wv, dec_norm1[:, None], dec_norm2[:, None], dec_norm3[:, None]]),
    )
    gains = w_qkv[:, 3 * width :].astype(F32).T
    w_qkv = w_qkv[:, : 3 * width]
    gain1, gain2, gain3 = gains[0:1], gains[1:2], gains[2:3]
    w_out = groups.gather(enc_wo.T, dec_wo.T)
    w_gate = groups.gather(enc_wgate, dec_wgate)
    w_up = groups.gather(enc_wup, dec_wup)
    w_down = groups.gather(enc_wdown.T, dec_wdown.T)
    w_cross = groups.gather(columns([cross_wk, cross_wv]), columns([cross_wq, cross_wo.T]))
    w_cq, w_co = w_cross[:, :width], w_cross[:, width:]
    cot_own = dec_cot[0]
    cot_all = gather_tokens(cot_own)

    enc_ids = enc_seg[0, 0].astype(F32)
    ids_rel = jnp.concatenate(
        [
            lax.dynamic_slice_in_dim(enc_ids, (DecoderRows.flip(b) ^ tp) * enc_count, enc_count)
            for b in range(4)
        ]
    )
    dec_ids = dec_seg[0]
    cross_ids = sum(groups.send(dec_ids[r], 3, r) for r in range(3)).astype(F32)
    enc_hot = one_hot_blocks(enc_relative(), True)
    dec_hot = one_hot_blocks(dec_relative(), False)
    enc_bias = dot(enc_table, jnp.asarray(enc_hot, BF16), TN).reshape(heads, 5, QB, QB)
    dec_bias = dot(dec_table, jnp.asarray(dec_hot, BF16), TN).reshape(heads, DEC_LEN, DEC_LEN)

    enc_cfg = dict(
        name="enc", heads=heads, bq=QB, bk=enc_len, steps=enc_len // QB, follow=False,
        bias="blocks", causal=False, k=width, v=2 * width,
    )
    dec_cfg = dict(
        name="dec", heads=heads, bq=DEC_LEN, bk=DEC_LEN, steps=3, follow=True,
        bias="full", causal=True, k=width, v=2 * width,
    )
    cross_cfg = dict(
        name="cross", heads=heads, bq=DEC_LEN, bk=enc_len, steps=1, follow=False,
        bias=None, causal=False, k=0, v=width,
    )
    enc_idk = jnp.broadcast_to(ids_rel[:, None], (enc_len, QB))
    enc_idq = ids_rel.reshape(enc_len // QB, 1, QB)
    dec_idk = jnp.broadcast_to(dec_ids.astype(F32).reshape(-1, 1), (3 * DEC_LEN, DEC_LEN))
    dec_idq = dec_ids.astype(F32).reshape(3, 1, DEC_LEN)
    cross_idk = jnp.broadcast_to(ids_rel[:, None], (enc_len, DEC_LEN))
    cross_idq = cross_ids.reshape(1, 1, DEC_LEN)

    x_f32 = x_own.astype(F32)
    norm1_all = rms_scale(x_all.astype(F32), gain1).astype(BF16)
    qkv = dot(norm1_all, w_qkv, NN).astype(BF16)

    def enc_attend(qkv):
        return attention_forward(enc_cfg, tp_arg, qkv, qkv, enc_idk, enc_idq, enc_bias)

    def dec_attend(qkv):
        ordered = rows.to_rows(qkv, enc_count)
        out, lse = attention_forward(dec_cfg, tp_arg, ordered, ordered, dec_idk, dec_idq, dec_bias)
        return rows.to_relative(out, enc_count), jnp.pad(
            lse.reshape(-1), (0, heads * enc_len - lse.size)
        ).reshape(enc_len // QB, heads, QB)

    att, lse1 = lax.cond(is_enc, enc_attend, dec_attend, qkv)
    x1 = x_f32 + reduce_tokens(dot(att, w_out, NT).astype(BF16))

    norm2_all = gather_tokens(rms_scale(x1, gain2).astype(BF16))
    dec_q_rel = dot(norm2_all, w_cq, NN).astype(BF16)
    dec_q = rows.to_rows(dec_q_rel, enc_count).reshape(3, DEC_LEN, width)
    cross_q = sum(groups.send(dec_q[r], 3, r) for r in range(3))
    gate2 = dot(norm2_all, w_gate, NN)
    up2 = dot(norm2_all, w_up, NN)
    hidden2 = gated(gate2, up2)
    x2 = x1 + reduce_tokens(dot(hidden2, w_down, NT).astype(BF16))
    memory = gather_tokens(rms_scale(x2, gain3).astype(BF16))

    cross_kv = dot(memory, w_cross, NN).astype(BF16)
    cross_o, lse2 = attention_forward(cross_cfg, tp_arg, cross_q, cross_kv, cross_idk, cross_idq)
    dec_o = jnp.concatenate([groups.send(cross_o, r, 3) for r in range(3)], axis=0)
    dec_o_rel = rows.to_relative(dec_o, dec_count)

    x2d = x1[:dec_count] + reduce_tokens(dot(dec_o_rel, w_co, NT).astype(BF16))
    norm3_all = gather_tokens(rms_scale(x2d, gain3).astype(BF16))
    gate3 = dot(norm3_all, w_gate, NN)
    up3 = dot(norm3_all, w_up, NN)
    grad_hidden3 = dot(cot_all, w_down, NN)
    hidden3, grad_gate3, grad_up3 = gated_back(gate3, up3, grad_hidden3)
    grad_n3 = reduce_tokens((dot(grad_gate3, w_gate, NT) + dot(grad_up3, w_up, NT)).astype(BF16))
    grad_step, gain_d3 = norm_backward(x2d, gain3, grad_n3)
    grad_x2d = cot_own.astype(F32) + grad_step
    grad2_all = gather_tokens(grad_x2d.astype(BF16))
    grad_o_rel = dot(grad2_all, w_co, NN).astype(BF16)
    grad_o_rows = rows.to_rows(grad_o_rel, dec_count).reshape(3, DEC_LEN, width)
    cross_go = sum(groups.send(grad_o_rows[r], 3, r) for r in range(3))
    dec_out = x2d + reduce_tokens(dot(hidden3, w_down, NT).astype(BF16))

    cross_gq, cross_gkv = attention_backward(
        cross_cfg, tp_arg, cross_q, cross_kv, cross_idk, cross_idq, lse2, cross_go
    )
    dec_gq = jnp.concatenate([groups.send(cross_gq, r, 3) for r in range(3)], axis=0)
    dec_gq_rel = rows.to_relative(dec_gq, enc_count)
    grad_memory = reduce_tokens(dot(cross_gkv, w_cross, NT).astype(BF16)).astype(BF16).astype(F32)
    grad_e2, gain_ef = norm_backward(x2, gain3, grad_memory)

    grad_e2_all = gather_tokens(grad_e2.astype(BF16))
    grad_hidden2 = dot(grad_e2_all, w_down, NN)
    hidden2, grad_gate2, grad_up2 = gated_back(gate2, up2, grad_hidden2)
    zero = jnp.zeros((), BF16)
    grad_gate2 = jnp.where(is_enc, grad_gate2, zero)
    grad_up2 = jnp.where(is_enc, grad_up2, zero)
    grad_q_only = jnp.where(is_enc, zero, dec_gq_rel)
    grad_n2 = reduce_tokens(
        (
            dot(grad_gate2, w_gate, NT) + dot(grad_up2, w_up, NT) + dot(grad_q_only, w_cq, NT)
        ).astype(BF16)
    )
    grad_step, gain_2 = norm_backward(x1, gain2, grad_n2)
    grad_x1 = jnp.where(is_enc, grad_e2, pad_rows(grad_x2d, enc_count)) + grad_step

    def feed_grads(tokens, hidden, grad_gate, grad_up, grad_rows):
        return (
            dot(tokens, grad_gate, TN).astype(BF16),
            dot(tokens, grad_up, TN).astype(BF16),
            dot(grad_rows, hidden, TN).astype(BF16),
        )

    g_gate, g_up, g_down = lax.cond(
        is_enc,
        lambda enc, dec: feed_grads(*enc),
        lambda enc, dec: feed_grads(*dec),
        (norm2_all, hidden2, grad_gate2, grad_up2, grad_e2_all),
        (norm3_all, hidden3, grad_gate3, grad_up3, cot_all),
    )
    g_cross = jnp.where(
        is_enc,
        dot(memory, cross_gkv, TN),
        columns([dot(norm2_all, dec_gq_rel, TN), dot(grad2_all, dec_o_rel, TN)]),
    ).astype(BF16)

    grad_x1_all = gather_tokens(grad_x1.astype(BF16))
    grad_att = dot(grad_x1_all, w_out, NN).astype(BF16)
    g_out = dot(grad_x1_all, att, TN).astype(BF16)

    def enc_attend_back(qkv, lse, grad_att):
        gq, gkv, gb = attention_backward(
            enc_cfg, tp_arg, qkv, qkv, enc_idk, enc_idq, lse, grad_att, enc_bias
        )
        hot = jnp.asarray(enc_hot, F32)
        return columns([gq, gkv]), lax.dot_general(
            hot, gb.reshape(heads, -1), ((NT[0], NT[1]), ((), ())), precision=lax.Precision.HIGHEST
        )

    def dec_attend_back(qkv, lse, grad_att):
        ordered = rows.to_rows(qkv, enc_count)
        lse = lse.reshape(-1)[: 3 * heads * DEC_LEN].reshape(3, heads, DEC_LEN)
        gq, gkv, gb = attention_backward(
            dec_cfg, tp_arg, ordered, ordered, dec_idk, dec_idq, lse,
            rows.to_rows(grad_att, enc_count), dec_bias,
        )
        hot = jnp.asarray(dec_hot, F32)
        return rows.to_relative(columns([gq, gkv]), enc_count), lax.dot_general(
            hot, gb.reshape(heads, -1), ((NT[0], NT[1]), ((), ())), precision=lax.Precision.HIGHEST
        )

    grad_qkv, grad_table = lax.cond(is_enc, enc_attend_back, dec_attend_back, qkv, lse1, grad_att)
    grad_n1 = reduce_tokens(dot(grad_qkv, w_qkv, NT).astype(BF16))
    grad_step, gain_1 = norm_backward(x_f32, gain1, grad_n1)
    grad_x = grad_x1 + grad_step
    g_qkv = dot(norm1_all, grad_qkv, TN).astype(BF16)

    enc_gate, dec_gate = groups.scatter(g_gate)
    enc_up, dec_up = groups.scatter(g_up)
    enc_down, dec_down = groups.scatter(g_down)
    enc_cross, dec_cross = groups.scatter(g_cross)
    enc_out, dec_wout = groups.scatter(g_out)
    enc_qkv, dec_qkv = groups.scatter(g_qkv)

    gain_rows = jnp.stack([gain_1, gain_2, jnp.where(is_enc, gain_ef, gain_d3)])
    gain_rows = gain_rows + core_swap(gain_rows)
    gain_rows = gain_rows + pair_swap(gain_rows)
    small = jnp.concatenate([gain_rows.reshape(-1), grad_table.reshape(-1)])
    length = small.shape[0]
    small = jnp.pad(small, (0, -length % 1024)).reshape(-1, 128)
    enc_small, dec_small = groups.all_role_sums(small)

    def unpack(total):
        flat = total.reshape(-1)
        gain = flat[: gain_rows.size].reshape(gain_rows.shape)
        share = gain.shape[1] // groups.count
        mine = lax.dynamic_slice_in_dim(gain, groups.where * share, share, axis=1)
        return mine, flat[gain_rows.size : length].reshape(BUCKETS, heads)

    enc_gains, enc_table_grad = unpack(enc_small)
    dec_gains, dec_table_grad = unpack(dec_small)

    def part(value, index):
        return value[:, index * width : (index + 1) * width]

    zero_bf = jnp.zeros((), BF16)
    return (
        jnp.where(is_enc, zero_bf, dec_out.astype(BF16))[None],
        jnp.where(is_enc, grad_x.astype(BF16), zero_bf)[None],
        jnp.where(is_enc, zero_bf, grad_x[:dec_count].astype(BF16))[None],
        enc_gains[0],
        part(enc_qkv, 0),
        part(enc_qkv, 1),
        part(enc_qkv, 2),
        enc_out.T,
        enc_table_grad,
        enc_gains[1],
        enc_gate,
        enc_up,
        enc_down.T,
        enc_gains[2],
        dec_gains[0],
        part(dec_qkv, 0),
        part(dec_qkv, 1),
        part(dec_qkv, 2),
        dec_wout.T,
        dec_table_grad,
        dec_gains[1],
        part(dec_cross, 0),
        part(enc_cross, 0),
        part(enc_cross, 1),
        part(dec_cross, 1).T,
        dec_gains[2],
        dec_gate,
        dec_up,
        dec_down.T,
    )


def solution(mesh):
    vector, matrix, turned = P("grp"), P("grp", "tp"), P("tp", "grp")
    tokens, ids, table = P("grp", "tp", None), P("grp", None, None), P(None, "tp")
    enc = (vector, matrix, matrix, matrix, turned, table, vector, matrix, matrix, turned, vector)
    dec = (vector, matrix, matrix, matrix, turned, table, vector, matrix, matrix, matrix, turned)
    dec = dec + (vector, matrix, matrix, turned)
    return jax.shard_map(
        body,
        mesh=mesh,
        in_specs=(tokens, tokens, tokens, ids, ids) + enc + dec,
        out_specs=(tokens, tokens, tokens) + enc + dec,
        check_vma=False,
    )
```

time: 2900 us -> 930 us (0.32)
  blocking collectives: 694 us -> 0 us
  waiting for transfers between devices: 961 us -> 319 us
  local copies, waits for them, and re-layouts: 723 us -> 157 us
  other arithmetic: 242 us -> 59.2 us
  starting transfers between devices: 83.6 us -> 198 us
  Pallas kernels: 0 us -> 39 us
    reduce_scatter x13 -> x0, waiting for transfers between devices: 460 us -> none  [the longest x7 247 us: reduce_tokens(): lax.psum_scatter(for_sending(values), 'tp', scatter_dimension=0, tiled=True)]
    all_gather x19 -> x0, waiting for transfers between devices: 444 us -> none  [the longest x7 121 us: gather_tokens(): return lax.all_gather(values, 'tp', axis=0, tiled=True)]
    all_gather x12 -> x0, blocking collectives: 409 us -> none  [the longest x1 34.4 us: body(): lax.all_gather(dec_wq, 'grp', axis=0, tiled=True)]
    ppermute x9 -> x127, waiting for transfers between devices: 49.9 us -> 319 us  [the longest x17 91.7 us: pair_swap(): return lax.ppermute(value, 'tp', SWAP_PAIR)]
    psum x1 -> x0, blocking collectives: 246 us -> none  [body(): lax.psum((grad_gain_e1 * enc_flag, grad_gain_e2 * enc_flag, grad_gain_ef...]
    reshape x50 -> x9, local copies, waits for them, and re-layouts: 181 us -> 4.56 us  [the longest x1 3.2 us: gather(): return full.reshape(-1, own.shape[1])]
    cond x86 -> x5, local copies, waits for them, and re-layouts: 175 us -> 11.6 us  [the longest x3 11.6 us: body(): lax.cond(is_enc, lambda enc, dec: feed_grads(*enc), lambda enc, dec: feed...]
    ppermute x9 -> x127, starting transfers between devices: 75 us -> 198 us  [the longest x39 114 us: shift(): lax.ppermute(value, 'grp', [(i, (i + hop) % self.count) for i in range(se...]
  transfers between devices with their start and end apart: 42 -> 127, of which waited for: 27 -> 47; matrix products, arithmetic and copies ran while one was open for 5% -> 28% of each run, Pallas kernels for 0% -> 2%
where the time goes in v1:
time: 930 us; the launch traced here: 918 us
  waiting for transfers between devices  319 us (34%)
  starting transfers between devices  198 us (21%)
  local copies, waits for them, and re-layouts  157 us (17%)
  matrix products  140 us (15%)
  other arithmetic  59.2 us (6%)
  Pallas kernels  39 us (4%)
    dot_general x32, matrix products, dot(): lax.dot_general(left, right, (dims, ((), ())), preferred_element_type=F32)  123 us
    ppermute x39, starting transfers between devices, shift(): lax.ppermute(value, 'grp', [(i, (i + hop) % self.count) for i in range(se...  114 us
    ppermute x17, waiting for transfers between devices, pair_swap(): return lax.ppermute(value, 'tp', SWAP_PAIR)  91.7 us
    ppermute x6, waiting for transfers between devices, scatter(): arrived = lax.ppermute(away, 'grp', self.swap)  83.5 us
    ppermute x39, waiting for transfers between devices, shift(): lax.ppermute(value, 'grp', [(i, (i + hop) % self.count) for i in range(se...  66.3 us
    ppermute x24, waiting for transfers between devices, gather(): other = lax.ppermute(shard, 'grp', self.swap)  49.4 us
    ppermute x24, starting transfers between devices, gather(): other = lax.ppermute(shard, 'grp', self.swap)  31.2 us
    dynamic_update_slice x19, local copies, waits for them, and re-layouts, gather(): lax.dynamic_update_slice(full, shard[None, None], (source, self.place, 0,...  30.3 us
  transfers between devices with their start and end apart: 127, of which 47 were waited for; matrix products, arithmetic and copies ran while one was open for 28% of the time, Pallas kernels for 2%

profile of v1, /device:TPU:0, one launch (start us, length us, event | category | flops | bytes accessed | tf_op | source)
XLA Modules:
  0.0 917.9 jit_solution(6815527122687087014)
XLA Ops:
  150.5 16.8 %conditional.3 = ((bf16[1024,192]{1,0:T(8,128)(2,1)}, f32[8,3,128]{2,1,0:T(4,128)})) conditional(s32[]{:T(128)} %convert_element_type.415, (s32[]{:T(128)}, bf16[1024,576]{0,1:T(8,128)(2,1)}, s32[1]{0:T(128)}, f32[576,192]{1,0:T(8,128)}, f32[3,1,192]{2,1,0:T(1,128)S(1)}, /*index=5*/f32[3,192,192]{2,1,0:T(8,128)S(1)}) %tuple.39, (s32[1]{0:T(128)}, ...), branch_computations={%region_1.2_spmd, %region_2.3_spmd} | conditional | flops 6586487 | bytes 7898680 | solution.py:548
  152.2 14.6 %enc_forward.1 = (bf16[1024,192]{1,0:T(8,128)(2,1)}, f32[8,3,128]{2,1,0:T(4,128)}) custom-call(s32[1]{0:T(128)} %get-tuple-element.88.tp_ref, bf16[1024,576]{1,0:T(8,128)(2,1)S(1)} %copy.239.q_ref.kv_ref, bf16[1024,576]{1,0:T(8,128)(2,1)S(1)} %copy.239.q_ref.kv_ref, f32[1024,128]{1,0:T(8,128)} %get-tuple-element.90.idk_ref, ...), custom_call_target="tpu_custom_call" | custom-call | tf_op jit(solution)/shard_map/cond/branch_1_fun/enc_forward/pallas_call | solution.py:201
  209.5 14.0 %collective-permute-start.51 = (bf16[192,992]{1,0:T(8,128)(2,1)S(1)}, bf16[192,992]{1,0:T(8,128)(2,1)S(1)}, u32[]{:S(2)}, u32[]{:S(2)}) collective-permute-start(bf16[192,992]{1,0:T(8,128)(2,1)S(1)} %copy-done.94), channel_id=1, source_target_pairs={{0,24},{4,28},{8,0},{12,4},{16,8},{20,12},{24,16},{28,20},{1,25},{... | collective-permute-start | bytes 1142792 | tf_op jit(solution)/shard_map/ppermute | solution.py:329
  247.5 13.5 %collective-permute-done.50 = bf16[192,992]{1,0:T(8,128)(2,1)S(1)} collective-permute-done((bf16[192,992]{1,0:T(8,128)(2,1)S(1)}, bf16[192,992]{1,0:T(8,128)(2,1)S(1)}, u32[]{:S(2)}, u32[]{:S(2)}) %collective-permute-start.50) | collective-permute-done | bytes 380960 | tf_op jit(solution)/shard_map/ppermute | solution.py:349
  327.5 9.6 %collective-permute-done.55 = bf16[256,1536]{1,0:T(8,128)(2,1)S(1)} collective-permute-done((bf16[256,1536]{1,0:T(8,128)(2,1)S(1)}, bf16[256,1536]{1,0:T(8,128)(2,1)S(1)}, u32[]{:S(2)}, u32[]{:S(2)}) %collective-permute-start.55) | collective-permute-done | bytes 786464 | tf_op jit(solution)/shard_map/ppermute | solution.py:297
  367.4 11.0 %collective-permute-done.65 = bf16[144,1536]{1,0:T(8,128)(2,1)S(1)} collective-permute-done((bf16[144,1536]{1,0:T(8,128)(2,1)S(1)}, bf16[144,1536]{1,0:T(8,128)(2,1)S(1)}, u32[]{:S(2)}, u32[]{:S(2)}) %collective-permute-start.65) | collective-permute-done | bytes 442400 | tf_op jit(solution)/shard_map/ppermute | solution.py:297
  388.3 8.2 collective-permute-done.66
  419.5 10.9 %collective-permute-done.75 = bf16[144,1536]{1,0:T(8,128)(2,1)S(1)} collective-permute-done((bf16[144,1536]{1,0:T(8,128)(2,1)S(1)}, bf16[144,1536]{1,0:T(8,128)(2,1)S(1)}, u32[]{:S(2)}, u32[]{:S(2)}) %collective-permute-start.75) | collective-permute-done | bytes 442400 | tf_op jit(solution)/shard_map/ppermute | solution.py:297
  434.2 10.4 %collective-permute-done.76 = bf16[144,1536]{1,0:T(8,128)(2,1)} collective-permute-done((bf16[144,1536]{1,0:T(8,128)(2,1)}, bf16[144,1536]{1,0:T(8,128)(2,1)}, u32[]{:S(2)}, u32[]{:S(2)}) %collective-permute-start.76) | collective-permute-done | bytes 442400 | tf_op jit(solution)/shard_map/ppermute | solution.py:297
  452.3 11.3 %collective-permute-done.79 = bf16[192,192]{1,0:T(8,128)(2,1)S(1)} collective-permute-done((bf16[192,192]{1,0:T(8,128)(2,1)S(1)}, bf16[192,192]{1,0:T(8,128)(2,1)S(1)}, u32[]{:S(2)}, u32[]{:S(2)}) %collective-permute-start.79) | collective-permute-done | bytes 73760 | tf_op jit(solution)/shard_map/ppermute | solution.py:335
  484.0 13.6 %collective-permute-done.83 = bf16[256,1536]{1,0:T(8,128)(2,1)S(1)} collective-permute-done((bf16[256,1536]{1,0:T(8,128)(2,1)S(1)}, bf16[256,1536]{1,0:T(8,128)(2,1)S(1)}, u32[]{:S(2)}, u32[]{:S(2)}) %collective-permute-start.83) | collective-permute-done | bytes 786464 | tf_op jit(solution)/shard_map/ppermute | solution.py:297
  509.1 10.1 %collective-permute-done.84 = bf16[256,1536]{1,0:T(8,128)(2,1)S(1)} collective-permute-done((bf16[256,1536]{1,0:T(8,128)(2,1)S(1)}, bf16[256,1536]{1,0:T(8,128)(2,1)S(1)}, u32[]{:S(2)}, u32[]{:S(2)}) %collective-permute-start.84) | collective-permute-done | bytes 786464 | tf_op jit(solution)/shard_map/ppermute | solution.py:297
  525.4 14.5 %fusion.44 = (bf16[1024,992]{0,1:T(8,128)(2,1)}, bf16[1024,992]{0,1:T(8,128)(2,1)S(1)}) fusion(pred[]{:T(512)S(6)} %lt.614, f32[1024,992]{0,1:T(8,128)S(1)} %copy-done.171, f32[1024,992]{0,1:T(8,128)} %get-tuple-element.617, bf16[1536,992]{1,0:T(8,128)(2,1)} %bitcast.90, bf16[256,1536]{1,0:T(8,128)(2,1)S(1)} %collective-permute-done.86, ...), kind=kOutput, calls=%fused_computation.133 | convolution fusion | flops 3159556096 | bytes 18382848 | tf_op jit(solution)/shard_map/dot_general | solution.py:53
  561.2 48.3 %conditional.5 = (bf16[4,2,192,992]{3,2,1,0:T(8,128)(2,1)}, bf16[4,2,192,992]{3,2,1,0:T(8,128)(2,1)}, bf16[4,2,192,992]{3,2,1,0:T(8,128)(2,1)}, bf16[4,2,192,992...) conditional(s32[]{:T(128)} %convert_element_type.415, ...), branch_computations={%region_17.18_spmd, %region_18.19_spmd} | conditional | flops 9366257664 | bytes 61526092 | solution.py:611
  624.9 24.9 %collective-permute-done.111 = bf16[4,192,992]{2,1,0:T(8,128)(2,1)} collective-permute-done((bf16[4,192,992]{2,1,0:T(8,128)(2,1)}, bf16[4,192,992]{2,1,0:T(8,128)(2,1)}, u32[]{:S(2)}, u32[]{:S(2)}) %collective-permute-start.111) | collective-permute-done | bytes 1523744 | tf_op jit(solution)/shard_map/ppermute | solution.py:385
  659.9 23.6 %collective-permute-done.115 = bf16[4,192,992]{2,1,0:T(8,128)(2,1)S(1)} collective-permute-done((bf16[4,192,992]{2,1,0:T(8,128)(2,1)S(1)}, bf16[4,192,992]{2,1,0:T(8,128)(2,1)S(1)}, u32[]{:S(2)}, u32[]{:S(2)}) %collective-permute-start.115) | collective-permute-done | bytes 1523744 | tf_op jit(solution)/shard_map/ppermute | solution.py:385
  686.9 28.6 %collective-permute-done.119 = bf16[4,192,992]{2,1,0:T(8,128)(2,1)S(1)} collective-permute-done((bf16[4,192,992]{2,1,0:T(8,128)(2,1)S(1)}, bf16[4,192,992]{2,1,0:T(8,128)(2,1)S(1)}, u32[]{:S(2)}, u32[]{:S(2)}) %collective-permute-start.119) | collective-permute-done | bytes 1523744 | tf_op jit(solution)/shard_map/ppermute | solution.py:385
  729.5 16.1 %collective-permute-start.121 = (bf16[192,992]{1,0:T(8,128)(2,1)S(1)}, bf16[192,992]{1,0:T(8,128)(2,1)S(1)}, u32[]{:S(2)}, u32[]{:S(2)}) collective-permute-start(bf16[192,992]{1,0:T(8,128)(2,1)S(1)} %get-tuple-element.524), channel_id=1, source_target_pairs={{0,16},{4,20},{8,24},{12,28},{16,0},{20,4},{24,8},{28,12},{1,17},{... | collective-permute-start | bytes 1142792 | tf_op jit(solution)/shard_map/ppermute | solution.py:329
  745.6 12.7 %collective-permute-done.117 = bf16[192,992]{1,0:T(8,128)(2,1)S(1)} collective-permute-done((bf16[192,992]{1,0:T(8,128)(2,1)S(1)}, bf16[192,992]{1,0:T(8,128)(2,1)S(1)}, u32[]{:S(2)}, u32[]{:S(2)}) %collective-permute-start.117) | collective-permute-done | bytes 380960 | tf_op jit(solution)/shard_map/ppermute | solution.py:329
  758.3 9.3 %collective-permute-start.122 = (bf16[192,992]{1,0:T(8,128)(2,1)S(1)}, bf16[192,992]{1,0:T(8,128)(2,1)S(1)}, u32[]{:S(2)}, u32[]{:S(2)}) collective-permute-start(bf16[192,992]{1,0:T(8,128)(2,1)S(1)} %get-tuple-element.523), channel_id=1, source_target_pairs={{0,24},{4,28},{8,0},{12,4},{16,8},{20,12},{24,16},{28,20},{1,25},{... | collective-permute-start | bytes 1142792 | tf_op jit(solution)/shard_map/ppermute | solution.py:329
  784.6 39.2 %conditional.4 = (bf16[1024,576]{1,0:T(8,128)(2,1)S(1)}, f32[96]{0:T(128)S(1)}) conditional(s32[]{:T(128)} %convert_element_type.415, (s32[]{:T(128)}, bf16[1024,576]{0,1:T(8,128)(2,1)}, f32[8,3,128]{2,1,0:T(4,128)S(1)}, bf16[1024,192]{0,1:T(8,128)(2,1)S(1)}, s32[1]{0:T(128)}, /*index=5*/f32[576,192]{1,0:T(8,128)}, ...), branch_computations={%region_10.11_spmd.clone, %region_11.12_spmd.clone} | conditional | flops 96731136 | bytes 19494360 | solution.py:649
  787.9 18.3 %enc_backward.1 = (bf16[1024,192]{1,0:T(8,128)(2,1)S(1)}, bf16[1024,384]{1,0:T(8,128)(2,1)S(1)}, f32[3,5,128,128]{3,2,1,0:T(8,128)S(1)}) custom-call(s32[1]{0:T(128)} %get-tuple-element.200.tp_ref, bf16[1024,576]{1,0:T(8,128)(2,1)S(1)} %copy.253.q_ref.kv_ref, bf16[1024,576]{1,0:T(8,128)(2,1)S(1)} %copy.253.q_ref.kv_ref, ...), custom_call_target="tpu_custom_call" | custom-call | tf_op jit(solution)/shard_map/cond/branch_1_fun/enc_backward/pallas_call | solution.py:239
  806.8 16.7 %fusion.22 = f32[32,3]{1,0:T(8,128)S(1)} fusion(f32[32,81920]{1,0:T(8,128)} %constant.639.clone.2, f32[1,3,640,128]{3,2,1,0:T(8,128)S(1)} %bitcast.424), kind=kOutput, calls=%fused_computation.69 | convolution fusion | flops 94371840 | bytes 11469184 | tf_op jit(solution)/shard_map/cond/branch_1_fun/dot_general | solution.py:633
  901.2 8.4 collective-permute-start.102
  (853 shorter events, 611.6 us)
Async XLA Ops:
  9.0 87.0 %collective-permute-start.3 = (bf16[192,579]{1,0:T(8,128)(2,1)}, bf16[192,579]{1,0:T(8,128)(2,1)}, u32[]{:S(2)}, u32[]{:S(2)}) collective-permute-start(bf16[192,579]{1,0:T(8,128)(2,1)} %get-tuple-element.567), channel_id=1, source_target_pairs={{0,4},{4,0},{8,12},{12,8},{16,20},{20,16},{24,28},{28,24},{1,5},{5... | collective-permute-start | bytes 667016 | tf_op jit(solution)/shard_map/ppermute | solution.py:349
  12.8 39.1 %collective-permute-start.10 = (bf16[192,192]{0,1:T(8,128)(2,1)}, bf16[192,192]{0,1:T(8,128)(2,1)}, u32[]{:S(2)}, u32[]{:S(2)}) collective-permute-start(bf16[192,192]{0,1:T(8,128)(2,1)} %get-tuple-element.593), channel_id=1, source_target_pairs={{0,4},{4,0},{8,12},{12,8},{16,20},{20,16},{24,28},{28,24},{1,5},{5... | collective-permute-start | bytes 221192 | tf_op jit(solution)/shard_map/ppermute | solution.py:349
  51.9 83.1 %collective-permute-start = (bf16[256,1536]{1,0:T(8,128)(2,1)S(1)}, bf16[256,1536]{1,0:T(8,128)(2,1)}, u32[]{:S(2)}, u32[]{:S(2)}) collective-permute-start(bf16[256,1536]{1,0:T(8,128)(2,1)S(1)} %get-tuple-element.476), channel_id=1, source_target_pairs={{0,2},{2,0},{1,3},{3,1},{4,6},{6,4},{5,7},{7,5},{8,10},{10,8},{9,1... | collective-permute-start | bytes 2359304 | tf_op jit(solution)/shard_map/ppermute | solution.py:297
  67.2 70.9 %collective-permute-start.1 = (bf16[256,1536]{1,0:T(8,128)(2,1)S(1)}, bf16[256,1536]{1,0:T(8,128)(2,1)}, u32[]{:S(2)}, u32[]{:S(2)}) collective-permute-start(bf16[256,1536]{1,0:T(8,128)(2,1)S(1)} %get-tuple-element.476), channel_id=1, source_target_pairs={{0,1},{1,0},{2,3},{3,2},{4,5},{5,4},{6,7},{7,6},{8,9},{9,8},{10,11... | collective-permute-start | bytes 2359304 | tf_op jit(solution)/shard_map/ppermute | solution.py:293
  68.4 45.4 %collective-permute-start.6 = (bf16[192,579]{1,0:T(8,128)(2,1)}, bf16[192,579]{1,0:T(8,128)(2,1)}, u32[]{:S(2)}, u32[]{:S(2)}) collective-permute-start(bf16[192,579]{1,0:T(8,128)(2,1)} %get-tuple-element.565), channel_id=1, source_target_pairs={{0,16},{4,20},{8,24},{12,28},{16,0},{20,4},{24,8},{28,12},{1,17},{... | collective-permute-start | bytes 667016 | tf_op jit(solution)/shard_map/ppermute | solution.py:329
  113.8 72.3 %collective-permute-start.35 = (bf16[192,992]{1,0:T(8,128)(2,1)}, bf16[192,992]{1,0:T(8,128)(2,1)}, u32[]{:S(2)}, u32[]{:S(2)}) collective-permute-start(bf16[192,992]{1,0:T(8,128)(2,1)} %get-tuple-element.545), channel_id=1, source_target_pairs={{0,16},{4,20},{8,24},{12,28},{16,0},{20,4},{24,8},{28,12},{1,17},{... | collective-permute-start | bytes 1142792 | tf_op jit(solution)/shard_map/ppermute | solution.py:329
  121.9 87.7 %collective-permute-start.37 = (bf16[192,992]{1,0:T(8,128)(2,1)}, bf16[192,992]{1,0:T(8,128)(2,1)S(1)}, u32[]{:S(2)}, u32[]{:S(2)}) collective-permute-start(bf16[192,992]{1,0:T(8,128)(2,1)} %get-tuple-element.543), channel_id=1, source_target_pairs={{0,24},{4,28},{8,0},{12,4},{16,8},{20,12},{24,16},{28,20},{1,25},{... | collective-permute-start | bytes 1142792 | tf_op jit(solution)/shard_map/ppermute | solution.py:329
  186.2 40.3 %collective-permute-start.44 = (bf16[192,992]{1,0:T(8,128)(2,1)S(1)}, bf16[192,992]{1,0:T(8,128)(2,1)S(1)}, u32[]{:S(2)}, u32[]{:S(2)}) collective-permute-start(bf16[192,992]{1,0:T(8,128)(2,1)S(1)} %copy-done.95), channel_id=1, source_target_pairs={{0,24},{4,28},{8,0},{12,4},{16,8},{20,12},{24,16},{28,20},{1,25},{... | collective-permute-start | bytes 1142792 | tf_op jit(solution)/shard_map/ppermute | solution.py:329
  223.6 39.5 %collective-permute-start.38 = (bf16[192,992]{1,0:T(8,128)(2,1)S(1)}, bf16[192,992]{1,0:T(8,128)(2,1)S(1)}, u32[]{:S(2)}, u32[]{:S(2)}) collective-permute-start(bf16[192,992]{1,0:T(8,128)(2,1)S(1)} %collective-permute-done.37), channel_id=1, source_target_pairs={{0,4},{4,0},{8,12},{12,8},{16,20},{20,16},{24,28},{28,24},{1,5},{5... | collective-permute-start | bytes 1142792 | tf_op jit(solution)/shard_map/ppermute | solution.py:349
  501.4 48.1 %collective-permute-start.70 = (bf16[144,1536]{1,0:T(8,128)(2,1)}, bf16[144,1536]{1,0:T(8,128)(2,1)}, u32[]{:S(2)}, u32[]{:S(2)}) collective-permute-start(bf16[144,1536]{1,0:T(8,128)(2,1)} %slice.455), channel_id=1, source_target_pairs={{0,2},{2,0},{1,3},{3,1},{4,6},{6,4},{5,7},{7,5},{8,10},{10,8},{9,1... | collective-permute-start | bytes 1327112 | tf_op jit(solution)/shard_map/ppermute | solution.py:297
  549.5 65.5 %collective-permute-start.90 = (bf16[512,1536]{1,0:T(8,128)(2,1)}, bf16[512,1536]{1,0:T(8,128)(2,1)}, u32[]{:S(2)}, u32[]{:S(2)}) collective-permute-start(bf16[512,1536]{1,0:T(8,128)(2,1)} %slice.344), channel_id=1, source_target_pairs={{0,1},{1,0},{2,3},{3,2},{4,5},{5,4},{6,7},{7,6},{8,9},{9,8},{10,11... | collective-permute-start | bytes 4718600 | tf_op jit(solution)/shard_map/ppermute | solution.py:293
  555.0 58.1 %collective-permute-start.124 = (bf16[192,384]{1,0:T(8,128)(2,1)}, bf16[192,384]{1,0:T(8,128)(2,1)S(1)}, u32[]{:S(2)}, u32[]{:S(2)}) collective-permute-start(bf16[192,384]{1,0:T(8,128)(2,1)} %get-tuple-element.553), channel_id=1, source_target_pairs={{0,8},{4,12},{8,16},{12,20},{16,24},{20,28},{24,0},{28,4},{1,9},{5... | collective-permute-start | bytes 442376 | tf_op jit(solution)/shard_map/ppermute | solution.py:329
  557.0 56.1 %collective-permute-start.125 = (bf16[192,384]{1,0:T(8,128)(2,1)}, bf16[192,384]{1,0:T(8,128)(2,1)S(1)}, u32[]{:S(2)}, u32[]{:S(2)}) collective-permute-start(bf16[192,384]{1,0:T(8,128)(2,1)} %get-tuple-element.552), channel_id=1, source_target_pairs={{0,16},{4,20},{8,24},{12,28},{16,0},{20,4},{24,8},{28,12},{1,17},{... | collective-permute-start | bytes 442376 | tf_op jit(solution)/shard_map/ppermute | solution.py:329
  557.0 56.1 %collective-permute-start.126 = (bf16[192,384]{1,0:T(8,128)(2,1)}, bf16[192,384]{1,0:T(8,128)(2,1)S(1)}, u32[]{:S(2)}, u32[]{:S(2)}) collective-permute-start(bf16[192,384]{1,0:T(8,128)(2,1)} %get-tuple-element.551), channel_id=1, source_target_pairs={{0,24},{4,28},{8,0},{12,4},{16,8},{20,12},{24,16},{28,20},{1,25},{... | collective-permute-start | bytes 442376 | tf_op jit(solution)/shard_map/ppermute | solution.py:329
  621.2 62.3 %collective-permute-start.115 = (bf16[4,192,992]{2,1,0:T(8,128)(2,1)S(1)}, bf16[4,192,992]{2,1,0:T(8,128)(2,1)S(1)}, u32[]{:S(2)}, u32[]{:S(2)}) collective-permute-start(bf16[4,192,992]{2,1,0:T(8,128)(2,1)S(1)} %dynamic-slice_bitcast_fusion.1), channel_id=1, source_target_pairs={{0,4},{4,0},{8,12},{12,8},{16,20},{20,16},{24,28},{28,24},{1,5},{5... | collective-permute-start | bytes 4571144 | tf_op jit(solution)/shard_map/ppermute | solution.py:385
  624.0 91.5 %collective-permute-start.119 = (bf16[4,192,992]{2,1,0:T(8,128)(2,1)S(1)}, bf16[4,192,992]{2,1,0:T(8,128)(2,1)S(1)}, u32[]{:S(2)}, u32[]{:S(2)}) collective-permute-start(bf16[4,192,992]{2,1,0:T(8,128)(2,1)S(1)} %dynamic-slice_bitcast_fusion), channel_id=1, source_target_pairs={{0,4},{4,0},{8,12},{12,8},{16,20},{20,16},{24,28},{28,24},{1,5},{5... | collective-permute-start | bytes 4571144 | tf_op jit(solution)/shard_map/ppermute | solution.py:385
  652.7 62.9 %collective-permute-start.112 = (bf16[192,992]{1,0:T(8,128)(2,1)S(1)}, bf16[192,992]{1,0:T(8,128)(2,1)S(1)}, u32[]{:S(2)}, u32[]{:S(2)}) collective-permute-start(bf16[192,992]{1,0:T(8,128)(2,1)S(1)} %get-tuple-element.531), channel_id=1, source_target_pairs={{0,8},{4,12},{8,16},{12,20},{16,24},{20,28},{24,0},{28,4},{1,9},{5... | collective-permute-start | bytes 1142792 | tf_op jit(solution)/shard_map/ppermute | solution.py:329
  652.8 63.9 %collective-permute-start.113 = (bf16[192,992]{1,0:T(8,128)(2,1)S(1)}, bf16[192,992]{1,0:T(8,128)(2,1)S(1)}, u32[]{:S(2)}, u32[]{:S(2)}) collective-permute-start(bf16[192,992]{1,0:T(8,128)(2,1)S(1)} %get-tuple-element.530), channel_id=1, source_target_pairs={{0,16},{4,20},{8,24},{12,28},{16,0},{20,4},{24,8},{28,12},{1,17},{... | collective-permute-start | bytes 1142792 | tf_op jit(solution)/shard_map/ppermute | solution.py:329
  654.3 67.3 %collective-permute-start.114 = (bf16[192,992]{1,0:T(8,128)(2,1)S(1)}, bf16[192,992]{1,0:T(8,128)(2,1)S(1)}, u32[]{:S(2)}, u32[]{:S(2)}) collective-permute-start(bf16[192,992]{1,0:T(8,128)(2,1)S(1)} %get-tuple-element.529), channel_id=1, source_target_pairs={{0,24},{4,28},{8,0},{12,4},{16,8},{20,12},{24,16},{28,20},{1,25},{... | collective-permute-start | bytes 1142792 | tf_op jit(solution)/shard_map/ppermute | solution.py:329
  683.5 84.1 %collective-permute-start.92 = (bf16[256,1536]{1,0:T(8,128)(2,1)S(1)}, bf16[256,1536]{1,0:T(8,128)(2,1)S(1)}, u32[]{:S(2)}, u32[]{:S(2)}) collective-permute-start(bf16[256,1536]{1,0:T(8,128)(2,1)S(1)} %get-tuple-element.473), channel_id=1, source_target_pairs={{0,2},{2,0},{1,3},{3,1},{4,6},{6,4},{5,7},{7,5},{8,10},{10,8},{9,1... | collective-permute-start | bytes 2359304 | tf_op jit(solution)/shard_map/ppermute | solution.py:297
  715.5 42.7 %collective-permute-start.117 = (bf16[192,992]{1,0:T(8,128)(2,1)S(1)}, bf16[192,992]{1,0:T(8,128)(2,1)S(1)}, u32[]{:S(2)}, u32[]{:S(2)}) collective-permute-start(bf16[192,992]{1,0:T(8,128)(2,1)S(1)} %get-tuple-element.527), channel_id=1, source_target_pairs={{0,16},{4,20},{8,24},{12,28},{16,0},{20,4},{24,8},{28,12},{1,17},{... | collective-permute-start | bytes 1142792 | tf_op jit(solution)/shard_map/ppermute | solution.py:329
  716.7 50.9 %collective-permute-start.118 = (bf16[192,992]{1,0:T(8,128)(2,1)S(1)}, bf16[192,992]{1,0:T(8,128)(2,1)S(1)}, u32[]{:S(2)}, u32[]{:S(2)}) collective-permute-start(bf16[192,992]{1,0:T(8,128)(2,1)S(1)} %get-tuple-element.526), channel_id=1, source_target_pairs={{0,24},{4,28},{8,0},{12,4},{16,8},{20,12},{24,16},{28,20},{1,25},{... | collective-permute-start | bytes 1142792 | tf_op jit(solution)/shard_map/ppermute | solution.py:329
  721.6 49.7 %collective-permute-start.120 = (bf16[192,992]{1,0:T(8,128)(2,1)S(1)}, bf16[192,992]{1,0:T(8,128)(2,1)S(1)}, u32[]{:S(2)}, u32[]{:S(2)}) collective-permute-start(bf16[192,992]{1,0:T(8,128)(2,1)S(1)} %get-tuple-element.525), channel_id=1, source_target_pairs={{0,8},{4,12},{8,16},{12,20},{16,24},{20,28},{24,0},{28,4},{1,9},{5... | collective-permute-start | bytes 1142792 | tf_op jit(solution)/shard_map/ppermute | solution.py:329
  729.5 48.2 %collective-permute-start.121 = (bf16[192,992]{1,0:T(8,128)(2,1)S(1)}, bf16[192,992]{1,0:T(8,128)(2,1)S(1)}, u32[]{:S(2)}, u32[]{:S(2)}) collective-permute-start(bf16[192,992]{1,0:T(8,128)(2,1)S(1)} %get-tuple-element.524), channel_id=1, source_target_pairs={{0,16},{4,20},{8,24},{12,28},{16,0},{20,4},{24,8},{28,12},{1,17},{... | collective-permute-start | bytes 1142792 | tf_op jit(solution)/shard_map/ppermute | solution.py:329
  (278 other events, 4157.7 us)

commit v2 on v1

--- a/solution.py
+++ b/solution.py
@@ -1,3 +1,4 @@
+import math
 from functools import partial
 
 import jax
@@ -47,6 +48,10 @@
 
 def dec_relative():
     return np.arange(DEC_LEN)[:, None] - np.arange(DEC_LEN)[None, :]
+
+
+def after(value, *others):
+    return lax.optimization_barrier((value,) + others)[0]
 
 
 def dot(left, right, dims):
@@ -255,6 +260,73 @@
     )(tp, q, kv, idk, idq, *extra, lse, grad_out)
 
 
+def product_kernel(quarter, share, step, jobs, widths, role_ref, *refs):
+    operands, out_refs = refs[: 2 * len(jobs)], refs[2 * len(jobs) :]
+    starts = [sum(widths[:k]) for k in range(len(widths))]
+    for index, (on_role, column) in enumerate(jobs):
+        left_ref, right_ref = operands[2 * index], operands[2 * index + 1]
+
+        @pl.when(role_ref[0] == on_role)
+        def _():
+            result = dot(left_ref[...], right_ref[...], TN).astype(BF16)
+            rows_here, cols_here = result.shape
+            first = pl.program_id(0) * (rows_here // step)
+            for unit in range(rows_here // step):
+                row = (first + unit) * step
+                owner, offset = row // share, pl.multiple_of(row % share, step)
+                for out_ref, start, cols in zip(out_refs, starts, widths):
+                    low, high = max(start, column), min(start + cols, column + cols_here)
+                    if low < high:
+                        out_ref[
+                            owner % quarter,
+                            owner // quarter,
+                            pl.ds(offset, step),
+                            low - start : high - start,
+                        ] = result[unit * step : (unit + 1) * step, low - column : high - column]
+
+
+def token_product(groups, widths, *jobs):
+    rows_count = jobs[0][1].shape[1]
+    tile = 256
+    share = rows_count // groups.count
+    step = math.gcd(share, 64)
+    offsets, described, operands, specs = {}, [], [], []
+    for role, left, right in jobs:
+        count, cols = right.shape
+        described.append((role, offsets.get(role, 0)))
+        offsets[role] = offsets.get(role, 0) + cols
+
+        def left_map(i, s, role=role):
+            return (0, jnp.where(s[0] == role, i, 0))
+
+        operands += [left, right]
+        specs += [
+            pl.BlockSpec((count, tile), left_map),
+            pl.BlockSpec((count, cols), lambda i, s: (0, 0), pipeline_mode=pl.Buffered(1)),
+        ]
+    shapes = [(groups.quarter, 4, share, cols) for cols in widths]
+    role = jnp.where(groups.is_enc, 0, 1).astype(jnp.int32)[None]
+    return pl.pallas_call(
+        partial(product_kernel, groups.quarter, share, step, described, widths),
+        out_shape=tuple(jax.ShapeDtypeStruct(dims, BF16) for dims in shapes),
+        grid_spec=pltpu.PrefetchScalarGridSpec(
+            num_scalar_prefetch=1,
+            grid=(rows_count // tile,),
+            in_specs=specs,
+            out_specs=tuple(pl.BlockSpec(dims, lambda i, s: (0, 0, 0, 0)) for dims in shapes),
+        ),
+        compiler_params=pltpu.CompilerParams(vmem_limit_bytes=56 << 20),
+        name="token_product",
+    )(role, *operands)
+
+
+def bucket_sums(hot, values):
+    high = values.astype(BF16)
+    low = (values - high.astype(F32)).astype(BF16)
+    sums = dot(jnp.asarray(hot, BF16), jnp.concatenate([high, low], axis=0), NT)
+    return sums[:, : values.shape[0]] + sums[:, values.shape[0] :]
+
+
 def rms_scale(hidden, gain_vec):
     return (
         hidden * lax.rsqrt(jnp.mean(hidden * hidden, axis=-1, keepdims=True) + EPSILON) * gain_vec
@@ -269,20 +341,77 @@
     return grad_in, jnp.sum(grad_out * hidden * rate, axis=0)
 
 
+GELU_SCALE = float(np.sqrt(2.0 / np.pi))
+GELU_CUBIC = 0.044715
+
+
+def gelu_parts(value):
+    square = value * value
+    tanh = jnp.tanh(GELU_SCALE * (value + GELU_CUBIC * (value * square)))
+    half = 0.5 * (1.0 + tanh)
+    slope = half + 0.5 * value * (1.0 - tanh * tanh) * (
+        GELU_SCALE * (1.0 + 3.0 * GELU_CUBIC * square)
+    )
+    return value * half, slope
+
+
 def gelu(value):
-    return jax.nn.gelu(value, approximate=True)
-
-
-def gated(gate_val, up_val):
-    return (gelu(gate_val) * up_val).astype(BF16)
-
-
-def gated_back(gate_val, up_val, grad_hidden):
-    activated, gelu_back = jax.vjp(gelu, gate_val)
-    hidden_bf = (activated * up_val).astype(BF16)
-    grad_gate = gelu_back(grad_hidden * up_val)[0].astype(BF16)
+    cubic = value + GELU_CUBIC * (value * value * value)
+    return value * (0.5 * (1.0 + jnp.tanh(GELU_SCALE * cubic)))
+
+
+def feed_kernel(tok_ref, wg_ref, wu_ref, wd_ref, out_ref, gate_ref, up_ref):
+    tokens = tok_ref[...]
+    gate = dot(tokens, wg_ref[...], NN)
+    up = dot(tokens, wu_ref[...], NN)
+    gate_ref[...] = gate
+    up_ref[...] = up
+    hidden = (gelu(gate) * up).astype(BF16)
+    out_ref[...] = dot(hidden, wd_ref[...], NT).astype(BF16)
+
+
+def feed_grads(gate, up, grads, wg_ref, wu_ref, wd_ref, gn_ref, both_ref, hid_ref):
+    units = gate.shape[1]
+    grad_hidden = dot(grads, wd_ref[...], NN)
+    activated, slope = gelu_parts(gate)
+    hid_ref[...] = (activated * up).astype(BF16)
+    grad_gate = (grad_hidden * up * slope).astype(BF16)
     grad_up = (grad_hidden * activated).astype(BF16)
-    return hidden_bf, grad_gate, grad_up
+    both_ref[:, :units] = grad_gate
+    both_ref[:, units:] = grad_up
+    gn_ref[...] = (dot(grad_gate, wg_ref[...], NT) + dot(grad_up, wu_ref[...], NT)).astype(BF16)
+
+
+def feed_back_kernel(gate_ref, up_ref, ga_ref, wg_ref, wu_ref, wd_ref, gn_ref, both_ref, hid_ref):
+    feed_grads(
+        gate_ref[...], up_ref[...], ga_ref[...], wg_ref, wu_ref, wd_ref, gn_ref, both_ref, hid_ref
+    )
+
+
+def feed_both_kernel(
+    tok_ref, ga_ref, wg_ref, wu_ref, wd_ref, gn_ref, both_ref, hid_ref, out_ref
+):
+    tokens = tok_ref[...]
+    gate = dot(tokens, wg_ref[...], NN)
+    up = dot(tokens, wu_ref[...], NN)
+    feed_grads(gate, up, ga_ref[...], wg_ref, wu_ref, wd_ref, gn_ref, both_ref, hid_ref)
+    out_ref[...] = dot(hid_ref[...], wd_ref[...], NT).astype(BF16)
+
+
+def feed_call(name, kernel, tile, streamed, weights, outs):
+    count = streamed[0].shape[0]
+    return pl.pallas_call(
+        kernel,
+        out_shape=tuple(jax.ShapeDtypeStruct((count, cols), kind) for cols, kind in outs),
+        grid=(count // tile,),
+        in_specs=[pl.BlockSpec((tile, a.shape[1]), lambda i: (i, 0)) for a in streamed]
+        + [
+            pl.BlockSpec(w.shape, lambda i: (0, 0), pipeline_mode=pl.Buffered(1)) for w in weights
+        ],
+        out_specs=tuple(pl.BlockSpec((tile, cols), lambda i: (i, 0)) for cols, _ in outs),
+        compiler_params=pltpu.CompilerParams(vmem_limit_bytes=50 << 20),
+        name=name,
+    )(*streamed, *weights)
 
 
 SWAP_CORE = [(0, 1), (1, 0), (2, 3), (3, 2)]
@@ -297,16 +426,23 @@
     return lax.ppermute(value, "tp", SWAP_PAIR)
 
 
-def gather_tokens(own):
+def gather_tokens(own, meanwhile=None):
     far = pair_swap(own)
+    if meanwhile is not None:
+        far = after(far, meanwhile(own))
     return jnp.concatenate([own, far, core_swap(own), core_swap(far)], axis=0)
 
 
-def reduce_tokens(partial_bf):
+def reduce_tokens(partial_bf, meanwhile=None, first=None):
     count = partial_bf.shape[0] // 4
     other = core_swap(partial_bf[2 * count :])
+    if first is not None:
+        other = after(other, first(partial_bf))
     half = partial_bf[: 2 * count].astype(F32) + other.astype(F32)
-    far = pair_swap(half[count:].astype(BF16))
+    away = half[count:].astype(BF16)
+    far = pair_swap(away)
+    if meanwhile is not None:
+        far = after(far, meanwhile(away))
     return half[:count] + far.astype(F32)
 
 
@@ -323,6 +459,9 @@
             [a * self.quarter + j for j in range(self.quarter)] for a in range(4)
         ]
         self.swap = [(i, i ^ 1) for i in range(self.count)]
+        self.roles = [
+            [a * self.quarter + j for a in range(4)] for j in range(self.quarter)
+        ]
 
     def shift(self, value, steps):
         hop = steps * self.quarter
@@ -336,27 +475,48 @@
             value, "grp", [(source * q + j, target * q + j) for j in range(q)]
         )
 
-    def gather(self, enc, dec):
-        own = jnp.where(self.is_enc, enc, dec)
-        held = [own]
-        for step in (1, 2, 3):
-            target = (self.role + step) % 4
-            held.append(self.shift(jnp.where(target < 3, enc, dec), step))
-        full = jnp.zeros((4, self.quarter) + own.shape, own.dtype)
-        for step, shard in enumerate(held):
-            source = (self.role - step) % 4
-            if self.quarter == 2:
-                other = lax.ppermute(shard, "grp", self.swap)
-                full = lax.dynamic_update_slice(
-                    full, shard[None, None], (source, self.place, 0, 0)
-                )
-                full = lax.dynamic_update_slice(
-                    full, other[None, None], (source, 1 - self.place, 0, 0)
-                )
+    def gather(self, chunks, eager):
+        fulls, last, brought = [], {}, []
+        for (enc, dec), one_by_one in zip(chunks, eager):
+            rows, cols = enc.shape
+            shards = [jnp.where(self.is_enc, enc, dec)]
+            for step in (1, 2, 3):
+                payload = jnp.where((self.role + step) % 4 < 3, enc, dec)
+                if step in last:
+                    payload = after(payload, last[step])
+                last[step] = self.shift(payload, step)
+                shards.append(last[step])
+            brought.append(tuple(shards[1:]))
+            sources = [(self.role - step) % 4 for step in range(4)]
+            full = jnp.zeros((4, self.quarter, rows, cols), enc.dtype)
+            if one_by_one and self.quarter == 2:
+                for source, shard in zip(sources, shards):
+                    other = lax.ppermute(shard, "grp", self.swap)
+                    full = lax.dynamic_update_slice(
+                        full, shard[None, None], (source, self.place, 0, 0)
+                    )
+                    full = lax.dynamic_update_slice(
+                        full, other[None, None], (source, 1 - self.place, 0, 0)
+                    )
             else:
-                group = lax.all_gather(shard, "grp", axis_index_groups=self.peers)
-                full = lax.dynamic_update_slice(full, group[None], (source, 0, 0, 0))
-        return full.reshape(-1, own.shape[1])
+                held = jnp.zeros((4, rows, cols), enc.dtype)
+                for source, shard in zip(sources, shards):
+                    held = lax.dynamic_update_slice(held, shard[None], (source, 0, 0))
+                if self.quarter == 2:
+                    other = lax.ppermute(held, "grp", self.swap)
+                    full = lax.dynamic_update_slice(full, held[:, None], (0, self.place, 0, 0))
+                    full = lax.dynamic_update_slice(
+                        full, other[:, None], (0, 1 - self.place, 0, 0)
+                    )
+                else:
+                    full = lax.all_gather(held, "grp", axis=1, axis_index_groups=self.peers)
+            fulls.append(full.reshape(-1, cols))
+        return fulls, brought
+
+    def to_quarters(self, blocks):
+        return lax.all_to_all(
+            blocks, "grp", 0, 0, tiled=True, axis_index_groups=self.roles
+        )
 
     def peer_sum(self, value):
         if self.quarter == 2:
@@ -376,19 +536,14 @@
             dec_total = dec_total + jnp.where(source_enc, 0.0, block)
         return enc_total, dec_total
 
-    def scatter(self, grad_bf):
-        rows = grad_bf.shape[0] // self.count
-        blocks = grad_bf.reshape(4, self.quarter, rows, grad_bf.shape[1])
-        if self.quarter == 2:
-            away = lax.dynamic_index_in_dim(blocks, 1 - self.place, 1, keepdims=False)
-            home = lax.dynamic_index_in_dim(blocks, self.place, 1, keepdims=False)
-            arrived = lax.ppermute(away, "grp", self.swap)
-            mine = (home.astype(F32) + arrived.astype(F32)).astype(BF16)
-        else:
-            mine = lax.psum_scatter(
-                blocks, "grp", scatter_dimension=1, axis_index_groups=self.peers
-            )
-        return self.role_sums(mine)
+    def to_place(self, product):
+        return lax.psum_scatter(
+            product, "grp", scatter_dimension=0, axis_index_groups=self.peers
+        )
+
+    def to_owner(self, mine):
+        parts = self.to_quarters(mine).astype(F32)
+        return parts[0] + parts[1] + parts[2], parts[3]
 
     def all_role_sums(self, value):
         value = self.peer_sum(value)
@@ -482,21 +637,42 @@
 
     x_own = jnp.where(is_enc, enc_in[0], pad_rows(dec_in[0], enc_count))
     x_all = gather_tokens(x_own)
-    w_qkv = groups.gather(
-        columns([enc_wq, enc_wk, enc_wv, enc_norm1[:, None], enc_norm2[:, None], enc_normf[:, None]]),
-        columns([dec_wq, dec_wk, dec_wv, dec_norm1[:, None], dec_norm2[:, None], dec_norm3[:, None]]),
-    )
-    gains = w_qkv[:, 3 * width :].astype(F32).T
-    w_qkv = w_qkv[:, : 3 * width]
+    units = enc_wgate.shape[1]
+    padded = -units % 128
+
+    def first_chunk(weights, gains):
+        gains = jnp.pad(jnp.stack(gains, axis=1), ((0, 0), (0, -len(gains) % 64)))
+        return columns(list(weights) + [gains])
+
+    def second_chunk(weights):
+        return jnp.pad(columns(weights), ((0, 0), (0, -3 * width % 128)))
+
+    def wide(weight):
+        return jnp.pad(weight, ((0, 0), (0, padded)))
+
+    (first, second, w_gate, w_up, w_down), brought = groups.gather(
+        [
+            (
+                first_chunk([enc_wq, enc_wk, enc_wv], [enc_norm1, enc_norm2, enc_normf]),
+                first_chunk([dec_wq, dec_wk, dec_wv], [dec_norm1, dec_norm2, dec_norm3]),
+            ),
+            (
+                second_chunk([enc_wo.T, cross_wk, cross_wv]),
+                second_chunk([dec_wo.T, cross_wq, cross_wo.T]),
+            ),
+            (wide(enc_wgate), wide(dec_wgate)),
+            (wide(enc_wup), wide(dec_wup)),
+            (wide(enc_wdown.T), wide(dec_wdown.T)),
+        ],
+        (True, True, False, False, False),
+    )
+    w_qkv = first[:, : 3 * width]
+    gains = first[:, 3 * width : 3 * width + 3].astype(F32).T
     gain1, gain2, gain3 = gains[0:1], gains[1:2], gains[2:3]
-    w_out = groups.gather(enc_wo.T, dec_wo.T)
-    w_gate = groups.gather(enc_wgate, dec_wgate)
-    w_up = groups.gather(enc_wup, dec_wup)
-    w_down = groups.gather(enc_wdown.T, dec_wdown.T)
-    w_cross = groups.gather(columns([cross_wk, cross_wv]), columns([cross_wq, cross_wo.T]))
+    w_out, w_cross = second[:, :width], second[:, width : 3 * width]
     w_cq, w_co = w_cross[:, :width], w_cross[:, width:]
     cot_own = dec_cot[0]
-    cot_all = gather_tokens(cot_own)
+    enc_table, dec_table = after((enc_table, dec_table), brought[0])
 
     enc_ids = enc_seg[0, 0].astype(F32)
     ids_rel = jnp.concatenate(
@@ -545,17 +721,22 @@
             lse.reshape(-1), (0, heads * enc_len - lse.size)
         ).reshape(enc_len // QB, heads, QB)
 
-    att, lse1 = lax.cond(is_enc, enc_attend, dec_attend, qkv)
-    x1 = x_f32 + reduce_tokens(dot(att, w_out, NT).astype(BF16))
+    att, lse1 = lax.cond(is_enc, enc_attend, dec_attend, after(qkv, brought[2]))
+    x1 = x_f32 + reduce_tokens(dot(after(att, brought[3]), w_out, NT).astype(BF16))
 
     norm2_all = gather_tokens(rms_scale(x1, gain2).astype(BF16))
+    cot_all = gather_tokens(after(cot_own, norm2_all))
     dec_q_rel = dot(norm2_all, w_cq, NN).astype(BF16)
     dec_q = rows.to_rows(dec_q_rel, enc_count).reshape(3, DEC_LEN, width)
     cross_q = sum(groups.send(dec_q[r], 3, r) for r in range(3))
-    gate2 = dot(norm2_all, w_gate, NN)
-    up2 = dot(norm2_all, w_up, NN)
-    hidden2 = gated(gate2, up2)
-    x2 = x1 + reduce_tokens(dot(hidden2, w_down, NT).astype(BF16))
+    feed_weights = (w_gate, w_up, after(w_down, cross_q, cross_ids))
+    wide_units = w_gate.shape[1]
+    width_all = x_own.shape[1]
+    feed_out2, gate2, up2 = feed_call(
+        "feed_forward", feed_kernel, 256, (norm2_all,), feed_weights,
+        ((width_all, BF16), (wide_units, F32), (wide_units, F32)),
+    )
+    x2 = x1 + reduce_tokens(feed_out2)
     memory = gather_tokens(rms_scale(x2, gain3).astype(BF16))
 
     cross_kv = dot(memory, w_cross, NN).astype(BF16)
@@ -565,74 +746,82 @@
 
     x2d = x1[:dec_count] + reduce_tokens(dot(dec_o_rel, w_co, NT).astype(BF16))
     norm3_all = gather_tokens(rms_scale(x2d, gain3).astype(BF16))
-    gate3 = dot(norm3_all, w_gate, NN)
-    up3 = dot(norm3_all, w_up, NN)
-    grad_hidden3 = dot(cot_all, w_down, NN)
-    hidden3, grad_gate3, grad_up3 = gated_back(gate3, up3, grad_hidden3)
-    grad_n3 = reduce_tokens((dot(grad_gate3, w_gate, NT) + dot(grad_up3, w_up, NT)).astype(BF16))
+    grad_outs = ((width_all, BF16), (2 * wide_units, BF16), (wide_units, BF16))
+    partial_n3, both3, hidden3, feed_out3 = feed_call(
+        "feed_both", feed_both_kernel, 192, (norm3_all, cot_all), feed_weights,
+        grad_outs + ((width_all, BF16),),
+    )
+    grad_n3 = reduce_tokens(partial_n3)
     grad_step, gain_d3 = norm_backward(x2d, gain3, grad_n3)
     grad_x2d = cot_own.astype(F32) + grad_step
     grad2_all = gather_tokens(grad_x2d.astype(BF16))
     grad_o_rel = dot(grad2_all, w_co, NN).astype(BF16)
     grad_o_rows = rows.to_rows(grad_o_rel, dec_count).reshape(3, DEC_LEN, width)
     cross_go = sum(groups.send(grad_o_rows[r], 3, r) for r in range(3))
-    dec_out = x2d + reduce_tokens(dot(hidden3, w_down, NT).astype(BF16))
-
+    dec_out = x2d + reduce_tokens(after(feed_out3, grad_o_rel))
+
+    cross_go = after(cross_go, dec_out)
     cross_gq, cross_gkv = attention_backward(
         cross_cfg, tp_arg, cross_q, cross_kv, cross_idk, cross_idq, lse2, cross_go
     )
     dec_gq = jnp.concatenate([groups.send(cross_gq, r, 3) for r in range(3)], axis=0)
     dec_gq_rel = rows.to_relative(dec_gq, enc_count)
-    grad_memory = reduce_tokens(dot(cross_gkv, w_cross, NT).astype(BF16)).astype(BF16).astype(F32)
+    placed = {}
+
+    def while_memory(anchor):
+        left, right = after((memory, norm2_all), anchor)
+        (product,) = token_product(
+            groups,
+            (2 * width,),
+            (0, left, cross_gkv),
+            (1, right, dec_gq_rel),
+            (1, grad2_all, dec_o_rel),
+        )
+        placed["cross"] = groups.to_place(product)
+        return product
+
+    grad_memory = reduce_tokens(dot(cross_gkv, w_cross, NT).astype(BF16), while_memory)
+    grad_memory = grad_memory.astype(BF16).astype(F32)
     grad_e2, gain_ef = norm_backward(x2, gain3, grad_memory)
 
     grad_e2_all = gather_tokens(grad_e2.astype(BF16))
-    grad_hidden2 = dot(grad_e2_all, w_down, NN)
-    hidden2, grad_gate2, grad_up2 = gated_back(gate2, up2, grad_hidden2)
-    zero = jnp.zeros((), BF16)
-    grad_gate2 = jnp.where(is_enc, grad_gate2, zero)
-    grad_up2 = jnp.where(is_enc, grad_up2, zero)
-    grad_q_only = jnp.where(is_enc, zero, dec_gq_rel)
-    grad_n2 = reduce_tokens(
-        (
-            dot(grad_gate2, w_gate, NT) + dot(grad_up2, w_up, NT) + dot(grad_q_only, w_cq, NT)
-        ).astype(BF16)
-    )
+    partial_n2, both2, hidden2 = feed_call(
+        "feed_back", feed_back_kernel, 256, (gate2, up2, grad_e2_all), feed_weights, grad_outs
+    )
+
+    products = token_product(
+        groups,
+        (wide_units, wide_units),
+        (0, after(norm2_all, partial_n2), both2),
+        (1, norm3_all, both3),
+    )
+    for index, product in enumerate(products):
+        placed[index] = groups.to_place(product)
+    dec_partial = dot(after(dec_gq_rel, products), w_cq, NT).astype(BF16)
+    partial_n2 = jnp.where(is_enc, partial_n2, dec_partial)
+
+    def while_n2(anchor):
+        grads, others = after((grad_e2_all, cot_all), anchor)
+        (product,) = token_product(
+            groups, (wide_units,), (0, grads, hidden2), (1, others, hidden3)
+        )
+        placed[2] = groups.to_place(product)
+        sums["cross"] = groups.to_owner(after(placed["cross"], product))
+        return product, sums["cross"]
+
+    sums = {}
+    grad_n2 = reduce_tokens(partial_n2, while_n2)
     grad_step, gain_2 = norm_backward(x1, gain2, grad_n2)
     grad_x1 = jnp.where(is_enc, grad_e2, pad_rows(grad_x2d, enc_count)) + grad_step
-
-    def feed_grads(tokens, hidden, grad_gate, grad_up, grad_rows):
-        return (
-            dot(tokens, grad_gate, TN).astype(BF16),
-            dot(tokens, grad_up, TN).astype(BF16),
-            dot(grad_rows, hidden, TN).astype(BF16),
-        )
-
-    g_gate, g_up, g_down = lax.cond(
-        is_enc,
-        lambda enc, dec: feed_grads(*enc),
-        lambda enc, dec: feed_grads(*dec),
-        (norm2_all, hidden2, grad_gate2, grad_up2, grad_e2_all),
-        (norm3_all, hidden3, grad_gate3, grad_up3, cot_all),
-    )
-    g_cross = jnp.where(
-        is_enc,
-        dot(memory, cross_gkv, TN),
-        columns([dot(norm2_all, dec_gq_rel, TN), dot(grad2_all, dec_o_rel, TN)]),
-    ).astype(BF16)
+    sums[0] = groups.to_owner(after(placed[0], grad_x1))
 
     grad_x1_all = gather_tokens(grad_x1.astype(BF16))
     grad_att = dot(grad_x1_all, w_out, NN).astype(BF16)
-    g_out = dot(grad_x1_all, att, TN).astype(BF16)
-
     def enc_attend_back(qkv, lse, grad_att):
         gq, gkv, gb = attention_backward(
             enc_cfg, tp_arg, qkv, qkv, enc_idk, enc_idq, lse, grad_att, enc_bias
         )
-        hot = jnp.asarray(enc_hot, F32)
-        return columns([gq, gkv]), lax.dot_general(
-            hot, gb.reshape(heads, -1), ((NT[0], NT[1]), ((), ())), precision=lax.Precision.HIGHEST
-        )
+        return columns([gq, gkv]), gb.reshape(heads, -1)
 
     def dec_attend_back(qkv, lse, grad_att):
         ordered = rows.to_rows(qkv, enc_count)
@@ -641,28 +830,49 @@
             dec_cfg, tp_arg, ordered, ordered, dec_idk, dec_idq, lse,
             rows.to_rows(grad_att, enc_count), dec_bias,
         )
-        hot = jnp.asarray(dec_hot, F32)
-        return rows.to_relative(columns([gq, gkv]), enc_count), lax.dot_general(
-            hot, gb.reshape(heads, -1), ((NT[0], NT[1]), ((), ())), precision=lax.Precision.HIGHEST
-        )
-
-    grad_qkv, grad_table = lax.cond(is_enc, enc_attend_back, dec_attend_back, qkv, lse1, grad_att)
-    grad_n1 = reduce_tokens(dot(grad_qkv, w_qkv, NT).astype(BF16))
+        gb = gb.reshape(heads, -1)
+        return (
+            rows.to_relative(columns([gq, gkv]), enc_count),
+            jnp.pad(gb, ((0, 0), (0, enc_hot.shape[1] - gb.shape[1]))),
+        )
+
+    grad_qkv, grad_bias = lax.cond(is_enc, enc_attend_back, dec_attend_back, qkv, lse1, grad_att)
+    partial_n1 = dot(grad_qkv, w_qkv, NT).astype(BF16)
+
+    def while_n1(anchor):
+        left, right = after((norm1_all, grad_x1_all), anchor)
+        (product,) = token_product(
+            groups,
+            (4 * width,),
+            (0, left, grad_qkv),
+            (0, right, att),
+            (1, left, grad_qkv),
+            (1, right, att),
+        )
+        placed["first"] = groups.to_place(product)
+        tables["grad"] = lax.cond(
+            is_enc,
+            lambda gb: bucket_sums(enc_hot, gb),
+            lambda gb: bucket_sums(dec_hot, gb[:, : dec_hot.shape[1]]),
+            after(grad_bias, product),
+        )
+        return product, tables["grad"]
+
+    tables = {}
+
+    sums[1] = groups.to_owner(after(placed[1], partial_n1, sums[0]))
+    grad_n1 = reduce_tokens(partial_n1, while_n1)
     grad_step, gain_1 = norm_backward(x_f32, gain1, grad_n1)
     grad_x = grad_x1 + grad_step
-    g_qkv = dot(norm1_all, grad_qkv, TN).astype(BF16)
-
-    enc_gate, dec_gate = groups.scatter(g_gate)
-    enc_up, dec_up = groups.scatter(g_up)
-    enc_down, dec_down = groups.scatter(g_down)
-    enc_cross, dec_cross = groups.scatter(g_cross)
-    enc_out, dec_wout = groups.scatter(g_out)
-    enc_qkv, dec_qkv = groups.scatter(g_qkv)
+    sums[2] = groups.to_owner(after(placed[2], gain_1, sums[1]))
+    enc_first, dec_first = groups.to_owner(after(placed["first"], sums[2]))
+    enc_cross, dec_cross = sums["cross"]
+    (enc_gate, dec_gate), (enc_up, dec_up), (enc_down, dec_down) = sums[0], sums[1], sums[2]
 
     gain_rows = jnp.stack([gain_1, gain_2, jnp.where(is_enc, gain_ef, gain_d3)])
     gain_rows = gain_rows + core_swap(gain_rows)
     gain_rows = gain_rows + pair_swap(gain_rows)
-    small = jnp.concatenate([gain_rows.reshape(-1), grad_table.reshape(-1)])
+    small = jnp.concatenate([gain_rows.reshape(-1), tables["grad"].reshape(-1)])
     length = small.shape[0]
     small = jnp.pad(small, (0, -length % 1024)).reshape(-1, 128)
     enc_small, dec_small = groups.all_role_sums(small)
@@ -686,21 +896,21 @@
         jnp.where(is_enc, grad_x.astype(BF16), zero_bf)[None],
         jnp.where(is_enc, zero_bf, grad_x[:dec_count].astype(BF16))[None],
         enc_gains[0],
-        part(enc_qkv, 0),
-        part(enc_qkv, 1),
-        part(enc_qkv, 2),
-        enc_out.T,
+        part(enc_first, 0),
+        part(enc_first, 1),
+        part(enc_first, 2),
+        part(enc_first, 3).T,
         enc_table_grad,
         enc_gains[1],
-        enc_gate,
-        enc_up,
-        enc_down.T,
+        enc_gate[:, :units],
+        enc_up[:, :units],
+        enc_down[:, :units].T,
         enc_gains[2],
         dec_gains[0],
-        part(dec_qkv, 0),
-        part(dec_qkv, 1),
-        part(dec_qkv, 2),
-        dec_wout.T,
+        part(dec_first, 0),
+        part(dec_first, 1),
+        part(dec_first, 2),
+        part(dec_first, 3).T,
         dec_table_grad,
         dec_gains[1],
         part(dec_cross, 0),
@@ -708,9 +918,9 @@
         part(enc_cross, 1),
         part(dec_cross, 1).T,
         dec_gains[2],
-        dec_gate,
-        dec_up,
-        dec_down.T,
+        dec_gate[:, :units],
+        dec_up[:, :units],
+        dec_down[:, :units].T,
     )
 
 

time: 930 us -> 819 us (0.88)
  matrix products: 140 us -> 39 us
  Pallas kernels: 39 us -> 132 us
  local copies, waits for them, and re-layouts: 157 us -> 78.5 us
  starting transfers between devices: 198 us -> 130 us
  waiting for transfers between devices: 319 us -> 345 us
  between operations: 4.72 us -> 16.5 us
  other arithmetic: 59.2 us -> 68.9 us
    pallas_call x0 -> x7, Pallas kernels: none -> 93.9 us  [the longest x3 53.3 us: feed_call(): pl.pallas_call(kernel, out_shape=tuple((jax.ShapeDtypeStruct((count, cols...]
    dot_general x32 -> x13, matrix products: 123 us -> 39 us  [dot(): lax.dot_general(left, right, (dims, ((), ())), preferred_element_type=F32)]
    ppermute x39 -> x18, starting transfers between devices: 114 us -> 43.8 us  [shift(): lax.ppermute(value, 'grp', [(i, (i + hop) % self.count) for i in range(se...]
    ppermute x17, waiting for transfers between devices: 91.7 us -> 142 us  [pair_swap(): return lax.ppermute(value, 'tp', SWAP_PAIR)]
    all_to_all x0 -> x5, waiting for transfers between devices: none -> 47.3 us  [to_quarters(): lax.all_to_all(blocks, 'grp', 0, 0, tiled=True, axis_index_groups=self.ro...]
    ppermute x24 -> x8, waiting for transfers between devices: 49.4 us -> 12.1 us  [gather(): other = lax.ppermute(shard, 'grp', self.swap)]
    ppermute x6 -> x3, waiting for transfers between devices: 83.5 us -> 47.1 us  [gather(): other = lax.ppermute(held, 'grp', self.swap)]
    dynamic_update_slice x24 -> x8, local copies, waits for them, and re-layouts: 30.2 us -> 5.98 us  [gather(): lax.dynamic_update_slice(full, other[None, None], (source, 1 - self.place...]
  transfers between devices with their start and end apart: 127 -> 97, of which waited for: 47 -> 46; matrix products, arithmetic and copies ran while one was open for 28% -> 17% of each run, Pallas kernels for 2% -> 11%
where the time goes in v2:
time: 819 us; the launch traced here: 810 us
  waiting for transfers between devices  345 us (42%)
  Pallas kernels  132 us (16%)
  starting transfers between devices  130 us (16%)
  local copies, waits for them, and re-layouts  78.5 us (10%)
  other arithmetic  68.9 us (8%)
  matrix products  39 us (5%)
  between operations  16.5 us (2%)
    ppermute x17, waiting for transfers between devices, pair_swap(): return lax.ppermute(value, 'tp', SWAP_PAIR)  142 us
    ppermute x18, waiting for transfers between devices, shift(): lax.ppermute(value, 'grp', [(i, (i + hop) % self.count) for i in range(se...  55.2 us
    pallas_call x3, Pallas kernels, feed_call(): pl.pallas_call(kernel, out_shape=tuple((jax.ShapeDtypeStruct((count, cols...  53.3 us
    all_to_all x5, waiting for transfers between devices, to_quarters(): lax.all_to_all(blocks, 'grp', 0, 0, tiled=True, axis_index_groups=self.ro...  47.3 us
    ppermute x3, waiting for transfers between devices, gather(): other = lax.ppermute(held, 'grp', self.swap)  47.1 us
    ppermute x18, starting transfers between devices, shift(): lax.ppermute(value, 'grp', [(i, (i + hop) % self.count) for i in range(se...  43.8 us
    pallas_call x4, Pallas kernels, token_product(): pl.pallas_call(partial(product_kernel, groups.quarter, share, step, descr...  40.6 us
    dot_general x13, matrix products, dot(): lax.dot_general(left, right, (dims, ((), ())), preferred_element_type=F32)  39 us
  transfers between devices with their start and end apart: 97, of which 46 were waited for; matrix products, arithmetic and copies ran while one was open for 17% of the time, Pallas kernels for 11%

profile of v2, /device:TPU:0, one launch (start us, length us, event | category | flops | bytes accessed | tf_op | source)
XLA Modules:
  0.0 810.2 jit_solution(12161257078282005484)
XLA Ops:
  97.6 13.1 %collective-permute-done.15 = bf16[192,1024]{1,0:T(8,128)(2,1)S(1)} collective-permute-done((bf16[192,1024]{1,0:T(8,128)(2,1)S(1)}, bf16[192,1024]{1,0:T(8,128)(2,1)S(1)}, u32[]{:S(2)}, u32[]{:S(2)}) %collective-permute-start.15) | collective-permute-done | bytes 393248 | tf_op jit(solution)/shard_map/ppermute | solution.py:468
  133.6 16.3 %conditional.3 = ((bf16[1024,192]{1,0:T(8,128)(2,1)}, f32[8,3,128]{2,1,0:T(4,128)})) conditional(s32[]{:T(128)} %convert_element_type.258, (s32[]{:T(128)}, bf16[1024,576]{0,1:T(8,128)(2,1)}, s32[1]{0:T(128)}, f32[576,192]{1,0:T(8,128)}, f32[3,1,192]{2,1,0:T(1,128)S(1)}, /*index=5*/f32[3,192,192]{2,1,0:T(8,128)S(1)}) %tuple.236, (s32[1]{0:T(128)}, ...), branch_computations={%region_1.2_spmd, %region_2.3_spmd} | conditional | flops 6586487 | bytes 6129180 | solution.py:724
  135.3 14.6 %enc_forward.1 = (bf16[1024,192]{1,0:T(8,128)(2,1)}, f32[8,3,128]{2,1,0:T(4,128)}) custom-call(s32[1]{0:T(128)} %get-tuple-element.71.tp_ref, bf16[1024,576]{1,0:T(8,128)(2,1)S(1)} %copy.125.q_ref.kv_ref, bf16[1024,576]{1,0:T(8,128)(2,1)S(1)} %copy.125.q_ref.kv_ref, f32[1024,128]{1,0:T(8,128)} %get-tuple-element.73.idk_ref, ...), custom_call_target="tpu_custom_call" | custom-call | tf_op jit(solution)/shard_map/cond/branch_1_fun/enc_forward/pallas_call | solution.py:206
  217.4 22.6 %collective-permute-done.32 = bf16[4,192,1024]{2,1,0:T(8,128)(2,1)S(1)} collective-permute-done((bf16[4,192,1024]{2,1,0:T(8,128)(2,1)S(1)}, bf16[4,192,1024]{2,1,0:T(8,128)(2,1)S(1)}, u32[]{:S(2)}, u32[]{:S(2)}) %collective-permute-start.32) | collective-permute-done | bytes 1572896 | tf_op jit(solution)/shard_map/ppermute | solution.py:506
  247.8 24.5 %collective-permute-done.36 = bf16[4,192,1024]{2,1,0:T(8,128)(2,1)S(1)} collective-permute-done((bf16[4,192,1024]{2,1,0:T(8,128)(2,1)S(1)}, bf16[4,192,1024]{2,1,0:T(8,128)(2,1)S(1)}, u32[]{:S(2)}, u32[]{:S(2)}) %collective-permute-start.36) | collective-permute-done | bytes 1572896 | tf_op jit(solution)/shard_map/ppermute | solution.py:506
  274.2 14.7 %feed_forward.1 = (bf16[1024,1536]{1,0:T(8,128)(2,1)S(1)}, f32[1024,1024]{1,0:T(8,128)}, f32[1024,1024]{1,0:T(8,128)}) custom-call(bf16[1024,1536]{1,0:T(8,128)(2,1)} %copy-done.8, bf16[1536,1024]{1,0:T(8,128)(2,1)} %bitcast.214, bf16[1536,1024]{1,0:T(8,128)(2,1)} %bitcast.217, bf16[1536,1024]{1,0:T(8,128)(2,1)} %bitcast.211), custom_call_target="tpu_custom_call" | custom-call | tf_op jit(solution)/shard_map/feed_forward/pallas_call | solution.py:403
  293.6 19.1 %collective-permute-done.41 = bf16[256,1536]{1,0:T(8,128)(2,1)S(1)} collective-permute-done((bf16[256,1536]{1,0:T(8,128)(2,1)S(1)}, bf16[256,1536]{1,0:T(8,128)(2,1)S(1)}, u32[]{:S(2)}, u32[]{:S(2)}) %collective-permute-start.41) | collective-permute-done | bytes 786464 | tf_op jit(solution)/shard_map/ppermute | solution.py:426
  315.0 18.2 %collective-permute-done.42 = bf16[256,1536]{1,0:T(8,128)(2,1)S(1)} collective-permute-done((bf16[256,1536]{1,0:T(8,128)(2,1)S(1)}, bf16[256,1536]{1,0:T(8,128)(2,1)S(1)}, u32[]{:S(2)}, u32[]{:S(2)}) %collective-permute-start.42) | collective-permute-done | bytes 786464 | tf_op jit(solution)/shard_map/ppermute | solution.py:426
  358.8 11.0 %collective-permute-done.49 = bf16[144,1536]{1,0:T(8,128)(2,1)S(1)} collective-permute-done((bf16[144,1536]{1,0:T(8,128)(2,1)S(1)}, bf16[144,1536]{1,0:T(8,128)(2,1)S(1)}, u32[]{:S(2)}, u32[]{:S(2)}) %collective-permute-start.49) | collective-permute-done | bytes 442400 | tf_op jit(solution)/shard_map/ppermute | solution.py:426
  391.0 20.5 %feed_both.1 = (bf16[576,1536]{1,0:T(8,128)(2,1)S(1)}, bf16[576,2048]{1,0:T(8,128)(2,1)}, bf16[576,1024]{1,0:T(8,128)(2,1)S(1)}, bf16[576,1536]{1,0:T(8,128)(2,1)}) custom-call(bf16[576,1536]{1,0:T(8,128)(2,1)} %pad_maximum_fusion.9.tok_ref.refs_2_, bf16[576,1536]{1,0:T(8,128)(2,1)} %copy-done.29, bf16[1536,1024]{1,0:T(8,128)(2,1)} %bitcast.215, ...), custom_call_target="tpu_custom_call" | custom-call | tf_op jit(solution)/shard_map/feed_both/pallas_call | solution.py:403
  415.0 11.7 %collective-permute-done.57 = bf16[144,1536]{1,0:T(8,128)(2,1)S(1)} collective-permute-done((bf16[144,1536]{1,0:T(8,128)(2,1)S(1)}, bf16[144,1536]{1,0:T(8,128)(2,1)S(1)}, u32[]{:S(2)}, u32[]{:S(2)}) %collective-permute-start.57) | collective-permute-done | bytes 442400 | tf_op jit(solution)/shard_map/ppermute | solution.py:426
  428.8 10.9 %collective-permute-done.58 = bf16[144,1536]{1,0:T(8,128)(2,1)S(1)} collective-permute-done((bf16[144,1536]{1,0:T(8,128)(2,1)S(1)}, bf16[144,1536]{1,0:T(8,128)(2,1)S(1)}, u32[]{:S(2)}, u32[]{:S(2)}) %collective-permute-start.58) | collective-permute-done | bytes 442400 | tf_op jit(solution)/shard_map/ppermute | solution.py:426
  452.9 11.9 %collective-permute-done.63 = bf16[192,192]{1,0:T(8,128)(2,1)S(1)} collective-permute-done((bf16[192,192]{1,0:T(8,128)(2,1)S(1)}, bf16[192,192]{1,0:T(8,128)(2,1)S(1)}, u32[]{:S(2)}, u32[]{:S(2)}) %collective-permute-start.63) | collective-permute-done | bytes 73760 | tf_op jit(solution)/shard_map/ppermute | solution.py:474
  502.1 17.3 %collective-permute-done.71 = bf16[256,1536]{1,0:T(8,128)(2,1)S(1)} collective-permute-done((bf16[256,1536]{1,0:T(8,128)(2,1)S(1)}, bf16[256,1536]{1,0:T(8,128)(2,1)S(1)}, u32[]{:S(2)}, u32[]{:S(2)}) %collective-permute-start.71) | collective-permute-done | bytes 786464 | tf_op jit(solution)/shard_map/ppermute | solution.py:426
  523.5 18.0 %feed_back.1 = (bf16[1024,1536]{1,0:T(8,128)(2,1)}, bf16[1024,2048]{1,0:T(8,128)(2,1)}, bf16[1024,1024]{1,0:T(8,128)(2,1)S(1)}) custom-call(f32[1024,1024]{1,0:T(8,128)} %get-tuple-element.218.gate_ref, f32[1024,1024]{1,0:T(8,128)} %get-tuple-element.219.up_ref, bf16[1024,1536]{1,0:T(8,128)(2,1)} %pad_maximum_fusion.7.ga_ref.refs_0_, ...), custom_call_target="tpu_custom_call" | custom-call | tf_op jit(solution)/shard_map/feed_back/pallas_call | solution.py:403
  542.7 13.8 %token_product.5 = (bf16[2,4,192,1024]{3,2,1,0:T(8,128)(2,1)}, bf16[2,4,192,1024]{3,2,1,0:T(8,128)(2,1)}) custom-call(s32[1]{0:T(128)} %bitcast.77.role_ref, bf16[1024,1536]{1,0:T(8,128)(2,1)} %copy-done.8, bf16[1024,2048]{1,0:T(8,128)(2,1)} %get-tuple-element.222.refs_1_, bf16[576,1536]{1,0:T(8,128)(2,1)} %pad_maximum_fusion.9.tok_ref.refs_2_, ...), custom_call_target="tpu_custom_call" | custom-call | tf_op jit(solution)/shard_map/token_product/pallas_call | solution.py:309
  584.5 15.2 %all-to-all-done = bf16[4,192,384]{2,1,0:T(8,128)(2,1)} async-done(((bf16[4,192,384]{2,1,0:T(8,128)(2,1)}), bf16[4,192,384]{2,1,0:T(8,128)(2,1)}, u32[]{:S(2)}, u32[]{:S(2)}) %all-to-all-start) | async-done | bytes 589856 | tf_op jit(solution)/shard_map/all_to_all | solution.py:517
  610.4 17.2 %collective-permute-done.76 = bf16[256,1536]{1,0:T(8,128)(2,1)S(1)} collective-permute-done((bf16[256,1536]{1,0:T(8,128)(2,1)}, bf16[256,1536]{1,0:T(8,128)(2,1)S(1)}, u32[]{:S(2)}, u32[]{:S(2)}) %collective-permute-start.76) | collective-permute-done | bytes 786464 | tf_op jit(solution)/shard_map/ppermute | solution.py:426
  636.9 23.5 %conditional.4 = (bf16[1024,576]{1,0:T(8,128)(2,1)S(1)}, f32[3,81920]{1,0:T(4,128)}) conditional(s32[]{:T(128)} %convert_element_type.258, (s32[]{:T(128)}, bf16[1024,576]{0,1:T(8,128)(2,1)}, f32[8,3,128]{2,1,0:T(4,128)S(1)}, bf16[1024,192]{0,1:T(8,128)(2,1)S(1)}, s32[1]{0:T(128)}, /*index=5*/f32[576,192]{1,0:T(8,128)}, ...), branch_computations={%region_11.12_spmd, %region_12.13_spmd} | conditional | flops 16662647 | bytes 15073380 | solution.py:839
  640.8 17.3 %enc_backward.1 = (bf16[1024,192]{1,0:T(8,128)(2,1)S(1)}, bf16[1024,384]{1,0:T(8,128)(2,1)S(1)}, f32[3,5,128,128]{3,2,1,0:T(8,128)S(1)}) custom-call(s32[1]{0:T(128)} %get-tuple-element.87.tp_ref, bf16[1024,576]{1,0:T(8,128)(2,1)S(1)} %copy.135.q_ref.kv_ref, bf16[1024,576]{1,0:T(8,128)(2,1)S(1)} %copy.135.q_ref.kv_ref, f32[1024,128]{1,0:T(8,128)S(1)} %copy-done.42, ...), custom_call_target="tpu_custom_call" | custom-call | tf_op jit(solution)/shard_map/cond/branch_1_fun/enc_backward/pallas_call | solution.py:244
  683.5 10.5 %token_product.7 = bf16[2,4,192,768]{3,2,1,0:T(8,128)(2,1)} custom-call(s32[1]{0:T(128)} %bitcast.77.role_ref, bf16[1024,1536]{1,0:T(8,128)(2,1)} %copy-done.17, bf16[1024,576]{1,0:T(8,128)(2,1)S(1)} %get-tuple-element.234.refs_1_.refs_5_, bf16[1024,1536]{1,0:T(8,128)(2,1)} %copy-done.18, bf16[1024,192]{1,0:T(8,128)(2,1)} %get-tuple-element.200.refs_3_.refs_7_, ...), custom_call_target="tpu_custom_call" | custom-call | tf_op jit(solution)/shard_map/token_product/pallas_call | solution.py:309
  702.1 11.6 %collective-permute-done.80 = bf16[256,1536]{1,0:T(8,128)(2,1)} collective-permute-done((bf16[256,1536]{1,0:T(8,128)(2,1)}, bf16[256,1536]{1,0:T(8,128)(2,1)}, u32[]{:S(2)}, u32[]{:S(2)}) %collective-permute-start.80) | collective-permute-done | bytes 786464 | tf_op jit(solution)/shard_map/ppermute | solution.py:426
  731.8 28.1 %all-to-all-done.3 = bf16[4,192,1024]{2,1,0:T(8,128)(2,1)S(1)} async-done(((bf16[4,192,1024]{2,1,0:T(8,128)(2,1)}), bf16[4,192,1024]{2,1,0:T(8,128)(2,1)S(1)}, u32[]{:S(2)}, u32[]{:S(2)}) %all-to-all-start.3) | async-done | bytes 1572896 | tf_op jit(solution)/shard_map/all_to_all | solution.py:517
  784.9 10.2 %collective-permute-done.85 = f32[40,128]{1,0:T(8,128)S(1)} collective-permute-done((f32[40,128]{1,0:T(8,128)S(1)}, f32[40,128]{1,0:T(8,128)S(1)}, u32[]{:S(2)}, u32[]{:S(2)}) %collective-permute-start.85) | collective-permute-done | bytes 20512 | tf_op jit(solution)/shard_map/ppermute | solution.py:468
  (637 shorter events, 447.4 us)
Async XLA Ops:
  7.4 569.5 %reduce-scatter.6.cloned.1.call-start = ((), (), s32[]{:S(2)}) async-start(), calls=%async_computation.10 | async-start | bytes 1769472 | tf_op jit(solution)/shard_map/reduce_scatter | solution.py:540
  9.8 112.0 %collective-permute-start.1 = (bf16[256,1536]{1,0:T(8,128)(2,1)S(1)}, bf16[256,1536]{1,0:T(8,128)(2,1)}, u32[]{:S(2)}, u32[]{:S(2)}) collective-permute-start(bf16[256,1536]{1,0:T(8,128)(2,1)S(1)} %get-tuple-element.429), channel_id=1, source_target_pairs={{0,1},{1,0},{2,3},{3,2},{4,5},{5,4},{6,7},{7,6},{8,9},{9,8},{10,11... | collective-permute-start | bytes 2359304 | tf_op jit(solution)/shard_map/ppermute | solution.py:422
  10.3 77.0 %collective-permute-start = (bf16[256,1536]{1,0:T(8,128)(2,1)S(1)}, bf16[256,1536]{1,0:T(8,128)(2,1)}, u32[]{:S(2)}, u32[]{:S(2)}) collective-permute-start(bf16[256,1536]{1,0:T(8,128)(2,1)S(1)} %get-tuple-element.429), channel_id=1, source_target_pairs={{0,2},{2,0},{1,3},{3,1},{4,6},{6,4},{5,7},{7,5},{8,10},{10,8},{9,1... | collective-permute-start | bytes 2359304 | tf_op jit(solution)/shard_map/ppermute | solution.py:426
  42.3 37.8 %collective-permute-start.14 = (bf16[192,640]{1,0:T(8,128)(2,1)}, bf16[192,640]{1,0:T(8,128)(2,1)}, u32[]{:S(2)}, u32[]{:S(2)}) collective-permute-start(bf16[192,640]{1,0:T(8,128)(2,1)} %get-tuple-element.191), channel_id=1, source_target_pairs={{0,24},{4,28},{8,0},{12,4},{16,8},{20,12},{24,16},{28,20},{1,25},{... | collective-permute-start | bytes 737288 | tf_op jit(solution)/shard_map/ppermute | solution.py:468
  48.2 32.7 %collective-permute-start.12 = (bf16[192,640]{1,0:T(8,128)(2,1)}, bf16[192,640]{1,0:T(8,128)(2,1)}, u32[]{:S(2)}, u32[]{:S(2)}) collective-permute-start(bf16[192,640]{1,0:T(8,128)(2,1)} %broadcast_select_fusion.11), channel_id=1, source_target_pairs={{0,16},{4,20},{8,24},{12,28},{16,0},{20,4},{24,8},{28,12},{1,17},{... | collective-permute-start | bytes 737288 | tf_op jit(solution)/shard_map/ppermute | solution.py:468
  80.1 30.7 %collective-permute-start.11 = (bf16[192,1024]{1,0:T(8,128)(2,1)S(1)}, bf16[192,1024]{1,0:T(8,128)(2,1)S(1)}, u32[]{:S(2)}, u32[]{:S(2)}) collective-permute-start(bf16[192,1024]{1,0:T(8,128)(2,1)S(1)} %copy-done.81), channel_id=1, source_target_pairs={{0,8},{4,12},{8,16},{12,20},{16,24},{20,28},{24,0},{28,4},{1,9},{5... | collective-permute-start | bytes 1179656 | tf_op jit(solution)/shard_map/ppermute | solution.py:468
  87.3 34.5 %collective-permute-start.2 = (bf16[256,1536]{1,0:T(8,128)(2,1)}, bf16[256,1536]{1,0:T(8,128)(2,1)S(1)}, u32[]{:S(2)}, u32[]{:S(2)}) collective-permute-start(bf16[256,1536]{1,0:T(8,128)(2,1)} %collective-permute-done), channel_id=1, source_target_pairs={{0,1},{1,0},{2,3},{3,2},{4,5},{5,4},{6,7},{7,6},{8,9},{9,8},{10,11... | collective-permute-start | bytes 2359304 | tf_op jit(solution)/shard_map/ppermute | solution.py:422
  110.7 39.2 %collective-permute-start.16 = (bf16[192,1024]{1,0:T(8,128)(2,1)}, bf16[192,1024]{1,0:T(8,128)(2,1)}, u32[]{:S(2)}, u32[]{:S(2)}) collective-permute-start(bf16[192,1024]{1,0:T(8,128)(2,1)} %get-tuple-element.197), channel_id=1, source_target_pairs={{0,8},{4,12},{8,16},{12,20},{16,24},{20,28},{24,0},{28,4},{1,9},{5... | collective-permute-start | bytes 1179656 | tf_op jit(solution)/shard_map/ppermute | solution.py:468
  118.9 31.0 %collective-permute-start.17 = (bf16[192,1024]{1,0:T(8,128)(2,1)}, bf16[192,1024]{1,0:T(8,128)(2,1)}, u32[]{:S(2)}, u32[]{:S(2)}) collective-permute-start(bf16[192,1024]{1,0:T(8,128)(2,1)} %get-tuple-element.198), channel_id=1, source_target_pairs={{0,16},{4,20},{8,24},{12,28},{16,0},{20,4},{24,8},{28,12},{1,17},{... | collective-permute-start | bytes 1179656 | tf_op jit(solution)/shard_map/ppermute | solution.py:468
  120.1 29.8 %collective-permute-start.18 = (bf16[192,1024]{1,0:T(8,128)(2,1)}, bf16[192,1024]{1,0:T(8,128)(2,1)}, u32[]{:S(2)}, u32[]{:S(2)}) collective-permute-start(bf16[192,1024]{1,0:T(8,128)(2,1)} %get-tuple-element.199), channel_id=1, source_target_pairs={{0,24},{4,28},{8,0},{12,4},{16,8},{20,12},{24,16},{28,20},{1,25},{... | collective-permute-start | bytes 1179656 | tf_op jit(solution)/shard_map/ppermute | solution.py:468
  168.7 48.4 %collective-permute-start.31 = (bf16[4,192,1024]{2,1,0:T(8,128)(2,1)}, bf16[4,192,1024]{2,1,0:T(8,128)(2,1)S(1)}, u32[]{:S(2)}, u32[]{:S(2)}) collective-permute-start(bf16[4,192,1024]{2,1,0:T(8,128)(2,1)} %bitcast_dynamic-update-slice_fusion.14), channel_id=1, source_target_pairs={{0,4},{4,0},{8,12},{12,8},{16,20},{20,16},{24,28},{28,24},{1,5},{5... | collective-permute-start | bytes 4718600 | tf_op jit(solution)/shard_map/ppermute | solution.py:506
  177.4 30.4 %collective-permute-start.34 = (bf16[192,1024]{1,0:T(8,128)(2,1)S(1)}, bf16[192,1024]{1,0:T(8,128)(2,1)S(1)}, u32[]{:S(2)}, u32[]{:S(2)}) collective-permute-start(bf16[192,1024]{1,0:T(8,128)(2,1)S(1)} %copy-done.85), channel_id=1, source_target_pairs={{0,16},{4,20},{8,24},{12,28},{16,0},{20,4},{24,8},{28,12},{1,17},{... | collective-permute-start | bytes 1179656 | tf_op jit(solution)/shard_map/ppermute | solution.py:468
  185.2 54.7 %collective-permute-start.32 = (bf16[4,192,1024]{2,1,0:T(8,128)(2,1)S(1)}, bf16[4,192,1024]{2,1,0:T(8,128)(2,1)S(1)}, u32[]{:S(2)}, u32[]{:S(2)}) collective-permute-start(bf16[4,192,1024]{2,1,0:T(8,128)(2,1)S(1)} %bitcast_dynamic-update-slice_fusion.10), channel_id=1, source_target_pairs={{0,4},{4,0},{8,12},{12,8},{16,20},{20,16},{24,28},{28,24},{1,5},{5... | collective-permute-start | bytes 4718600 | tf_op jit(solution)/shard_map/ppermute | solution.py:506
  215.1 57.2 %collective-permute-start.36 = (bf16[4,192,1024]{2,1,0:T(8,128)(2,1)S(1)}, bf16[4,192,1024]{2,1,0:T(8,128)(2,1)S(1)}, u32[]{:S(2)}, u32[]{:S(2)}) collective-permute-start(bf16[4,192,1024]{2,1,0:T(8,128)(2,1)S(1)} %bitcast_dynamic-update-slice_fusion.6), channel_id=1, source_target_pairs={{0,4},{4,0},{8,12},{12,8},{16,20},{20,16},{24,28},{28,24},{1,5},{5... | collective-permute-start | bytes 4718600 | tf_op jit(solution)/shard_map/ppermute | solution.py:506
  357.3 30.7 %collective-permute-start.54 = (bf16[144,1536]{1,0:T(8,128)(2,1)S(1)}, bf16[144,1536]{1,0:T(8,128)(2,1)S(1)}, u32[]{:S(2)}, u32[]{:S(2)}) collective-permute-start(bf16[144,1536]{1,0:T(8,128)(2,1)S(1)} %bitcast.230), channel_id=1, source_target_pairs={{0,1},{1,0},{2,3},{3,2},{4,5},{5,4},{6,7},{7,6},{8,9},{9,8},{10,11... | collective-permute-start | bytes 1327112 | tf_op jit(solution)/shard_map/ppermute | solution.py:422
  494.8 132.8 %reduce-scatter.14.cloned.1.call-start = ((), (), s32[]{:S(2)}) async-start(), calls=%async_computation.14 | async-start | bytes 4718592 | tf_op jit(solution)/shard_map/reduce_scatter | solution.py:540
  556.6 117.4 %reduce-scatter.12.cloned.1.call-start = ((), (), s32[]{:S(2)}) async-start(), calls=%async_computation.13 | async-start | bytes 4718592 | tf_op jit(solution)/shard_map/reduce_scatter | solution.py:540
  583.0 136.2 %reduce-scatter.10.cloned.1.call-start = ((), (), s32[]{:S(2)}) async-start(), calls=%async_computation.12 | async-start | bytes 4718592 | tf_op jit(solution)/shard_map/reduce_scatter | solution.py:540
  627.6 43.2 %all-to-all-start.1 = ((bf16[4,192,1024]{2,1,0:T(8,128)(2,1)}), bf16[4,192,1024]{2,1,0:T(8,128)(2,1)}, u32[]{:S(2)}, u32[]{:S(2)}) async-start(bf16[4,192,1024]{2,1,0:T(8,128)(2,1)} %bitcast.235), calls=%async_computation.6 | async-start | bytes 3145728 | tf_op jit(solution)/shard_map/all_to_all | solution.py:517
  674.0 41.9 %all-to-all-start.2 = ((bf16[4,192,1024]{2,1,0:T(8,128)(2,1)}), bf16[4,192,1024]{2,1,0:T(8,128)(2,1)}, u32[]{:S(2)}, u32[]{:S(2)}) async-start(bf16[4,192,1024]{2,1,0:T(8,128)(2,1)} %bitcast.234), calls=%async_computation.7 | async-start | bytes 3145728 | tf_op jit(solution)/shard_map/all_to_all | solution.py:517
  678.4 83.3 %reduce-scatter.8.cloned.1.call-start = ((), (), s32[]{:S(2)}) async-start(), calls=%async_computation.11 | async-start | bytes 3538944 | tf_op jit(solution)/shard_map/reduce_scatter | solution.py:540
  719.1 40.8 %all-to-all-start.3 = ((bf16[4,192,1024]{2,1,0:T(8,128)(2,1)}), bf16[4,192,1024]{2,1,0:T(8,128)(2,1)S(1)}, u32[]{:S(2)}, u32[]{:S(2)}) async-start(bf16[4,192,1024]{2,1,0:T(8,128)(2,1)} %bitcast.233), calls=%async_computation.8 | async-start | bytes 3145728 | tf_op jit(solution)/shard_map/all_to_all | solution.py:517
  730.7 37.8 %collective-permute-start.83 = (f32[40,128]{1,0:T(8,128)}, f32[40,128]{1,0:T(8,128)}, u32[]{:S(2)}, u32[]{:S(2)}) collective-permute-start(f32[40,128]{1,0:T(8,128)} %fusion.106), channel_id=1, source_target_pairs={{0,4},{4,0},{8,12},{12,8},{16,20},{20,16},{24,28},{28,24},{1,5},{5... | collective-permute-start | bytes 61448 | tf_op jit(solution)/shard_map/ppermute | solution.py:523
  761.7 38.4 %all-to-all-start.4 = ((bf16[4,192,768]{2,1,0:T(8,128)(2,1)}), bf16[4,192,768]{2,1,0:T(8,128)(2,1)S(1)}, u32[]{:S(2)}, u32[]{:S(2)}) async-start(bf16[4,192,768]{2,1,0:T(8,128)(2,1)} %bitcast.249), calls=%async_computation.9 | async-start | bytes 2359296 | tf_op jit(solution)/shard_map/all_to_all | solution.py:517
  (189 other events, 2095.0 us)
Sparse Core Ops, SparseCore 0:
  494.9 28.6 reduce-scatter.5
  556.7 47.2 reduce-scatter.13
  606.2 43.3 reduce-scatter.11
  651.8 43.3 reduce-scatter.9
  697.3 34.7 reduce-scatter.7

commit v3 on v2

--- a/solution.py
+++ b/solution.py
@@ -291,8 +291,9 @@
     share = rows_count // groups.count
     step = math.gcd(share, 64)
     offsets, described, operands, specs = {}, [], [], []
-    for role, left, right in jobs:
+    for role, left, right, *block in jobs:
         count, cols = right.shape
+        cols = sum(widths) if block else cols
         described.append((role, offsets.get(role, 0)))
         offsets[role] = offsets.get(role, 0) + cols
 
@@ -302,7 +303,11 @@
         operands += [left, right]
         specs += [
             pl.BlockSpec((count, tile), left_map),
-            pl.BlockSpec((count, cols), lambda i, s: (0, 0), pipeline_mode=pl.Buffered(1)),
+            pl.BlockSpec(
+                (count, cols),
+                lambda i, s, block=(block or [0])[0]: (0, block),
+                pipeline_mode=pl.Buffered(1),
+            ),
         ]
     shapes = [(groups.quarter, 4, share, cols) for cols in widths]
     role = jnp.where(groups.is_enc, 0, 1).astype(jnp.int32)[None]
@@ -418,12 +423,20 @@
 SWAP_PAIR = [(0, 2), (2, 0), (1, 3), (3, 1)]
 
 
-def core_swap(value):
-    return lax.ppermute(value, "tp", SWAP_CORE)
-
-
-def pair_swap(value):
-    return lax.ppermute(value, "tp", SWAP_PAIR)
+def tp_swap(value, pairs, groups=None):
+    if groups is None:
+        return lax.ppermute(value, "tp", pairs)
+    size = lax.axis_size("tp")
+    flat = [(g * size + source, g * size + target) for g in groups for source, target in pairs]
+    return lax.ppermute(value, ("grp", "tp"), flat)
+
+
+def core_swap(value, groups=None):
+    return tp_swap(value, SWAP_CORE, groups)
+
+
+def pair_swap(value, groups=None):
+    return tp_swap(value, SWAP_PAIR, groups)
 
 
 def gather_tokens(own, meanwhile=None):
@@ -433,14 +446,12 @@
     return jnp.concatenate([own, far, core_swap(own), core_swap(far)], axis=0)
 
 
-def reduce_tokens(partial_bf, meanwhile=None, first=None):
+def reduce_tokens(partial_bf, meanwhile=None, groups=None):
     count = partial_bf.shape[0] // 4
-    other = core_swap(partial_bf[2 * count :])
-    if first is not None:
-        other = after(other, first(partial_bf))
+    other = core_swap(partial_bf[2 * count :], groups)
     half = partial_bf[: 2 * count].astype(F32) + other.astype(F32)
     away = half[count:].astype(BF16)
-    far = pair_swap(away)
+    far = pair_swap(away, groups)
     if meanwhile is not None:
         far = after(far, meanwhile(away))
     return half[:count] + far.astype(F32)
@@ -459,6 +470,7 @@
             [a * self.quarter + j for j in range(self.quarter)] for a in range(4)
         ]
         self.swap = [(i, i ^ 1) for i in range(self.count)]
+        self.swapped = None
         self.roles = [
             [a * self.quarter + j for a in range(4)] for j in range(self.quarter)
         ]
@@ -475,9 +487,9 @@
             value, "grp", [(source * q + j, target * q + j) for j in range(q)]
         )
 
-    def gather(self, chunks, eager):
+    def gather(self, chunks):
         fulls, last, brought = [], {}, []
-        for (enc, dec), one_by_one in zip(chunks, eager):
+        for enc, dec in chunks:
             rows, cols = enc.shape
             shards = [jnp.where(self.is_enc, enc, dec)]
             for step in (1, 2, 3):
@@ -487,10 +499,10 @@
                 last[step] = self.shift(payload, step)
                 shards.append(last[step])
             brought.append(tuple(shards[1:]))
-            sources = [(self.role - step) % 4 for step in range(4)]
             full = jnp.zeros((4, self.quarter, rows, cols), enc.dtype)
-            if one_by_one and self.quarter == 2:
-                for source, shard in zip(sources, shards):
+            for step, shard in enumerate(shards):
+                source = (self.role - step) % 4
+                if self.quarter == 2:
                     other = lax.ppermute(shard, "grp", self.swap)
                     full = lax.dynamic_update_slice(
                         full, shard[None, None], (source, self.place, 0, 0)
@@ -498,20 +510,30 @@
                     full = lax.dynamic_update_slice(
                         full, other[None, None], (source, 1 - self.place, 0, 0)
                     )
-            else:
-                held = jnp.zeros((4, rows, cols), enc.dtype)
-                for source, shard in zip(sources, shards):
-                    held = lax.dynamic_update_slice(held, shard[None], (source, 0, 0))
-                if self.quarter == 2:
-                    other = lax.ppermute(held, "grp", self.swap)
-                    full = lax.dynamic_update_slice(full, held[:, None], (0, self.place, 0, 0))
-                    full = lax.dynamic_update_slice(
-                        full, other[:, None], (0, 1 - self.place, 0, 0)
-                    )
                 else:
-                    full = lax.all_gather(held, "grp", axis=1, axis_index_groups=self.peers)
+                    group = lax.all_gather(shard, "grp", axis_index_groups=self.peers)
+                    full = lax.dynamic_update_slice(full, group[None], (source, 0, 0, 0))
             fulls.append(full.reshape(-1, cols))
         return fulls, brought
+
+    def gather_whole(self, enc, dec, pieces, *anchors):
+        rows, cols = enc.shape
+        payload = jnp.stack([enc, enc, enc, dec])
+        held = self.to_quarters(after(payload, *anchors) if anchors else payload)
+        if self.quarter == 2:
+            full = jnp.zeros((4, 2, rows, cols), enc.dtype)
+            full = lax.dynamic_update_slice(full, held[:, None], (0, self.place, 0, 0))
+            for low in range(0, 4, 4 // pieces):
+                piece = held[low : low + 4 // pieces]
+                if self.swapped is not None:
+                    piece = after(piece, self.swapped)
+                self.swapped = lax.ppermute(piece, "grp", self.swap)
+                full = lax.dynamic_update_slice(
+                    full, self.swapped[:, None], (low, 1 - self.place, 0, 0)
+                )
+        else:
+            full = lax.all_gather(held, "grp", axis=1, axis_index_groups=self.peers)
+        return full.reshape(-1, cols), held
 
     def to_quarters(self, blocks):
         return lax.all_to_all(
@@ -640,36 +662,39 @@
     units = enc_wgate.shape[1]
     padded = -units % 128
 
-    def first_chunk(weights, gains):
+    def first_chunk(weights, gains, w_out):
         gains = jnp.pad(jnp.stack(gains, axis=1), ((0, 0), (0, -len(gains) % 64)))
-        return columns(list(weights) + [gains])
-
-    def second_chunk(weights):
-        return jnp.pad(columns(weights), ((0, 0), (0, -3 * width % 128)))
+        parts = columns(list(weights) + [gains, w_out])
+        return jnp.pad(parts, ((0, 0), (0, -parts.shape[1] % 128)))
 
     def wide(weight):
         return jnp.pad(weight, ((0, 0), (0, padded)))
 
-    (first, second, w_gate, w_up, w_down), brought = groups.gather(
+    (first,), brought = groups.gather(
         [
             (
-                first_chunk([enc_wq, enc_wk, enc_wv], [enc_norm1, enc_norm2, enc_normf]),
-                first_chunk([dec_wq, dec_wk, dec_wv], [dec_norm1, dec_norm2, dec_norm3]),
+                first_chunk(
+                    [enc_wq, enc_wk, enc_wv], [enc_norm1, enc_norm2, enc_normf], enc_wo.T
+                ),
+                first_chunk(
+                    [dec_wq, dec_wk, dec_wv], [dec_norm1, dec_norm2, dec_norm3], dec_wo.T
+                ),
             ),
-            (
-                second_chunk([enc_wo.T, cross_wk, cross_wv]),
-                second_chunk([dec_wo.T, cross_wq, cross_wo.T]),
-            ),
-            (wide(enc_wgate), wide(dec_wgate)),
-            (wide(enc_wup), wide(dec_wup)),
-            (wide(enc_wdown.T), wide(dec_wdown.T)),
-        ],
-        (True, True, False, False, False),
+        ]
+    )
+    w_gate, held_gate = groups.gather_whole(
+        wide(enc_wgate), wide(dec_wgate), 2, brought[0][0]
+    )
+    w_up, held_up = groups.gather_whole(wide(enc_wup), wide(dec_wup), 2, held_gate)
+    w_down, held_down = groups.gather_whole(wide(enc_wdown.T), wide(dec_wdown.T), 2, held_up)
+    w_cross, held_cross = groups.gather_whole(
+        columns([cross_wk, cross_wv]), columns([cross_wq, cross_wo.T]), 1, held_down
     )
     w_qkv = first[:, : 3 * width]
     gains = first[:, 3 * width : 3 * width + 3].astype(F32).T
+    gains = after(gains, held_gate)
     gain1, gain2, gain3 = gains[0:1], gains[1:2], gains[2:3]
-    w_out, w_cross = second[:, :width], second[:, width : 3 * width]
+    w_out = first[:, 3 * width + 64 : 4 * width + 64]
     w_cq, w_co = w_cross[:, :width], w_cross[:, width:]
     cot_own = dec_cot[0]
     enc_table, dec_table = after((enc_table, dec_table), brought[0])
@@ -682,7 +707,6 @@
         ]
     )
     dec_ids = dec_seg[0]
-    cross_ids = sum(groups.send(dec_ids[r], 3, r) for r in range(3)).astype(F32)
     enc_hot = one_hot_blocks(enc_relative(), True)
     dec_hot = one_hot_blocks(dec_relative(), False)
     enc_bias = dot(enc_table, jnp.asarray(enc_hot, BF16), TN).reshape(heads, 5, QB, QB)
@@ -705,7 +729,6 @@
     dec_idk = jnp.broadcast_to(dec_ids.astype(F32).reshape(-1, 1), (3 * DEC_LEN, DEC_LEN))
     dec_idq = dec_ids.astype(F32).reshape(3, 1, DEC_LEN)
     cross_idk = jnp.broadcast_to(ids_rel[:, None], (enc_len, DEC_LEN))
-    cross_idq = cross_ids.reshape(1, 1, DEC_LEN)
 
     x_f32 = x_own.astype(F32)
     norm1_all = rms_scale(x_all.astype(F32), gain1).astype(BF16)
@@ -721,23 +744,31 @@
             lse.reshape(-1), (0, heads * enc_len - lse.size)
         ).reshape(enc_len // QB, heads, QB)
 
-    att, lse1 = lax.cond(is_enc, enc_attend, dec_attend, after(qkv, brought[2]))
-    x1 = x_f32 + reduce_tokens(dot(after(att, brought[3]), w_out, NT).astype(BF16))
-
-    norm2_all = gather_tokens(rms_scale(x1, gain2).astype(BF16))
+    att, lse1 = lax.cond(is_enc, enc_attend, dec_attend, after(qkv, held_gate))
+    x1 = x_f32 + reduce_tokens(dot(after(att, held_up), w_out, NT).astype(BF16))
+
+    norm2_all = gather_tokens(after(rms_scale(x1, gain2).astype(BF16), held_down))
     cot_all = gather_tokens(after(cot_own, norm2_all))
-    dec_q_rel = dot(norm2_all, w_cq, NN).astype(BF16)
-    dec_q = rows.to_rows(dec_q_rel, enc_count).reshape(3, DEC_LEN, width)
-    cross_q = sum(groups.send(dec_q[r], 3, r) for r in range(3))
-    feed_weights = (w_gate, w_up, after(w_down, cross_q, cross_ids))
+    feed_weights = (w_gate, w_up, after(w_down, held_cross))
     wide_units = w_gate.shape[1]
     width_all = x_own.shape[1]
     feed_out2, gate2, up2 = feed_call(
         "feed_forward", feed_kernel, 256, (norm2_all,), feed_weights,
         ((width_all, BF16), (wide_units, F32), (wide_units, F32)),
     )
+    queries = {}
+
+    def while_feed(anchor):
+        dec_q_rel = dot(after(norm2_all, anchor), w_cq, NN).astype(BF16)
+        dec_q = rows.to_rows(dec_q_rel, enc_count).reshape(3, DEC_LEN, width)
+        dec_q = jnp.concatenate([dec_q, dec_ids.astype(BF16)[:, :, None]], axis=2)
+        queries["sent"] = sum(groups.send(dec_q[r], 3, r) for r in range(3))
+        return queries["sent"]
+
     x2 = x1 + reduce_tokens(feed_out2)
-    memory = gather_tokens(rms_scale(x2, gain3).astype(BF16))
+    memory = gather_tokens(rms_scale(x2, gain3).astype(BF16), while_feed)
+    cross_idq = queries["sent"][:, width].astype(F32).reshape(1, 1, DEC_LEN)
+    cross_q = queries["sent"][:, :width]
 
     cross_kv = dot(memory, w_cross, NN).astype(BF16)
     cross_o, lse2 = attention_forward(cross_cfg, tp_arg, cross_q, cross_kv, cross_idk, cross_idq)
@@ -748,7 +779,7 @@
     norm3_all = gather_tokens(rms_scale(x2d, gain3).astype(BF16))
     grad_outs = ((width_all, BF16), (2 * wide_units, BF16), (wide_units, BF16))
     partial_n3, both3, hidden3, feed_out3 = feed_call(
-        "feed_both", feed_both_kernel, 192, (norm3_all, cot_all), feed_weights,
+        "feed_both", feed_both_kernel, 288, (norm3_all, cot_all), feed_weights,
         grad_outs + ((width_all, BF16),),
     )
     grad_n3 = reduce_tokens(partial_n3)
@@ -758,9 +789,9 @@
     grad_o_rel = dot(grad2_all, w_co, NN).astype(BF16)
     grad_o_rows = rows.to_rows(grad_o_rel, dec_count).reshape(3, DEC_LEN, width)
     cross_go = sum(groups.send(grad_o_rows[r], 3, r) for r in range(3))
-    dec_out = x2d + reduce_tokens(after(feed_out3, grad_o_rel))
-
-    cross_go = after(cross_go, dec_out)
+    dec_groups = range(3 * groups.quarter, groups.count)
+    dec_out = x2d + reduce_tokens(after(feed_out3, cross_go), None, dec_groups)
+
     cross_gq, cross_gkv = attention_backward(
         cross_cfg, tp_arg, cross_q, cross_kv, cross_idk, cross_idq, lse2, cross_go
     )
@@ -789,34 +820,36 @@
         "feed_back", feed_back_kernel, 256, (gate2, up2, grad_e2_all), feed_weights, grad_outs
     )
 
-    products = token_product(
-        groups,
-        (wide_units, wide_units),
-        (0, after(norm2_all, partial_n2), both2),
-        (1, norm3_all, both3),
-    )
-    for index, product in enumerate(products):
+    def input_product(index, anchor):
+        tokens, others = after((norm2_all, norm3_all), anchor)
+        (product,) = token_product(
+            groups, (wide_units,), (0, tokens, both2, index), (1, others, both3, index)
+        )
         placed[index] = groups.to_place(product)
-    dec_partial = dot(after(dec_gq_rel, products), w_cq, NT).astype(BF16)
+        return product
+
+    product = input_product(0, partial_n2)
+    dec_partial = dot(after(dec_gq_rel, product), w_cq, NT).astype(BF16)
     partial_n2 = jnp.where(is_enc, partial_n2, dec_partial)
 
     def while_n2(anchor):
-        grads, others = after((grad_e2_all, cot_all), anchor)
+        grads, others = after((grad_e2_all, cot_all), input_product(1, anchor))
         (product,) = token_product(
             groups, (wide_units,), (0, grads, hidden2), (1, others, hidden3)
         )
         placed[2] = groups.to_place(product)
-        sums["cross"] = groups.to_owner(after(placed["cross"], product))
-        return product, sums["cross"]
+        return product
 
     sums = {}
     grad_n2 = reduce_tokens(partial_n2, while_n2)
     grad_step, gain_2 = norm_backward(x1, gain2, grad_n2)
     grad_x1 = jnp.where(is_enc, grad_e2, pad_rows(grad_x2d, enc_count)) + grad_step
-    sums[0] = groups.to_owner(after(placed[0], grad_x1))
-
-    grad_x1_all = gather_tokens(grad_x1.astype(BF16))
+    sums["cross"] = groups.to_owner(after(placed["cross"], product))
+    sums[0] = groups.to_owner(after(placed[0], sums["cross"]))
+
+    grad_x1_all = gather_tokens(after(grad_x1.astype(BF16), placed[0]))
     grad_att = dot(grad_x1_all, w_out, NN).astype(BF16)
+    grad_att, sums[0] = lax.optimization_barrier((grad_att, sums[0]))
     def enc_attend_back(qkv, lse, grad_att):
         gq, gkv, gb = attention_backward(
             enc_cfg, tp_arg, qkv, qkv, enc_idk, enc_idq, lse, grad_att, enc_bias
@@ -837,7 +870,9 @@
         )
 
     grad_qkv, grad_bias = lax.cond(is_enc, enc_attend_back, dec_attend_back, qkv, lse1, grad_att)
+    sums[1] = groups.to_owner(after(placed[1], sums[0]))
     partial_n1 = dot(grad_qkv, w_qkv, NT).astype(BF16)
+    partial_n1, sums[1] = lax.optimization_barrier((partial_n1, sums[1]))
 
     def while_n1(anchor):
         left, right = after((norm1_all, grad_x1_all), anchor)
@@ -860,11 +895,11 @@
 
     tables = {}
 
-    sums[1] = groups.to_owner(after(placed[1], partial_n1, sums[0]))
+    sums[2] = groups.to_owner(after(placed[2], sums[1]))
     grad_n1 = reduce_tokens(partial_n1, while_n1)
+    grad_n1, sums[2] = lax.optimization_barrier((grad_n1, sums[2]))
     grad_step, gain_1 = norm_backward(x_f32, gain1, grad_n1)
     grad_x = grad_x1 + grad_step
-    sums[2] = groups.to_owner(after(placed[2], gain_1, sums[1]))
     enc_first, dec_first = groups.to_owner(after(placed["first"], sums[2]))
     enc_cross, dec_cross = sums["cross"]
     (enc_gate, dec_gate), (enc_up, dec_up), (enc_down, dec_down) = sums[0], sums[1], sums[2]

time: 819 us -> 763 us (0.932)
  waiting for transfers between devices: 345 us -> 290 us
  local copies, waits for them, and re-layouts: 78.5 us -> 92.8 us
  starting transfers between devices: 130 us -> 116 us
    ppermute x45 -> x49, waiting for transfers between devices: 215 us -> 168 us  [the longest x40 129 us: tp_swap(): return lax.ppermute(value, 'tp', pairs)]
    ppermute x18 -> x6, starting transfers between devices: 43.8 us -> 9.61 us  [shift(): lax.ppermute(value, 'grp', [(i, (i + hop) % self.count) for i in range(se...]
    all_to_all x5 -> x9, starting transfers between devices: 23.8 us -> 47.5 us  [to_quarters(): lax.all_to_all(blocks, 'grp', 0, 0, tiled=True, axis_index_groups=self.ro...]
    ppermute x18 -> x6, waiting for transfers between devices: 55.2 us -> 42.6 us  [shift(): lax.ppermute(value, 'grp', [(i, (i + hop) % self.count) for i in range(se...]
    ppermute x45 -> x49, starting transfers between devices: 23.4 us -> 33.6 us  [the longest x40 24.8 us: tp_swap(): return lax.ppermute(value, 'tp', pairs)]
    ppermute x15 -> x12, starting transfers between devices: 27.1 us -> 17.1 us  [send(): lax.ppermute(value, 'grp', [(source * q + j, target * q + j) for j in ran...]
    slice x9 -> x13, local copies, waits for them, and re-layouts: 3.44 us -> 11.7 us  [the longest x3 6.33 us: gather_whole(): piece = held[low:low + 4 // pieces]]
    ppermute x15 -> x12, waiting for transfers between devices: 14.6 us -> 21.6 us  [send(): lax.ppermute(value, 'grp', [(source * q + j, target * q + j) for j in ran...]
  transfers between devices with their start and end apart: 97 -> 86, of which waited for: 46 -> 46; matrix products, arithmetic and copies ran while one was open for 17% -> 21% of each run, Pallas kernels for 11% -> 12%
where the time goes in v3:
time: 763 us; the launch traced here: 752 us
  waiting for transfers between devices  290 us (38%)
  Pallas kernels  132 us (17%)
  starting transfers between devices  116 us (15%)
  local copies, waits for them, and re-layouts  92.8 us (12%)
  other arithmetic  70.1 us (9%)
  matrix products  35.1 us (5%)
  between operations  16.2 us (2%)
    ppermute x40, waiting for transfers between devices, tp_swap(): return lax.ppermute(value, 'tp', pairs)  129 us
    pallas_call x3, Pallas kernels, feed_call(): pl.pallas_call(kernel, out_shape=tuple((jax.ShapeDtypeStruct((count, cols...  49.6 us
    all_to_all x9, starting transfers between devices, to_quarters(): lax.all_to_all(blocks, 'grp', 0, 0, tiled=True, axis_index_groups=self.ro...  47.5 us
    pallas_call x5, Pallas kernels, token_product(): pl.pallas_call(partial(product_kernel, groups.quarter, share, step, descr...  44.3 us
    all_to_all x9, waiting for transfers between devices, to_quarters(): lax.all_to_all(blocks, 'grp', 0, 0, tiled=True, axis_index_groups=self.ro...  42.7 us
    ppermute x6, waiting for transfers between devices, shift(): lax.ppermute(value, 'grp', [(i, (i + hop) % self.count) for i in range(se...  42.6 us
    ppermute x7, waiting for transfers between devices, gather_whole(): self.swapped = lax.ppermute(piece, 'grp', self.swap)  39.1 us
    dot_general x13, matrix products, dot(): lax.dot_general(left, right, (dims, ((), ())), preferred_element_type=F32)  35.1 us
  transfers between devices with their start and end apart: 86, of which 46 were waited for; matrix products, arithmetic and copies ran while one was open for 21% of the time, Pallas kernels for 12%

profile of v3, /device:TPU:0, one launch (start us, length us, event | category | flops | bytes accessed | tf_op | source)
XLA Modules:
  0.0 752.0 jit_solution(16041706882928717766)
XLA Ops:
  41.5 16.3 %collective-permute-done.6 = bf16[192,896]{1,0:T(8,128)(2,1)} collective-permute-done((bf16[192,896]{1,0:T(8,128)(2,1)}, bf16[192,896]{1,0:T(8,128)(2,1)}, u32[]{:S(2)}, u32[]{:S(2)}) %collective-permute-start.6) | collective-permute-done | bytes 344096 | tf_op jit(solution)/shard_map/ppermute | solution.py:480
  72.4 10.8 %collective-permute-done.5 = bf16[192,896]{1,0:T(8,128)(2,1)S(1)} collective-permute-done((bf16[192,896]{1,0:T(8,128)(2,1)}, bf16[192,896]{1,0:T(8,128)(2,1)S(1)}, u32[]{:S(2)}, u32[]{:S(2)}) %collective-permute-start.5) | collective-permute-done | bytes 344096 | tf_op jit(solution)/shard_map/ppermute | solution.py:506
  112.1 16.2 %conditional.3 = ((bf16[1024,192]{1,0:T(8,128)(2,1)S(1)}, f32[8,3,128]{2,1,0:T(4,128)S(1)})) conditional(s32[]{:T(128)} %convert_element_type.281, (s32[]{:T(128)}, bf16[1024,576]{0,1:T(8,128)(2,1)}, s32[1]{0:T(128)}, f32[576,192]{1,0:T(8,128)}, f32[3,1,192]{2,1,0:T(1,128)S(1)}, /*index=5*/f32[3,192,192]{2,1,0:T(8,128)S(1)}) %tuple.233, (s32[1]{0:T(128)}, ...), branch_computations={%region_1.2_spmd, %region_2.3_spmd} | conditional | flops 6586487 | bytes 6129180 | solution.py:747
  114.0 14.3 %enc_forward.1 = (bf16[1024,192]{1,0:T(8,128)(2,1)S(1)}, f32[8,3,128]{2,1,0:T(4,128)S(1)}) custom-call(s32[1]{0:T(128)} %get-tuple-element.71.tp_ref, bf16[1024,576]{1,0:T(8,128)(2,1)S(1)} %copy.130.q_ref.kv_ref, bf16[1024,576]{1,0:T(8,128)(2,1)S(1)} %copy.130.q_ref.kv_ref, f32[1024,128]{1,0:T(8,128)} %get-tuple-element.73.idk_ref, ...), custom_call_target="tpu_custom_call" | custom-call | tf_op jit(solution)/shard_map/cond/branch_1_fun/enc_forward/pallas_call | solution.py:206
  152.0 15.2 %collective-permute-done.17 = bf16[2,192,1024]{2,1,0:T(8,128)(2,1)S(1)} collective-permute-done((bf16[2,192,1024]{2,1,0:T(8,128)(2,1)S(1)}, bf16[2,192,1024]{2,1,0:T(8,128)(2,1)S(1)}, u32[]{:S(2)}, u32[]{:S(2)}) %collective-permute-start.17) | collective-permute-done | bytes 786464 | tf_op jit(solution)/shard_map/ppermute | solution.py:530
  211.0 11.0 %collective-permute-done.20 = bf16[2,192,1024]{2,1,0:T(8,128)(2,1)S(1)} collective-permute-done((bf16[2,192,1024]{2,1,0:T(8,128)(2,1)S(1)}, bf16[2,192,1024]{2,1,0:T(8,128)(2,1)S(1)}, u32[]{:S(2)}, u32[]{:S(2)}) %collective-permute-start.20) | collective-permute-done | bytes 786464 | tf_op jit(solution)/shard_map/ppermute | solution.py:530
  225.9 14.8 %feed_forward.1 = (bf16[1024,1536]{1,0:T(8,128)(2,1)S(1)}, f32[1024,1024]{1,0:T(8,128)}, f32[1024,1024]{1,0:T(8,128)}) custom-call(bf16[1024,1536]{1,0:T(8,128)(2,1)} %copy-done.5, bf16[1536,1024]{1,0:T(8,128)(2,1)} %bitcast.208, bf16[1536,1024]{1,0:T(8,128)(2,1)} %bitcast.211, bf16[1536,1024]{1,0:T(8,128)(2,1)} %bitcast.54.wd_ref), custom_call_target="tpu_custom_call" | custom-call | tf_op jit(solution)/shard_map/feed_forward/pallas_call | solution.py:408
  308.5 11.0 %collective-permute-done.34 = bf16[144,1536]{1,0:T(8,128)(2,1)S(1)} collective-permute-done((bf16[144,1536]{1,0:T(8,128)(2,1)S(1)}, bf16[144,1536]{1,0:T(8,128)(2,1)S(1)}, u32[]{:S(2)}, u32[]{:S(2)}) %collective-permute-start.34) | collective-permute-done | bytes 442400 | tf_op jit(solution)/shard_map/ppermute | solution.py:428
  340.8 16.7 %feed_both.1 = (bf16[576,1536]{1,0:T(8,128)(2,1)S(1)}, bf16[576,2048]{1,0:T(8,128)(2,1)}, bf16[576,1024]{1,0:T(8,128)(2,1)S(1)}, bf16[576,1536]{1,0:T(8,128)(2,1)}) custom-call(bf16[576,1536]{1,0:T(8,128)(2,1)} %pad_maximum_fusion.7.tok_ref.refs_2_, bf16[576,1536]{1,0:T(8,128)(2,1)} %copy-done.32, bf16[1536,1024]{1,0:T(8,128)(2,1)} %bitcast.209, ...), custom_call_target="tpu_custom_call" | custom-call | tf_op jit(solution)/shard_map/feed_both/pallas_call | solution.py:408
  361.9 10.7 %collective-permute-done.42 = bf16[144,1536]{1,0:T(8,128)(2,1)S(1)} collective-permute-done((bf16[144,1536]{1,0:T(8,128)(2,1)S(1)}, bf16[144,1536]{1,0:T(8,128)(2,1)S(1)}, u32[]{:S(2)}, u32[]{:S(2)}) %collective-permute-start.42) | collective-permute-done | bytes 442400 | tf_op jit(solution)/shard_map/ppermute | solution.py:428
  376.4 9.9 %collective-permute-done.43 = bf16[144,1536]{1,0:T(8,128)(2,1)S(1)} collective-permute-done((bf16[144,1536]{1,0:T(8,128)(2,1)S(1)}, bf16[144,1536]{1,0:T(8,128)(2,1)S(1)}, u32[]{:S(2)}, u32[]{:S(2)}) %collective-permute-start.43) | collective-permute-done | bytes 442400 | tf_op jit(solution)/shard_map/ppermute | solution.py:428
  393.5 12.1 %collective-permute-done.46 = bf16[192,192]{1,0:T(8,128)(2,1)S(1)} collective-permute-done((bf16[192,192]{1,0:T(8,128)(2,1)S(1)}, bf16[192,192]{1,0:T(8,128)(2,1)S(1)}, u32[]{:S(2)}, u32[]{:S(2)}) %collective-permute-start.46) | collective-permute-done | bytes 73760 | tf_op jit(solution)/shard_map/ppermute | solution.py:486
  442.4 17.2 %collective-permute-done.56 = bf16[256,1536]{1,0:T(8,128)(2,1)S(1)} collective-permute-done((bf16[256,1536]{1,0:T(8,128)(2,1)S(1)}, bf16[256,1536]{1,0:T(8,128)(2,1)S(1)}, u32[]{:S(2)}, u32[]{:S(2)}) %collective-permute-start.56) | collective-permute-done | bytes 786464 | tf_op jit(solution)/shard_map/ppermute | solution.py:428
  463.8 18.1 %feed_back.1 = (bf16[1024,1536]{1,0:T(8,128)(2,1)}, bf16[1024,2048]{1,0:T(8,128)(2,1)}, bf16[1024,1024]{1,0:T(8,128)(2,1)S(1)}) custom-call(f32[1024,1024]{1,0:T(8,128)} %get-tuple-element.231.gate_ref, f32[1024,1024]{1,0:T(8,128)} %get-tuple-element.232.up_ref, bf16[1024,1536]{1,0:T(8,128)(2,1)} %pad_maximum_fusion.6.ga_ref.refs_0_, ...), custom_call_target="tpu_custom_call" | custom-call | tf_op jit(solution)/shard_map/feed_back/pallas_call | solution.py:408
  483.2 9.1 %token_product.6 = bf16[2,4,192,1024]{3,2,1,0:T(8,128)(2,1)} custom-call(s32[1]{0:T(128)} %bitcast.68.role_ref, bf16[1024,1536]{1,0:T(8,128)(2,1)} %copy-done.5, bf16[1024,2048]{1,0:T(8,128)(2,1)} %get-tuple-element.235.refs_1_, bf16[576,1536]{1,0:T(8,128)(2,1)} %pad_maximum_fusion.7.tok_ref.refs_2_, bf16[576,2048]{1,0:T(8,128)(2,1)} %get-tuple-element.237.refs_3_), custom_call_target="tpu_custom_call" | custom-call | tf_op jit(solution)/shard_map/token_product/pallas_call | solution.py:314
  503.3 9.1 %token_product.7 = bf16[2,4,192,1024]{3,2,1,0:T(8,128)(2,1)} custom-call(s32[1]{0:T(128)} %bitcast.68.role_ref, bf16[1024,1536]{1,0:T(8,128)(2,1)} %copy-done.5, bf16[1024,2048]{1,0:T(8,128)(2,1)} %get-tuple-element.235.refs_1_, bf16[576,1536]{1,0:T(8,128)(2,1)} %pad_maximum_fusion.7.tok_ref.refs_2_, bf16[576,2048]{1,0:T(8,128)(2,1)} %get-tuple-element.237.refs_3_), custom_call_target="tpu_custom_call" | custom-call | tf_op jit(solution)/shard_map/token_product/pallas_call | solution.py:314
  517.5 14.9 %all-to-all-done.4 = bf16[4,192,384]{2,1,0:T(8,128)(2,1)S(1)} async-done(((bf16[4,192,384]{2,1,0:T(8,128)(2,1)}), bf16[4,192,384]{2,1,0:T(8,128)(2,1)S(1)}, u32[]{:S(2)}, u32[]{:S(2)}) %all-to-all-start.4) | async-done | bytes 589856 | tf_op jit(solution)/shard_map/all_to_all | solution.py:539
  533.3 9.2 %token_product.8 = bf16[2,4,192,1024]{3,2,1,0:T(8,128)(2,1)} custom-call(s32[1]{0:T(128)} %bitcast.68.role_ref, bf16[1024,1536]{1,0:T(8,128)(2,1)} %pad_maximum_fusion.6.ga_ref.refs_0_, bf16[1024,1024]{1,0:T(8,128)(2,1)} %copy-done.2, bf16[576,1536]{1,0:T(8,128)(2,1)} %copy-done.32, bf16[576,1024]{1,0:T(8,128)(2,1)} %copy-done.3), custom_call_target="tpu_custom_call" | custom-call | tf_op jit(solution)/shard_map/token_product/pallas_call | solution.py:314
  555.6 17.3 %collective-permute-done.61 = bf16[256,1536]{1,0:T(8,128)(2,1)S(1)} collective-permute-done((bf16[256,1536]{1,0:T(8,128)(2,1)}, bf16[256,1536]{1,0:T(8,128)(2,1)S(1)}, u32[]{:S(2)}, u32[]{:S(2)}) %collective-permute-start.61) | collective-permute-done | bytes 786464 | tf_op jit(solution)/shard_map/ppermute | solution.py:428
  594.2 22.4 %conditional.4 = (bf16[1024,576]{1,0:T(8,128)(2,1)S(1)}, f32[3,81920]{1,0:T(4,128)S(1)}) conditional(s32[]{:T(128)} %convert_element_type.281, (s32[]{:T(128)}, bf16[1024,576]{0,1:T(8,128)(2,1)}, f32[8,3,128]{2,1,0:T(4,128)S(1)}, bf16[1024,192]{0,1:T(8,128)(2,1)S(1)}, s32[1]{0:T(128)}, /*index=5*/f32[576,192]{1,0:T(8,128)}, ...), branch_computations={%region_12.13_spmd, %region_13.14_spmd} | conditional | flops 16662647 | bytes 15073380 | solution.py:872
  598.0 17.3 %enc_backward.1 = (bf16[1024,192]{1,0:T(8,128)(2,1)S(1)}, bf16[1024,384]{1,0:T(8,128)(2,1)S(1)}, f32[3,5,128,128]{3,2,1,0:T(8,128)S(1)}) custom-call(s32[1]{0:T(128)} %get-tuple-element.87.tp_ref, bf16[1024,576]{1,0:T(8,128)(2,1)S(1)} %copy.147.q_ref.kv_ref, bf16[1024,576]{1,0:T(8,128)(2,1)S(1)} %copy.147.q_ref.kv_ref, f32[1024,128]{1,0:T(8,128)S(1)} %copy-done.42, ...), custom_call_target="tpu_custom_call" | custom-call | tf_op jit(solution)/shard_map/cond/branch_1_fun/enc_backward/pallas_call | solution.py:244
  648.4 9.8 %token_product.9 = bf16[2,4,192,768]{3,2,1,0:T(8,128)(2,1)} custom-call(s32[1]{0:T(128)} %bitcast.68.role_ref, bf16[1024,1536]{1,0:T(8,128)(2,1)} %copy-done.18, bf16[1024,576]{1,0:T(8,128)(2,1)S(1)} %get-tuple-element.251.refs_1_.refs_5_, bf16[1024,1536]{1,0:T(8,128)(2,1)} %copy-done.22, bf16[1024,192]{1,0:T(8,128)(2,1)S(1)} %copy-done.35, ...), custom_call_target="tpu_custom_call" | custom-call | tf_op jit(solution)/shard_map/token_product/pallas_call | solution.py:314
  694.5 14.0 %all-to-all-start.8 = ((bf16[4,192,768]{2,1,0:T(8,128)(2,1)}), bf16[4,192,768]{2,1,0:T(8,128)(2,1)S(1)}, u32[]{:S(2)}, u32[]{:S(2)}) async-start(bf16[4,192,768]{2,1,0:T(8,128)(2,1)} %bitcast.223), calls=%async_computation.13 | async-start | bytes 2359296 | tf_op jit(solution)/shard_map/all_to_all | solution.py:539
  728.3 10.3 %collective-permute-done.70 = f32[40,128]{1,0:T(8,128)S(1)} collective-permute-done((f32[40,128]{1,0:T(8,128)S(1)}, f32[40,128]{1,0:T(8,128)S(1)}, u32[]{:S(2)}, u32[]{:S(2)}) %collective-permute-start.70) | collective-permute-done | bytes 20512 | tf_op jit(solution)/shard_map/ppermute | solution.py:480
  (589 shorter events, 452.5 us)
Async XLA Ops:
  9.7 86.4 %collective-permute-start.1 = (bf16[256,1536]{1,0:T(8,128)(2,1)S(1)}, bf16[256,1536]{1,0:T(8,128)(2,1)}, u32[]{:S(2)}, u32[]{:S(2)}) collective-permute-start(bf16[256,1536]{1,0:T(8,128)(2,1)S(1)} %get-tuple-element.451), channel_id=1, source_target_pairs={{0,1},{1,0},{2,3},{3,2},{4,5},{5,4},{6,7},{7,6},{8,9},{9,8},{10,11... | collective-permute-start | bytes 2359304 | tf_op jit(solution)/shard_map/ppermute | solution.py:428
  10.2 78.8 %collective-permute-start = (bf16[256,1536]{1,0:T(8,128)(2,1)S(1)}, bf16[256,1536]{1,0:T(8,128)(2,1)}, u32[]{:S(2)}, u32[]{:S(2)}) collective-permute-start(bf16[256,1536]{1,0:T(8,128)(2,1)S(1)} %get-tuple-element.451), channel_id=1, source_target_pairs={{0,2},{2,0},{1,3},{3,1},{4,6},{6,4},{5,7},{7,5},{8,10},{10,8},{9,1... | collective-permute-start | bytes 2359304 | tf_op jit(solution)/shard_map/ppermute | solution.py:428
  15.0 25.8 %collective-permute-start.8 = (bf16[192,896]{1,0:T(8,128)(2,1)}, bf16[192,896]{1,0:T(8,128)(2,1)S(1)}, u32[]{:S(2)}, u32[]{:S(2)}) collective-permute-start(bf16[192,896]{1,0:T(8,128)(2,1)} %get-tuple-element.501), channel_id=1, source_target_pairs={{0,24},{4,28},{8,0},{12,4},{16,8},{20,12},{24,16},{28,20},{1,25},{... | collective-permute-start | bytes 1032200 | tf_op jit(solution)/shard_map/ppermute | solution.py:480
  18.6 39.2 %collective-permute-start.6 = (bf16[192,896]{1,0:T(8,128)(2,1)}, bf16[192,896]{1,0:T(8,128)(2,1)}, u32[]{:S(2)}, u32[]{:S(2)}) collective-permute-start(bf16[192,896]{1,0:T(8,128)(2,1)} %get-tuple-element.503), channel_id=1, source_target_pairs={{0,16},{4,20},{8,24},{12,28},{16,0},{20,4},{24,8},{28,12},{1,17},{... | collective-permute-start | bytes 1032200 | tf_op jit(solution)/shard_map/ppermute | solution.py:480
  35.7 31.2 %collective-permute-start.3 = (bf16[192,896]{1,0:T(8,128)(2,1)}, bf16[192,896]{1,0:T(8,128)(2,1)}, u32[]{:S(2)}, u32[]{:S(2)}) collective-permute-start(bf16[192,896]{1,0:T(8,128)(2,1)} %get-tuple-element.464), channel_id=1, source_target_pairs={{0,4},{4,0},{8,12},{12,8},{16,20},{20,16},{24,28},{28,24},{1,5},{5... | collective-permute-start | bytes 1032200 | tf_op jit(solution)/shard_map/ppermute | solution.py:506
  37.2 53.4 %all-to-all-start = ((bf16[4,192,1024]{2,1,0:T(8,128)(2,1)}), bf16[4,192,1024]{2,1,0:T(8,128)(2,1)S(1)}, u32[]{:S(2)}, u32[]{:S(2)}) async-start(bf16[4,192,1024]{2,1,0:T(8,128)(2,1)} %pad_maximum_fusion.9), calls=%async_computation | async-start | bytes 3145728 | tf_op jit(solution)/shard_map/all_to_all | solution.py:539
  64.8 25.0 %collective-permute-start.9 = (bf16[192,896]{1,0:T(8,128)(2,1)S(1)}, bf16[192,896]{1,0:T(8,128)(2,1)S(1)}, u32[]{:S(2)}, u32[]{:S(2)}) collective-permute-start(bf16[192,896]{1,0:T(8,128)(2,1)S(1)} %copy-done.62), channel_id=1, source_target_pairs={{0,4},{4,0},{8,12},{12,8},{16,20},{20,16},{24,28},{28,24},{1,5},{5... | collective-permute-start | bytes 1032200 | tf_op jit(solution)/shard_map/ppermute | solution.py:506
  66.9 21.3 %collective-permute-start.7 = (bf16[192,896]{1,0:T(8,128)(2,1)}, bf16[192,896]{1,0:T(8,128)(2,1)S(1)}, u32[]{:S(2)}, u32[]{:S(2)}) collective-permute-start(bf16[192,896]{1,0:T(8,128)(2,1)} %collective-permute-done.6), channel_id=1, source_target_pairs={{0,4},{4,0},{8,12},{12,8},{16,20},{20,16},{24,28},{28,24},{1,5},{5... | collective-permute-start | bytes 1032200 | tf_op jit(solution)/shard_map/ppermute | solution.py:506
  90.6 42.3 %all-to-all-start.1 = ((bf16[4,192,1024]{2,1,0:T(8,128)(2,1)}), bf16[4,192,1024]{2,1,0:T(8,128)(2,1)}, u32[]{:S(2)}, u32[]{:S(2)}) async-start(bf16[4,192,1024]{2,1,0:T(8,128)(2,1)} %pad_maximum_fusion.10), calls=%async_computation.1 | async-start | bytes 3145728 | tf_op jit(solution)/shard_map/all_to_all | solution.py:539
  99.4 28.9 %collective-permute-start.15 = (bf16[2,192,1024]{2,1,0:T(8,128)(2,1)}, bf16[2,192,1024]{2,1,0:T(8,128)(2,1)}, u32[]{:S(2)}, u32[]{:S(2)}) collective-permute-start(bf16[2,192,1024]{2,1,0:T(8,128)(2,1)} %get-tuple-element.493), channel_id=1, source_target_pairs={{0,4},{4,0},{8,12},{12,8},{16,20},{20,16},{24,28},{28,24},{1,5},{5... | collective-permute-start | bytes 2359304 | tf_op jit(solution)/shard_map/ppermute | solution.py:530
  136.4 31.3 %collective-permute-start.10 = (bf16[512,1536]{1,0:T(8,128)(2,1)}, bf16[512,1536]{1,0:T(8,128)(2,1)S(1)}, u32[]{:S(2)}, u32[]{:S(2)}) collective-permute-start(bf16[512,1536]{1,0:T(8,128)(2,1)} %slice.456), channel_id=1, source_target_pairs={{0,1},{1,0},{2,3},{3,2},{4,5},{5,4},{6,7},{7,6},{8,9},{9,8},{10,11... | collective-permute-start | bytes 4718600 | tf_op jit(solution)/shard_map/ppermute | solution.py:428
  138.9 41.5 %all-to-all-start.2 = ((bf16[4,192,1024]{2,1,0:T(8,128)(2,1)}), bf16[4,192,1024]{2,1,0:T(8,128)(2,1)}, u32[]{:S(2)}, u32[]{:S(2)}) async-start(bf16[4,192,1024]{2,1,0:T(8,128)(2,1)} %pad_maximum_fusion.11), calls=%async_computation.2 | async-start | bytes 3145728 | tf_op jit(solution)/shard_map/all_to_all | solution.py:539
  192.3 30.7 %all-to-all-start.3 = ((bf16[4,192,384]{2,1,0:T(8,128)(2,1)}), bf16[4,192,384]{2,1,0:T(8,128)(2,1)}, u32[]{:S(2)}, u32[]{:S(2)}) async-start(bf16[4,192,384]{2,1,0:T(8,128)(2,1)} %pad_maximum_fusion.12), calls=%async_computation.3 | async-start | bytes 1179648 | tf_op jit(solution)/shard_map/all_to_all | solution.py:539
  196.7 315.7 %reduce-scatter.8.cloned.1.call-start = ((), (), s32[]{:S(2)}) async-start(), calls=%async_computation.15 | async-start | bytes 1769472 | tf_op jit(solution)/shard_map/reduce_scatter | solution.py:562
  308.0 29.7 %collective-permute-start.39 = (bf16[144,1536]{1,0:T(8,128)(2,1)S(1)}, bf16[144,1536]{1,0:T(8,128)(2,1)S(1)}, u32[]{:S(2)}, u32[]{:S(2)}) collective-permute-start(bf16[144,1536]{1,0:T(8,128)(2,1)S(1)} %bitcast.217), channel_id=1, source_target_pairs={{0,1},{1,0},{2,3},{3,2},{4,5},{5,4},{6,7},{7,6},{8,9},{9,8},{10,11... | collective-permute-start | bytes 1327112 | tf_op jit(solution)/shard_map/ppermute | solution.py:428
  432.1 113.2 %reduce-scatter.6.cloned.1.call-start = ((), (), s32[]{:S(2)}) async-start(), calls=%async_computation.14 | async-start | bytes 4718592 | tf_op jit(solution)/shard_map/reduce_scatter | solution.py:562
  492.3 97.3 %reduce-scatter.10.cloned.1.call-start = ((), (), s32[]{:S(2)}) async-start(), calls=%async_computation.16 | async-start | bytes 4718592 | tf_op jit(solution)/shard_map/reduce_scatter | solution.py:562
  516.0 26.5 %collective-permute-start.60 = (bf16[256,1536]{1,0:T(8,128)(2,1)}, bf16[256,1536]{1,0:T(8,128)(2,1)}, u32[]{:S(2)}, u32[]{:S(2)}) collective-permute-start(bf16[256,1536]{1,0:T(8,128)(2,1)} %slice.679), channel_id=1, source_target_pairs={{0,2},{2,0},{1,3},{3,1},{4,6},{6,4},{5,7},{7,5},{8,10},{10,8},{9,1... | collective-permute-start | bytes 2359304 | tf_op jit(solution)/shard_map/ppermute | solution.py:428
  545.3 41.1 %all-to-all-start.5 = ((bf16[4,192,1024]{2,1,0:T(8,128)(2,1)}), bf16[4,192,1024]{2,1,0:T(8,128)(2,1)}, u32[]{:S(2)}, u32[]{:S(2)}) async-start(bf16[4,192,1024]{2,1,0:T(8,128)(2,1)} %bitcast.222), calls=%async_computation.7 | async-start | bytes 3145728 | tf_op jit(solution)/shard_map/all_to_all | solution.py:539
  549.6 89.2 %reduce-scatter.12.cloned.1.call-start = ((), (), s32[]{:S(2)}) async-start(), calls=%async_computation.17 | async-start | bytes 4718592 | tf_op jit(solution)/shard_map/reduce_scatter | solution.py:562
  589.6 41.1 %all-to-all-start.6 = ((bf16[4,192,1024]{2,1,0:T(8,128)(2,1)}), bf16[4,192,1024]{2,1,0:T(8,128)(2,1)}, u32[]{:S(2)}, u32[]{:S(2)}) async-start(bf16[4,192,1024]{2,1,0:T(8,128)(2,1)} %bitcast.221), calls=%async_computation.9 | async-start | bytes 3145728 | tf_op jit(solution)/shard_map/all_to_all | solution.py:539
  638.8 45.3 %all-to-all-start.7 = ((bf16[4,192,1024]{2,1,0:T(8,128)(2,1)}), bf16[4,192,1024]{2,1,0:T(8,128)(2,1)}, u32[]{:S(2)}, u32[]{:S(2)}) async-start(bf16[4,192,1024]{2,1,0:T(8,128)(2,1)} %bitcast.220), calls=%async_computation.11 | async-start | bytes 3145728 | tf_op jit(solution)/shard_map/all_to_all | solution.py:539
  643.2 51.3 %reduce-scatter.14.cloned.1.call-start = ((), (), s32[]{:S(2)}) async-start(), calls=%async_computation.18 | async-start | bytes 3538944 | tf_op jit(solution)/shard_map/reduce_scatter | solution.py:562
  694.5 47.0 %all-to-all-start.8 = ((bf16[4,192,768]{2,1,0:T(8,128)(2,1)}), bf16[4,192,768]{2,1,0:T(8,128)(2,1)S(1)}, u32[]{:S(2)}, u32[]{:S(2)}) async-start(bf16[4,192,768]{2,1,0:T(8,128)(2,1)} %bitcast.223), calls=%async_computation.13 | async-start | bytes 2359296 | tf_op jit(solution)/shard_map/all_to_all | solution.py:539
  (163 other events, 1467.8 us)
Sparse Core Ops, SparseCore 0:
  432.2 27.9 reduce-scatter.7
  492.4 44.7 reduce-scatter.5
  539.5 43.3 reduce-scatter.9
  585.1 43.3 reduce-scatter.11
  658.4 35.9 reduce-scatter.13

commit v4 on v3

--- a/solution.py
+++ b/solution.py
@@ -375,9 +375,8 @@
     out_ref[...] = dot(hidden, wd_ref[...], NT).astype(BF16)
 
 
-def feed_grads(gate, up, grads, wg_ref, wu_ref, wd_ref, gn_ref, both_ref, hid_ref):
+def feed_grads(gate, up, grad_hidden, wg_ref, wu_ref, gn_ref, both_ref, hid_ref):
     units = gate.shape[1]
-    grad_hidden = dot(grads, wd_ref[...], NN)
     activated, slope = gelu_parts(gate)
     hid_ref[...] = (activated * up).astype(BF16)
     grad_gate = (grad_hidden * up * slope).astype(BF16)
@@ -387,20 +386,16 @@
     gn_ref[...] = (dot(grad_gate, wg_ref[...], NT) + dot(grad_up, wu_ref[...], NT)).astype(BF16)
 
 
-def feed_back_kernel(gate_ref, up_ref, ga_ref, wg_ref, wu_ref, wd_ref, gn_ref, both_ref, hid_ref):
-    feed_grads(
-        gate_ref[...], up_ref[...], ga_ref[...], wg_ref, wu_ref, wd_ref, gn_ref, both_ref, hid_ref
-    )
-
-
-def feed_both_kernel(
-    tok_ref, ga_ref, wg_ref, wu_ref, wd_ref, gn_ref, both_ref, hid_ref, out_ref
-):
+def feed_back_kernel(gate_ref, up_ref, ga_ref, wg_ref, wu_ref, wd_ref, *outs):
+    grad_hidden = dot(ga_ref[...], wd_ref[...], NN)
+    feed_grads(gate_ref[...], up_ref[...], grad_hidden, wg_ref, wu_ref, *outs)
+
+
+def feed_both_kernel(tok_ref, gh_ref, wg_ref, wu_ref, *outs):
     tokens = tok_ref[...]
     gate = dot(tokens, wg_ref[...], NN)
     up = dot(tokens, wu_ref[...], NN)
-    feed_grads(gate, up, ga_ref[...], wg_ref, wu_ref, wd_ref, gn_ref, both_ref, hid_ref)
-    out_ref[...] = dot(hid_ref[...], wd_ref[...], NT).astype(BF16)
+    feed_grads(gate, up, gh_ref[...], wg_ref, wu_ref, *outs)
 
 
 def feed_call(name, kernel, tile, streamed, weights, outs):
@@ -439,11 +434,11 @@
     return tp_swap(value, SWAP_PAIR, groups)
 
 
-def gather_tokens(own, meanwhile=None):
-    far = pair_swap(own)
+def gather_tokens(own, meanwhile=None, groups=None):
+    far = pair_swap(own, groups)
     if meanwhile is not None:
         far = after(far, meanwhile(own))
-    return jnp.concatenate([own, far, core_swap(own), core_swap(far)], axis=0)
+    return jnp.concatenate([own, far, core_swap(own, groups), core_swap(far, groups)], axis=0)
 
 
 def reduce_tokens(partial_bf, meanwhile=None, groups=None):
@@ -683,10 +678,10 @@
         ]
     )
     w_gate, held_gate = groups.gather_whole(
-        wide(enc_wgate), wide(dec_wgate), 2, brought[0][0]
+        wide(enc_wgate), wide(dec_wgate), 1, brought[0][0]
     )
     w_up, held_up = groups.gather_whole(wide(enc_wup), wide(dec_wup), 2, held_gate)
-    w_down, held_down = groups.gather_whole(wide(enc_wdown.T), wide(dec_wdown.T), 2, held_up)
+    w_down, held_down = groups.gather_whole(wide(enc_wdown.T), wide(dec_wdown.T), 1, held_up)
     w_cross, held_cross = groups.gather_whole(
         columns([cross_wk, cross_wv]), columns([cross_wq, cross_wo.T]), 1, held_down
     )
@@ -697,6 +692,8 @@
     w_out = first[:, 3 * width + 64 : 4 * width + 64]
     w_cq, w_co = w_cross[:, :width], w_cross[:, width:]
     cot_own = dec_cot[0]
+    dec_groups = range(3 * groups.quarter, groups.count)
+    cot_all = gather_tokens(cot_own, None, dec_groups)
     enc_table, dec_table = after((enc_table, dec_table), brought[0])
 
     enc_ids = enc_seg[0, 0].astype(F32)
@@ -744,11 +741,10 @@
             lse.reshape(-1), (0, heads * enc_len - lse.size)
         ).reshape(enc_len // QB, heads, QB)
 
-    att, lse1 = lax.cond(is_enc, enc_attend, dec_attend, after(qkv, held_gate))
+    att, lse1 = lax.cond(is_enc, enc_attend, dec_attend, after(qkv, held_gate, cot_all))
     x1 = x_f32 + reduce_tokens(dot(after(att, held_up), w_out, NT).astype(BF16))
 
     norm2_all = gather_tokens(after(rms_scale(x1, gain2).astype(BF16), held_down))
-    cot_all = gather_tokens(after(cot_own, norm2_all))
     feed_weights = (w_gate, w_up, after(w_down, held_cross))
     wide_units = w_gate.shape[1]
     width_all = x_own.shape[1]
@@ -765,7 +761,11 @@
         queries["sent"] = sum(groups.send(dec_q[r], 3, r) for r in range(3))
         return queries["sent"]
 
-    x2 = x1 + reduce_tokens(feed_out2)
+    def while_reduce(anchor):
+        queries["hidden"] = dot(after(cot_all, anchor), feed_weights[2], NN)
+        return queries["hidden"]
+
+    x2 = x1 + reduce_tokens(feed_out2, while_reduce)
     memory = gather_tokens(rms_scale(x2, gain3).astype(BF16), while_feed)
     cross_idq = queries["sent"][:, width].astype(F32).reshape(1, 1, DEC_LEN)
     cross_q = queries["sent"][:, :width]
@@ -778,9 +778,9 @@
     x2d = x1[:dec_count] + reduce_tokens(dot(dec_o_rel, w_co, NT).astype(BF16))
     norm3_all = gather_tokens(rms_scale(x2d, gain3).astype(BF16))
     grad_outs = ((width_all, BF16), (2 * wide_units, BF16), (wide_units, BF16))
-    partial_n3, both3, hidden3, feed_out3 = feed_call(
-        "feed_both", feed_both_kernel, 288, (norm3_all, cot_all), feed_weights,
-        grad_outs + ((width_all, BF16),),
+    partial_n3, both3, hidden3 = feed_call(
+        "feed_both", feed_both_kernel, 288, (norm3_all, queries["hidden"]), feed_weights[:2],
+        grad_outs,
     )
     grad_n3 = reduce_tokens(partial_n3)
     grad_step, gain_d3 = norm_backward(x2d, gain3, grad_n3)
@@ -789,9 +789,6 @@
     grad_o_rel = dot(grad2_all, w_co, NN).astype(BF16)
     grad_o_rows = rows.to_rows(grad_o_rel, dec_count).reshape(3, DEC_LEN, width)
     cross_go = sum(groups.send(grad_o_rows[r], 3, r) for r in range(3))
-    dec_groups = range(3 * groups.quarter, groups.count)
-    dec_out = x2d + reduce_tokens(after(feed_out3, cross_go), None, dec_groups)
-
     cross_gq, cross_gkv = attention_backward(
         cross_cfg, tp_arg, cross_q, cross_kv, cross_idk, cross_idq, lse2, cross_go
     )
@@ -815,6 +812,7 @@
     grad_memory = grad_memory.astype(BF16).astype(F32)
     grad_e2, gain_ef = norm_backward(x2, gain3, grad_memory)
 
+
     grad_e2_all = gather_tokens(grad_e2.astype(BF16))
     partial_n2, both2, hidden2 = feed_call(
         "feed_back", feed_back_kernel, 256, (gate2, up2, grad_e2_all), feed_weights, grad_outs
@@ -829,6 +827,7 @@
         return product
 
     product = input_product(0, partial_n2)
+    sums = {"cross": groups.to_owner(after(placed["cross"], product))}
     dec_partial = dot(after(dec_gq_rel, product), w_cq, NT).astype(BF16)
     partial_n2 = jnp.where(is_enc, partial_n2, dec_partial)
 
@@ -838,14 +837,13 @@
             groups, (wide_units,), (0, grads, hidden2), (1, others, hidden3)
         )
         placed[2] = groups.to_place(product)
+        placed["last"] = product
         return product
 
-    sums = {}
     grad_n2 = reduce_tokens(partial_n2, while_n2)
     grad_step, gain_2 = norm_backward(x1, gain2, grad_n2)
     grad_x1 = jnp.where(is_enc, grad_e2, pad_rows(grad_x2d, enc_count)) + grad_step
-    sums["cross"] = groups.to_owner(after(placed["cross"], product))
-    sums[0] = groups.to_owner(after(placed[0], sums["cross"]))
+    sums[0] = groups.to_owner(after(placed[0], sums["cross"], placed["last"]))
 
     grad_x1_all = gather_tokens(after(grad_x1.astype(BF16), placed[0]))
     grad_att = dot(grad_x1_all, w_out, NN).astype(BF16)
@@ -870,34 +868,33 @@
         )
 
     grad_qkv, grad_bias = lax.cond(is_enc, enc_attend_back, dec_attend_back, qkv, lse1, grad_att)
+    (product,) = token_product(
+        groups,
+        (4 * width,),
+        (0, norm1_all, grad_qkv),
+        (0, grad_x1_all, att),
+        (1, norm1_all, grad_qkv),
+        (1, grad_x1_all, att),
+    )
+    placed["first"] = groups.to_place(product)
     sums[1] = groups.to_owner(after(placed[1], sums[0]))
-    partial_n1 = dot(grad_qkv, w_qkv, NT).astype(BF16)
+    partial_n1 = dot(after(grad_qkv, product), w_qkv, NT).astype(BF16)
     partial_n1, sums[1] = lax.optimization_barrier((partial_n1, sums[1]))
 
     def while_n1(anchor):
-        left, right = after((norm1_all, grad_x1_all), anchor)
-        (product,) = token_product(
-            groups,
-            (4 * width,),
-            (0, left, grad_qkv),
-            (0, right, att),
-            (1, left, grad_qkv),
-            (1, right, att),
-        )
-        placed["first"] = groups.to_place(product)
         tables["grad"] = lax.cond(
             is_enc,
             lambda gb: bucket_sums(enc_hot, gb),
             lambda gb: bucket_sums(dec_hot, gb[:, : dec_hot.shape[1]]),
-            after(grad_bias, product),
-        )
-        return product, tables["grad"]
+            after(grad_bias, anchor),
+        )
+        feed_out3 = dot(after(hidden3, tables["grad"]), feed_weights[2], NT).astype(BF16)
+        queries["out"] = x2d + reduce_tokens(feed_out3, None, dec_groups)
+        return feed_out3
 
     tables = {}
-
     sums[2] = groups.to_owner(after(placed[2], sums[1]))
     grad_n1 = reduce_tokens(partial_n1, while_n1)
-    grad_n1, sums[2] = lax.optimization_barrier((grad_n1, sums[2]))
     grad_step, gain_1 = norm_backward(x_f32, gain1, grad_n1)
     grad_x = grad_x1 + grad_step
     enc_first, dec_first = groups.to_owner(after(placed["first"], sums[2]))
@@ -910,7 +907,7 @@
     small = jnp.concatenate([gain_rows.reshape(-1), tables["grad"].reshape(-1)])
     length = small.shape[0]
     small = jnp.pad(small, (0, -length % 1024)).reshape(-1, 128)
-    enc_small, dec_small = groups.all_role_sums(small)
+    enc_small, dec_small = groups.all_role_sums(after(small, sums[2]))
 
     def unpack(total):
         flat = total.reshape(-1)
@@ -927,7 +924,7 @@
 
     zero_bf = jnp.zeros((), BF16)
     return (
-        jnp.where(is_enc, zero_bf, dec_out.astype(BF16))[None],
+        jnp.where(is_enc, zero_bf, queries["out"].astype(BF16))[None],
         jnp.where(is_enc, grad_x.astype(BF16), zero_bf)[None],
         jnp.where(is_enc, zero_bf, grad_x[:dec_count].astype(BF16))[None],
         enc_gains[0],

time: 763 us -> 745 us (0.976)
  waiting for transfers between devices: 290 us -> 254 us
  matrix products: 35.1 us -> 45.1 us
  starting transfers between devices: 116 us -> 125 us
    ppermute x7 -> x5, waiting for transfers between devices: 39.1 us -> 22.3 us  [gather_whole(): self.swapped = lax.ppermute(piece, 'grp', self.swap)]
    ppermute x6, waiting for transfers between devices: 42.6 us -> 30.2 us  [shift(): lax.ppermute(value, 'grp', [(i, (i + hop) % self.count) for i in range(se...]
    ppermute x40 -> x37, starting transfers between devices: 24.8 us -> 34.9 us  [tp_swap(): return lax.ppermute(value, 'tp', pairs)]
    dot_general x13 -> x15, matrix products: 35.1 us -> 45.1 us  [dot(): lax.dot_general(left, right, (dims, ((), ())), preferred_element_type=F32)]
    unnamed x220 -> x193, local copies, waits for them, and re-layouts: 28.6 us -> 31.5 us
    ppermute x40 -> x37, waiting for transfers between devices: 129 us -> 130 us  [tp_swap(): return lax.ppermute(value, 'tp', pairs)]
  transfers between devices with their start and end apart: 86 -> 84, of which waited for: 46 -> 44; matrix products, arithmetic and copies ran while one was open for 21% -> 23% of each run, Pallas kernels for 12% -> 13%
where the time goes in v4:
time: 745 us; the launch traced here: 733 us
  waiting for transfers between devices  254 us (34%)
  Pallas kernels  127 us (17%)
  starting transfers between devices  125 us (17%)
  local copies, waits for them, and re-layouts  96.4 us (13%)
  other arithmetic  68.2 us (9%)
  matrix products  45.1 us (6%)
  between operations  16 us (2%)
    ppermute x37, waiting for transfers between devices, tp_swap(): return lax.ppermute(value, 'tp', pairs)  130 us
    pallas_call x5, Pallas kernels, token_product(): pl.pallas_call(partial(product_kernel, groups.quarter, share, step, descr...  45.2 us
    dot_general x15, matrix products, dot(): lax.dot_general(left, right, (dims, ((), ())), preferred_element_type=F32)  45.1 us
    pallas_call x3, Pallas kernels, feed_call(): pl.pallas_call(kernel, out_shape=tuple((jax.ShapeDtypeStruct((count, cols...  44.1 us
    all_to_all x9, starting transfers between devices, to_quarters(): lax.all_to_all(blocks, 'grp', 0, 0, tiled=True, axis_index_groups=self.ro...  40.7 us
    all_to_all x9, waiting for transfers between devices, to_quarters(): lax.all_to_all(blocks, 'grp', 0, 0, tiled=True, axis_index_groups=self.ro...  36.2 us
    ppermute x37, starting transfers between devices, tp_swap(): return lax.ppermute(value, 'tp', pairs)  34.9 us
    unnamed x193, local copies, waits for them, and re-layouts  31.5 us
  transfers between devices with their start and end apart: 84, of which 44 were waited for; matrix products, arithmetic and copies ran while one was open for 23% of the time, Pallas kernels for 13%

profile of v4, /device:TPU:0, one launch (start us, length us, event | category | flops | bytes accessed | tf_op | source)
XLA Modules:
  0.0 733.0 jit_solution(553117607260429928)
XLA Ops:
  111.3 16.4 %conditional.3 = ((bf16[1024,192]{1,0:T(8,128)(2,1)S(1)}, f32[8,3,128]{2,1,0:T(4,128)S(1)})) conditional(s32[]{:T(128)} %convert_element_type.284, (s32[]{:T(128)}, bf16[1024,576]{0,1:T(8,128)(2,1)}, s32[1]{0:T(128)}, f32[576,192]{1,0:T(8,128)}, f32[3,1,192]{2,1,0:T(1,128)S(1)}, /*index=5*/f32[3,192,192]{2,1,0:T(8,128)S(1)}) %tuple.227, (s32[1]{0:T(128)}, ...), branch_computations={%region_1.2_spmd, %region_2.3_spmd} | conditional | flops 6586487 | bytes 6129180 | solution.py:744
  113.5 14.3 %enc_forward.1 = (bf16[1024,192]{1,0:T(8,128)(2,1)S(1)}, f32[8,3,128]{2,1,0:T(4,128)S(1)}) custom-call(s32[1]{0:T(128)} %get-tuple-element.71.tp_ref, bf16[1024,576]{1,0:T(8,128)(2,1)S(1)} %copy.126.q_ref.kv_ref, bf16[1024,576]{1,0:T(8,128)(2,1)S(1)} %copy.126.q_ref.kv_ref, f32[1024,128]{1,0:T(8,128)} %get-tuple-element.73.idk_ref, ...), custom_call_target="tpu_custom_call" | custom-call | tf_op jit(solution)/shard_map/cond/branch_1_fun/enc_forward/pallas_call | solution.py:206
  147.3 13.5 %collective-permute-done.19 = bf16[2,192,1024]{2,1,0:T(8,128)(2,1)S(1)} collective-permute-done((bf16[2,192,1024]{2,1,0:T(8,128)(2,1)}, bf16[2,192,1024]{2,1,0:T(8,128)(2,1)S(1)}, u32[]{:S(2)}, u32[]{:S(2)}) %collective-permute-start.19) | collective-permute-done | bytes 786464 | tf_op jit(solution)/shard_map/ppermute | solution.py:525
  219.4 14.7 %feed_forward.1 = (bf16[1024,1536]{1,0:T(8,128)(2,1)S(1)}, f32[1024,1024]{1,0:T(8,128)}, f32[1024,1024]{1,0:T(8,128)}) custom-call(bf16[1024,1536]{1,0:T(8,128)(2,1)} %copy-done.6, bf16[1536,1024]{1,0:T(8,128)(2,1)} %bitcast.202, bf16[1536,1024]{1,0:T(8,128)(2,1)} %bitcast.205, bf16[1536,1024]{1,0:T(8,128)(2,1)} %bitcast.51.wd_ref), custom_call_target="tpu_custom_call" | custom-call | tf_op jit(solution)/shard_map/feed_forward/pallas_call | solution.py:403
  273.9 8.3 %collective-permute-done.25 = bf16[192,193]{1,0:T(8,128)(2,1)S(1)} collective-permute-done((bf16[192,193]{1,0:T(8,128)(2,1)S(1)}, bf16[192,193]{1,0:T(8,128)(2,1)S(1)}, u32[]{:S(2)}, u32[]{:S(2)}) %collective-permute-start.25) | collective-permute-done | bytes 74144 | tf_op jit(solution)/shard_map/ppermute | solution.py:481
  307.1 10.8 %collective-permute-done.35 = bf16[144,1536]{1,0:T(8,128)(2,1)S(1)} collective-permute-done((bf16[144,1536]{1,0:T(8,128)(2,1)S(1)}, bf16[144,1536]{1,0:T(8,128)(2,1)S(1)}, u32[]{:S(2)}, u32[]{:S(2)}) %collective-permute-start.35) | collective-permute-done | bytes 442400 | tf_op jit(solution)/shard_map/ppermute | solution.py:423
  319.8 10.0 %collective-permute-done.36 = bf16[144,1536]{1,0:T(8,128)(2,1)S(1)} collective-permute-done((bf16[144,1536]{1,0:T(8,128)(2,1)S(1)}, bf16[144,1536]{1,0:T(8,128)(2,1)S(1)}, u32[]{:S(2)}, u32[]{:S(2)}) %collective-permute-start.36) | collective-permute-done | bytes 442400 | tf_op jit(solution)/shard_map/ppermute | solution.py:423
  332.9 11.4 %feed_both.1 = (bf16[576,1536]{1,0:T(8,128)(2,1)S(1)}, bf16[576,2048]{1,0:T(8,128)(2,1)}, bf16[576,1024]{1,0:T(8,128)(2,1)S(1)}) custom-call(bf16[576,1536]{1,0:T(8,128)(2,1)} %pad_maximum_fusion.8.tok_ref.refs_2_, f32[576,1024]{1,0:T(8,128)} %fusion.108.gh_ref, bf16[1536,1024]{1,0:T(8,128)(2,1)} %bitcast.203, bf16[1536,1024]{1,0:T(8,128)(2,1)} %bitcast.206), custom_call_target="tpu_custom_call" | custom-call | tf_op jit(solution)/shard_map/feed_both/pallas_call | solution.py:403
  348.7 10.8 %collective-permute-done.40 = bf16[144,1536]{1,0:T(8,128)(2,1)S(1)} collective-permute-done((bf16[144,1536]{1,0:T(8,128)(2,1)S(1)}, bf16[144,1536]{1,0:T(8,128)(2,1)S(1)}, u32[]{:S(2)}, u32[]{:S(2)}) %collective-permute-start.40) | collective-permute-done | bytes 442400 | tf_op jit(solution)/shard_map/ppermute | solution.py:423
  362.5 10.0 %collective-permute-done.41 = bf16[144,1536]{1,0:T(8,128)(2,1)S(1)} collective-permute-done((bf16[144,1536]{1,0:T(8,128)(2,1)S(1)}, bf16[144,1536]{1,0:T(8,128)(2,1)S(1)}, u32[]{:S(2)}, u32[]{:S(2)}) %collective-permute-start.41) | collective-permute-done | bytes 442400 | tf_op jit(solution)/shard_map/ppermute | solution.py:423
  379.7 12.1 %collective-permute-done.44 = bf16[192,192]{1,0:T(8,128)(2,1)S(1)} collective-permute-done((bf16[192,192]{1,0:T(8,128)(2,1)S(1)}, bf16[192,192]{1,0:T(8,128)(2,1)S(1)}, u32[]{:S(2)}, u32[]{:S(2)}) %collective-permute-start.44) | collective-permute-done | bytes 73760 | tf_op jit(solution)/shard_map/ppermute | solution.py:481
  428.0 17.3 %collective-permute-done.52 = bf16[256,1536]{1,0:T(8,128)(2,1)S(1)} collective-permute-done((bf16[256,1536]{1,0:T(8,128)(2,1)S(1)}, bf16[256,1536]{1,0:T(8,128)(2,1)S(1)}, u32[]{:S(2)}, u32[]{:S(2)}) %collective-permute-start.52) | collective-permute-done | bytes 786464 | tf_op jit(solution)/shard_map/ppermute | solution.py:423
  449.5 18.0 %feed_back.1 = (bf16[1024,1536]{1,0:T(8,128)(2,1)}, bf16[1024,2048]{1,0:T(8,128)(2,1)}, bf16[1024,1024]{1,0:T(8,128)(2,1)S(1)}) custom-call(f32[1024,1024]{1,0:T(8,128)} %get-tuple-element.225.gate_ref, f32[1024,1024]{1,0:T(8,128)} %get-tuple-element.226.up_ref, bf16[1024,1536]{1,0:T(8,128)(2,1)} %pad_maximum_fusion.6.ga_ref.refs_0_, ...), custom_call_target="tpu_custom_call" | custom-call | tf_op jit(solution)/shard_map/feed_back/pallas_call | solution.py:403
  468.8 9.0 %token_product.6 = bf16[2,4,192,1024]{3,2,1,0:T(8,128)(2,1)} custom-call(s32[1]{0:T(128)} %bitcast.63.role_ref, bf16[1024,1536]{1,0:T(8,128)(2,1)} %copy-done.6, bf16[1024,2048]{1,0:T(8,128)(2,1)} %get-tuple-element.229.refs_1_, bf16[576,1536]{1,0:T(8,128)(2,1)} %pad_maximum_fusion.8.tok_ref.refs_2_, bf16[576,2048]{1,0:T(8,128)(2,1)} %get-tuple-element.231.refs_3_), custom_call_target="tpu_custom_call" | custom-call | tf_op jit(solution)/shard_map/token_product/pallas_call | solution.py:314
  488.9 9.1 %token_product.7 = bf16[2,4,192,1024]{3,2,1,0:T(8,128)(2,1)} custom-call(s32[1]{0:T(128)} %bitcast.63.role_ref, bf16[1024,1536]{1,0:T(8,128)(2,1)} %copy-done.6, bf16[1024,2048]{1,0:T(8,128)(2,1)} %get-tuple-element.229.refs_1_, bf16[576,1536]{1,0:T(8,128)(2,1)} %pad_maximum_fusion.8.tok_ref.refs_2_, bf16[576,2048]{1,0:T(8,128)(2,1)} %get-tuple-element.231.refs_3_), custom_call_target="tpu_custom_call" | custom-call | tf_op jit(solution)/shard_map/token_product/pallas_call | solution.py:314
  503.0 15.0 %all-to-all-done.4 = bf16[4,192,384]{2,1,0:T(8,128)(2,1)S(1)} async-done(((bf16[4,192,384]{2,1,0:T(8,128)(2,1)}), bf16[4,192,384]{2,1,0:T(8,128)(2,1)S(1)}, u32[]{:S(2)}, u32[]{:S(2)}) %all-to-all-start.4) | async-done | bytes 589856 | tf_op jit(solution)/shard_map/all_to_all | solution.py:534
  518.9 9.2 %token_product.8 = bf16[2,4,192,1024]{3,2,1,0:T(8,128)(2,1)} custom-call(s32[1]{0:T(128)} %bitcast.63.role_ref, bf16[1024,1536]{1,0:T(8,128)(2,1)} %pad_maximum_fusion.6.ga_ref.refs_0_, bf16[1024,1024]{1,0:T(8,128)(2,1)} %copy-done.2, bf16[576,1536]{1,0:T(8,128)(2,1)} %pad_maximum_fusion.7.refs_2_, bf16[576,1024]{1,0:T(8,128)(2,1)} %copy-done.3), custom_call_target="tpu_custom_call" | custom-call | tf_op jit(solution)/shard_map/token_product/pallas_call | solution.py:314
  541.2 17.5 %collective-permute-done.57 = bf16[256,1536]{1,0:T(8,128)(2,1)S(1)} collective-permute-done((bf16[256,1536]{1,0:T(8,128)(2,1)}, bf16[256,1536]{1,0:T(8,128)(2,1)S(1)}, u32[]{:S(2)}, u32[]{:S(2)}) %collective-permute-start.57) | collective-permute-done | bytes 786464 | tf_op jit(solution)/shard_map/ppermute | solution.py:423
  579.9 22.4 %conditional.4 = (bf16[1024,576]{1,0:T(8,128)(2,1)S(1)}, f32[3,81920]{1,0:T(4,128)S(1)}) conditional(s32[]{:T(128)} %convert_element_type.284, (s32[]{:T(128)}, bf16[1024,576]{0,1:T(8,128)(2,1)}, f32[8,3,128]{2,1,0:T(4,128)S(1)}, bf16[1024,192]{0,1:T(8,128)(2,1)S(1)}, s32[1]{0:T(128)}, /*index=5*/f32[576,192]{1,0:T(8,128)}, ...), branch_computations={%region_11.12_spmd, %region_12.13_spmd} | conditional | flops 16662647 | bytes 15073380 | solution.py:870
  583.8 17.3 %enc_backward.1 = (bf16[1024,192]{1,0:T(8,128)(2,1)S(1)}, bf16[1024,384]{1,0:T(8,128)(2,1)S(1)}, f32[3,5,128,128]{3,2,1,0:T(8,128)S(1)}) custom-call(s32[1]{0:T(128)} %get-tuple-element.87.tp_ref, bf16[1024,576]{1,0:T(8,128)(2,1)S(1)} %copy.141.q_ref.kv_ref, bf16[1024,576]{1,0:T(8,128)(2,1)S(1)} %copy.141.q_ref.kv_ref, f32[1024,128]{1,0:T(8,128)S(1)} %copy-done.43, ...), custom_call_target="tpu_custom_call" | custom-call | tf_op jit(solution)/shard_map/cond/branch_1_fun/enc_backward/pallas_call | solution.py:244
  602.3 10.7 %token_product.9 = bf16[2,4,192,768]{3,2,1,0:T(8,128)(2,1)} custom-call(s32[1]{0:T(128)} %bitcast.63.role_ref, bf16[1024,1536]{1,0:T(8,128)(2,1)} %copy-done.18, bf16[1024,576]{1,0:T(8,128)(2,1)S(1)} %get-tuple-element.245.refs_1_.refs_5_, bf16[1024,1536]{1,0:T(8,128)(2,1)} %copy-done.25, bf16[1024,192]{1,0:T(8,128)(2,1)} %copy-done.36, ...), custom_call_target="tpu_custom_call" | custom-call | tf_op jit(solution)/shard_map/token_product/pallas_call | solution.py:314
  655.5 11.3 %all-to-all-done.7 = bf16[4,192,1024]{2,1,0:T(8,128)(2,1)} async-done(((bf16[4,192,1024]{2,1,0:T(8,128)(2,1)}), bf16[4,192,1024]{2,1,0:T(8,128)(2,1)}, u32[]{:S(2)}, u32[]{:S(2)}) %all-to-all-start.7) | async-done | bytes 1572896 | tf_op jit(solution)/shard_map/all_to_all | solution.py:534
  690.7 9.0 %collective-permute-done.69 = f32[40,128]{1,0:T(8,128)S(1)} collective-permute-done((f32[40,128]{1,0:T(8,128)S(1)}, f32[40,128]{1,0:T(8,128)S(1)}, u32[]{:S(2)}, u32[]{:S(2)}) %collective-permute-start.69) | collective-permute-done | bytes 20512 | tf_op jit(solution)/shard_map/ppermute | solution.py:475
  699.7 10.2 %collective-permute-done.68 = f32[40,128]{1,0:T(8,128)S(1)} collective-permute-done((f32[40,128]{1,0:T(8,128)S(1)}, f32[40,128]{1,0:T(8,128)S(1)}, u32[]{:S(2)}, u32[]{:S(2)}) %collective-permute-start.68) | collective-permute-done | bytes 20512 | tf_op jit(solution)/shard_map/ppermute | solution.py:475
  (555 shorter events, 453.3 us)
Async XLA Ops:
  7.2 86.7 %collective-permute-start.11 = (bf16[144,1536]{1,0:T(8,128)(2,1)}, bf16[144,1536]{1,0:T(8,128)(2,1)}, u32[]{:S(2)}, u32[]{:S(2)}) collective-permute-start(bf16[144,1536]{1,0:T(8,128)(2,1)} %bitcast.211), channel_id=1, source_target_pairs={{24,25},{25,24},{26,27},{27,26},{28,29},{29,28},{30,31},{31,30}} | collective-permute-start | bytes 1327112 | tf_op jit(solution)/shard_map/ppermute | solution.py:426
  8.7 68.1 %collective-permute-start.10 = (bf16[144,1536]{1,0:T(8,128)(2,1)}, bf16[144,1536]{1,0:T(8,128)(2,1)}, u32[]{:S(2)}, u32[]{:S(2)}) collective-permute-start(bf16[144,1536]{1,0:T(8,128)(2,1)} %bitcast.212), channel_id=1, source_target_pairs={{24,26},{26,24},{25,27},{27,25},{28,30},{30,28},{29,31},{31,29}} | collective-permute-start | bytes 1327112 | tf_op jit(solution)/shard_map/ppermute | solution.py:426
  19.9 31.6 %collective-permute-start.8 = (bf16[192,896]{1,0:T(8,128)(2,1)}, bf16[192,896]{1,0:T(8,128)(2,1)S(1)}, u32[]{:S(2)}, u32[]{:S(2)}) collective-permute-start(bf16[192,896]{1,0:T(8,128)(2,1)} %get-tuple-element.487), channel_id=1, source_target_pairs={{0,24},{4,28},{8,0},{12,4},{16,8},{20,12},{24,16},{28,20},{1,25},{... | collective-permute-start | bytes 1032200 | tf_op jit(solution)/shard_map/ppermute | solution.py:475
  27.5 27.0 %collective-permute-start.6 = (bf16[192,896]{1,0:T(8,128)(2,1)S(1)}, bf16[192,896]{1,0:T(8,128)(2,1)S(1)}, u32[]{:S(2)}, u32[]{:S(2)}) collective-permute-start(bf16[192,896]{1,0:T(8,128)(2,1)S(1)} %get-tuple-element.489), channel_id=1, source_target_pairs={{0,16},{4,20},{8,24},{12,28},{16,0},{20,4},{24,8},{28,12},{1,17},{... | collective-permute-start | bytes 1032200 | tf_op jit(solution)/shard_map/ppermute | solution.py:475
  44.1 52.5 %collective-permute-start.1 = (bf16[256,1536]{1,0:T(8,128)(2,1)S(1)}, bf16[256,1536]{1,0:T(8,128)(2,1)}, u32[]{:S(2)}, u32[]{:S(2)}) collective-permute-start(bf16[256,1536]{1,0:T(8,128)(2,1)S(1)} %get-tuple-element.441), channel_id=1, source_target_pairs={{0,1},{1,0},{2,3},{3,2},{4,5},{5,4},{6,7},{7,6},{8,9},{9,8},{10,11... | collective-permute-start | bytes 2359304 | tf_op jit(solution)/shard_map/ppermute | solution.py:423
  44.1 45.1 %all-to-all-start = ((bf16[4,192,1024]{2,1,0:T(8,128)(2,1)}), bf16[4,192,1024]{2,1,0:T(8,128)(2,1)}, u32[]{:S(2)}, u32[]{:S(2)}) async-start(bf16[4,192,1024]{2,1,0:T(8,128)(2,1)} %pad_maximum_fusion.10), calls=%async_computation | async-start | bytes 3145728 | tf_op jit(solution)/shard_map/all_to_all | solution.py:534
  51.5 35.2 %collective-permute-start = (bf16[256,1536]{1,0:T(8,128)(2,1)S(1)}, bf16[256,1536]{1,0:T(8,128)(2,1)}, u32[]{:S(2)}, u32[]{:S(2)}) collective-permute-start(bf16[256,1536]{1,0:T(8,128)(2,1)S(1)} %get-tuple-element.441), channel_id=1, source_target_pairs={{0,2},{2,0},{1,3},{3,1},{4,6},{6,4},{5,7},{7,5},{8,10},{10,8},{9,1... | collective-permute-start | bytes 2359304 | tf_op jit(solution)/shard_map/ppermute | solution.py:423
  89.2 40.3 %all-to-all-start.1 = ((bf16[4,192,1024]{2,1,0:T(8,128)(2,1)}), bf16[4,192,1024]{2,1,0:T(8,128)(2,1)S(1)}, u32[]{:S(2)}, u32[]{:S(2)}) async-start(bf16[4,192,1024]{2,1,0:T(8,128)(2,1)} %pad_maximum_fusion.11), calls=%async_computation.1 | async-start | bytes 3145728 | tf_op jit(solution)/shard_map/all_to_all | solution.py:534
  98.6 42.9 %collective-permute-start.18 = (bf16[4,192,1024]{2,1,0:T(8,128)(2,1)}, bf16[4,192,1024]{2,1,0:T(8,128)(2,1)}, u32[]{:S(2)}, u32[]{:S(2)}) collective-permute-start(bf16[4,192,1024]{2,1,0:T(8,128)(2,1)} %all-to-all-done), channel_id=1, source_target_pairs={{0,4},{4,0},{8,12},{12,8},{16,20},{20,16},{24,28},{28,24},{1,5},{5... | collective-permute-start | bytes 4718600 | tf_op jit(solution)/shard_map/ppermute | solution.py:525
  133.5 28.8 %collective-permute-start.13 = (bf16[512,1536]{1,0:T(8,128)(2,1)}, bf16[512,1536]{1,0:T(8,128)(2,1)S(1)}, u32[]{:S(2)}, u32[]{:S(2)}) collective-permute-start(bf16[512,1536]{1,0:T(8,128)(2,1)} %slice.440), channel_id=1, source_target_pairs={{0,1},{1,0},{2,3},{3,2},{4,5},{5,4},{6,7},{7,6},{8,9},{9,8},{10,11... | collective-permute-start | bytes 4718600 | tf_op jit(solution)/shard_map/ppermute | solution.py:423
  135.9 43.4 %all-to-all-start.2 = ((bf16[4,192,1024]{2,1,0:T(8,128)(2,1)}), bf16[4,192,1024]{2,1,0:T(8,128)(2,1)}, u32[]{:S(2)}, u32[]{:S(2)}) async-start(bf16[4,192,1024]{2,1,0:T(8,128)(2,1)} %pad_maximum_fusion.12), calls=%async_computation.2 | async-start | bytes 3145728 | tf_op jit(solution)/shard_map/all_to_all | solution.py:534
  179.2 34.5 %collective-permute-start.21 = (bf16[4,192,1024]{2,1,0:T(8,128)(2,1)}, bf16[4,192,1024]{2,1,0:T(8,128)(2,1)}, u32[]{:S(2)}, u32[]{:S(2)}) collective-permute-start(bf16[4,192,1024]{2,1,0:T(8,128)(2,1)} %all-to-all-done.2), channel_id=1, source_target_pairs={{0,4},{4,0},{8,12},{12,8},{16,20},{20,16},{24,28},{28,24},{1,5},{5... | collective-permute-start | bytes 4718600 | tf_op jit(solution)/shard_map/ppermute | solution.py:525
  199.4 298.6 %reduce-scatter.8.cloned.1.call-start = ((), (), s32[]{:S(2)}) async-start(), calls=%async_computation.15 | async-start | bytes 1769472 | tf_op jit(solution)/shard_map/reduce_scatter | solution.py:557
  418.2 112.7 %reduce-scatter.6.cloned.1.call-start = ((), (), s32[]{:S(2)}) async-start(), calls=%async_computation.14 | async-start | bytes 4718592 | tf_op jit(solution)/shard_map/reduce_scatter | solution.py:557
  477.9 97.4 %reduce-scatter.10.cloned.1.call-start = ((), (), s32[]{:S(2)}) async-start(), calls=%async_computation.16 | async-start | bytes 4718592 | tf_op jit(solution)/shard_map/reduce_scatter | solution.py:557
  501.5 26.6 %collective-permute-start.56 = (bf16[256,1536]{1,0:T(8,128)(2,1)}, bf16[256,1536]{1,0:T(8,128)(2,1)}, u32[]{:S(2)}, u32[]{:S(2)}) collective-permute-start(bf16[256,1536]{1,0:T(8,128)(2,1)} %slice.669), channel_id=1, source_target_pairs={{0,2},{2,0},{1,3},{3,1},{4,6},{6,4},{5,7},{7,5},{8,10},{10,8},{9,1... | collective-permute-start | bytes 2359304 | tf_op jit(solution)/shard_map/ppermute | solution.py:423
  530.9 41.2 %all-to-all-start.5 = ((bf16[4,192,1024]{2,1,0:T(8,128)(2,1)}), bf16[4,192,1024]{2,1,0:T(8,128)(2,1)}, u32[]{:S(2)}, u32[]{:S(2)}) async-start(bf16[4,192,1024]{2,1,0:T(8,128)(2,1)} %bitcast.216), calls=%async_computation.7 | async-start | bytes 3145728 | tf_op jit(solution)/shard_map/all_to_all | solution.py:534
  535.3 89.1 %reduce-scatter.12.cloned.1.call-start = ((), (), s32[]{:S(2)}) async-start(), calls=%async_computation.17 | async-start | bytes 4718592 | tf_op jit(solution)/shard_map/reduce_scatter | solution.py:557
  575.3 43.5 %all-to-all-start.6 = ((bf16[4,192,1024]{2,1,0:T(8,128)(2,1)}), bf16[4,192,1024]{2,1,0:T(8,128)(2,1)}, u32[]{:S(2)}, u32[]{:S(2)}) async-start(bf16[4,192,1024]{2,1,0:T(8,128)(2,1)} %bitcast.215), calls=%async_computation.9 | async-start | bytes 3145728 | tf_op jit(solution)/shard_map/all_to_all | solution.py:534
  579.8 95.6 %reduce-scatter.14.cloned.1.call-start = ((), (), s32[]{:S(2)}) async-start(), calls=%async_computation.18 | async-start | bytes 3538944 | tf_op jit(solution)/shard_map/reduce_scatter | solution.py:557
  624.4 42.4 %all-to-all-start.7 = ((bf16[4,192,1024]{2,1,0:T(8,128)(2,1)}), bf16[4,192,1024]{2,1,0:T(8,128)(2,1)}, u32[]{:S(2)}, u32[]{:S(2)}) async-start(bf16[4,192,1024]{2,1,0:T(8,128)(2,1)} %bitcast.214), calls=%async_computation.11 | async-start | bytes 3145728 | tf_op jit(solution)/shard_map/all_to_all | solution.py:534
  649.6 38.9 %collective-permute-start.61 = (bf16[288,1536]{1,0:T(8,128)(2,1)}, bf16[288,1536]{1,0:T(8,128)(2,1)S(1)}, u32[]{:S(2)}, u32[]{:S(2)}) collective-permute-start(bf16[288,1536]{1,0:T(8,128)(2,1)} %slice.484), channel_id=1, source_target_pairs={{24,25},{25,24},{26,27},{27,26},{28,29},{29,28},{30,31},{31,30}} | collective-permute-start | bytes 2654216 | tf_op jit(solution)/shard_map/ppermute | solution.py:426
  675.4 45.8 %all-to-all-start.8 = ((bf16[4,192,768]{2,1,0:T(8,128)(2,1)}), bf16[4,192,768]{2,1,0:T(8,128)(2,1)}, u32[]{:S(2)}, u32[]{:S(2)}) async-start(bf16[4,192,768]{2,1,0:T(8,128)(2,1)} %bitcast.217), calls=%async_computation.13 | async-start | bytes 2359296 | tf_op jit(solution)/shard_map/all_to_all | solution.py:534
  690.0 30.3 %collective-permute-start.62 = (bf16[144,1536]{1,0:T(8,128)(2,1)S(1)}, bf16[144,1536]{1,0:T(8,128)(2,1)S(1)}, u32[]{:S(2)}, u32[]{:S(2)}) collective-permute-start(bf16[144,1536]{1,0:T(8,128)(2,1)S(1)} %slice.673), channel_id=1, source_target_pairs={{24,26},{26,24},{25,27},{27,25},{28,30},{30,28},{29,31},{31,29}} | collective-permute-start | bytes 1327112 | tf_op jit(solution)/shard_map/ppermute | solution.py:426
  (149 other events, 1385.6 us)
Sparse Core Ops, SparseCore 0:
  418.3 28.1 reduce-scatter.7
  478.0 44.9 reduce-scatter.5
  525.2 43.3 reduce-scatter.9
  570.8 43.3 reduce-scatter.11
  624.5 35.2 reduce-scatter.13

commit v5 on v4

--- a/solution.py
+++ b/solution.py
@@ -444,12 +444,11 @@
 def reduce_tokens(partial_bf, meanwhile=None, groups=None):
     count = partial_bf.shape[0] // 4
     other = core_swap(partial_bf[2 * count :], groups)
-    half = partial_bf[: 2 * count].astype(F32) + other.astype(F32)
-    away = half[count:].astype(BF16)
+    away = (partial_bf[count : 2 * count].astype(F32) + other[count:].astype(F32)).astype(BF16)
     far = pair_swap(away, groups)
     if meanwhile is not None:
         far = after(far, meanwhile(away))
-    return half[:count] + far.astype(F32)
+    return partial_bf[:count].astype(F32) + other[:count].astype(F32) + far.astype(F32)
 
 
 class Groups:
@@ -827,7 +826,7 @@
         return product
 
     product = input_product(0, partial_n2)
-    sums = {"cross": groups.to_owner(after(placed["cross"], product))}
+    sums = {}
     dec_partial = dot(after(dec_gq_rel, product), w_cq, NT).astype(BF16)
     partial_n2 = jnp.where(is_enc, partial_n2, dec_partial)
 
@@ -837,13 +836,13 @@
             groups, (wide_units,), (0, grads, hidden2), (1, others, hidden3)
         )
         placed[2] = groups.to_place(product)
-        placed["last"] = product
+        sums["cross"] = groups.to_owner(after(placed["cross"], product))
         return product
 
     grad_n2 = reduce_tokens(partial_n2, while_n2)
     grad_step, gain_2 = norm_backward(x1, gain2, grad_n2)
     grad_x1 = jnp.where(is_enc, grad_e2, pad_rows(grad_x2d, enc_count)) + grad_step
-    sums[0] = groups.to_owner(after(placed[0], sums["cross"], placed["last"]))
+    sums[0] = groups.to_owner(after(placed[0], sums["cross"]))
 
     grad_x1_all = gather_tokens(after(grad_x1.astype(BF16), placed[0]))
     grad_att = dot(grad_x1_all, w_out, NN).astype(BF16)

time: 745 us -> 736 us (0.988)
  local copies, waits for them, and re-layouts: 96.4 us -> 82.4 us
    convert_element_type x0 -> x8, other arithmetic: none -> 10.6 us  [reduce_tokens(): (partial_bf[count:2 * count].astype(F32) + other[count:].astype(F32)).ast...]
    ppermute x37, waiting for transfers between devices: 130 us -> 140 us  [tp_swap(): return lax.ppermute(value, 'tp', pairs)]
    unnamed x193 -> x187, local copies, waits for them, and re-layouts: 31.5 us -> 25.8 us
  transfers between devices with their start and end apart: 84 -> 84, of which waited for: 44 -> 45; matrix products, arithmetic and copies ran while one was open for 23% -> 23% of each run, Pallas kernels for 13% -> 13%
where the time goes in v5:
time: 736 us; the launch traced here: 724 us
  waiting for transfers between devices  254 us (35%)
  Pallas kernels  127 us (17%)
  starting transfers between devices  123 us (17%)
  local copies, waits for them, and re-layouts  82.4 us (11%)
  other arithmetic  75.5 us (10%)
  matrix products  44.8 us (6%)
  between operations  15.9 us (2%)
    ppermute x37, waiting for transfers between devices, tp_swap(): return lax.ppermute(value, 'tp', pairs)  140 us
    pallas_call x5, Pallas kernels, token_product(): pl.pallas_call(partial(product_kernel, groups.quarter, share, step, descr...  45.1 us
    dot_general x15, matrix products, dot(): lax.dot_general(left, right, (dims, ((), ())), preferred_element_type=F32)  44.8 us
    pallas_call x3, Pallas kernels, feed_call(): pl.pallas_call(kernel, out_shape=tuple((jax.ShapeDtypeStruct((count, cols...  44.1 us
    all_to_all x9, starting transfers between devices, to_quarters(): lax.all_to_all(blocks, 'grp', 0, 0, tiled=True, axis_index_groups=self.ro...  40.8 us
    ppermute x37, starting transfers between devices, tp_swap(): return lax.ppermute(value, 'tp', pairs)  31.7 us
    all_to_all x9, waiting for transfers between devices, to_quarters(): lax.all_to_all(blocks, 'grp', 0, 0, tiled=True, axis_index_groups=self.ro...  30.4 us
    ppermute x6, waiting for transfers between devices, shift(): lax.ppermute(value, 'grp', [(i, (i + hop) % self.count) for i in range(se...  29.9 us
  transfers between devices with their start and end apart: 84, of which 45 were waited for; matrix products, arithmetic and copies ran while one was open for 23% of the time, Pallas kernels for 13%

profile of v5, /device:TPU:0, one launch (start us, length us, event | category | flops | bytes accessed | tf_op | source)
XLA Modules:
  0.0 724.2 jit_solution(3732184067416252889)
XLA Ops:
  111.3 16.4 %conditional.3 = ((bf16[1024,192]{1,0:T(8,128)(2,1)S(1)}, f32[8,3,128]{2,1,0:T(4,128)S(1)})) conditional(s32[]{:T(128)} %convert_element_type.348, (s32[]{:T(128)}, bf16[1024,576]{0,1:T(8,128)(2,1)}, s32[1]{0:T(128)}, f32[576,192]{1,0:T(8,128)}, f32[3,1,192]{2,1,0:T(1,128)S(1)}, /*index=5*/f32[3,192,192]{2,1,0:T(8,128)S(1)}) %tuple.229, (s32[1]{0:T(128)}, ...), branch_computations={%region_1.2_spmd, %region_2.3_spmd} | conditional | flops 6586487 | bytes 6129180 | solution.py:743
  113.4 14.3 %enc_forward.1 = (bf16[1024,192]{1,0:T(8,128)(2,1)S(1)}, f32[8,3,128]{2,1,0:T(4,128)S(1)}) custom-call(s32[1]{0:T(128)} %get-tuple-element.71.tp_ref, bf16[1024,576]{1,0:T(8,128)(2,1)S(1)} %copy.126.q_ref.kv_ref, bf16[1024,576]{1,0:T(8,128)(2,1)S(1)} %copy.126.q_ref.kv_ref, f32[1024,128]{1,0:T(8,128)} %get-tuple-element.73.idk_ref, ...), custom_call_target="tpu_custom_call" | custom-call | tf_op jit(solution)/shard_map/cond/branch_1_fun/enc_forward/pallas_call | solution.py:206
  147.2 13.6 %collective-permute-done.19 = bf16[2,192,1024]{2,1,0:T(8,128)(2,1)S(1)} collective-permute-done((bf16[2,192,1024]{2,1,0:T(8,128)(2,1)}, bf16[2,192,1024]{2,1,0:T(8,128)(2,1)S(1)}, u32[]{:S(2)}, u32[]{:S(2)}) %collective-permute-start.19) | collective-permute-done | bytes 786464 | tf_op jit(solution)/shard_map/ppermute | solution.py:524
  180.7 8.8 %collective-permute-done.14 = bf16[256,1536]{1,0:T(8,128)(2,1)} collective-permute-done((bf16[256,1536]{1,0:T(8,128)(2,1)}, bf16[256,1536]{1,0:T(8,128)(2,1)}, u32[]{:S(2)}, u32[]{:S(2)}) %collective-permute-start.14) | collective-permute-done | bytes 786464 | tf_op jit(solution)/shard_map/ppermute | solution.py:423
  219.3 14.7 %feed_forward.1 = (bf16[1024,1536]{1,0:T(8,128)(2,1)S(1)}, f32[1024,1024]{1,0:T(8,128)}, f32[1024,1024]{1,0:T(8,128)}) custom-call(bf16[1024,1536]{1,0:T(8,128)(2,1)} %copy-done.6, bf16[1536,1024]{1,0:T(8,128)(2,1)} %bitcast.202, bf16[1536,1024]{1,0:T(8,128)(2,1)} %bitcast.205, bf16[1536,1024]{1,0:T(8,128)(2,1)} %bitcast.51.wd_ref), custom_call_target="tpu_custom_call" | custom-call | tf_op jit(solution)/shard_map/feed_forward/pallas_call | solution.py:403
  308.3 10.8 %collective-permute-done.35 = bf16[144,1536]{1,0:T(8,128)(2,1)S(1)} collective-permute-done((bf16[144,1536]{1,0:T(8,128)(2,1)S(1)}, bf16[144,1536]{1,0:T(8,128)(2,1)S(1)}, u32[]{:S(2)}, u32[]{:S(2)}) %collective-permute-start.35) | collective-permute-done | bytes 442400 | tf_op jit(solution)/shard_map/ppermute | solution.py:423
  321.1 10.0 %collective-permute-done.36 = bf16[144,1536]{1,0:T(8,128)(2,1)S(1)} collective-permute-done((bf16[144,1536]{1,0:T(8,128)(2,1)S(1)}, bf16[144,1536]{1,0:T(8,128)(2,1)S(1)}, u32[]{:S(2)}, u32[]{:S(2)}) %collective-permute-start.36) | collective-permute-done | bytes 442400 | tf_op jit(solution)/shard_map/ppermute | solution.py:423
  334.1 11.4 %feed_both.1 = (bf16[576,1536]{1,0:T(8,128)(2,1)S(1)}, bf16[576,2048]{1,0:T(8,128)(2,1)}, bf16[576,1024]{1,0:T(8,128)(2,1)S(1)}) custom-call(bf16[576,1536]{1,0:T(8,128)(2,1)} %pad_maximum_fusion.8.tok_ref.refs_2_, f32[576,1024]{1,0:T(8,128)} %fusion.100.gh_ref, bf16[1536,1024]{1,0:T(8,128)(2,1)} %bitcast.203, bf16[1536,1024]{1,0:T(8,128)(2,1)} %bitcast.206), custom_call_target="tpu_custom_call" | custom-call | tf_op jit(solution)/shard_map/feed_both/pallas_call | solution.py:403
  349.7 10.8 %collective-permute-done.40 = bf16[144,1536]{1,0:T(8,128)(2,1)S(1)} collective-permute-done((bf16[144,1536]{1,0:T(8,128)(2,1)S(1)}, bf16[144,1536]{1,0:T(8,128)(2,1)S(1)}, u32[]{:S(2)}, u32[]{:S(2)}) %collective-permute-start.40) | collective-permute-done | bytes 442400 | tf_op jit(solution)/shard_map/ppermute | solution.py:423
  363.7 10.0 %collective-permute-done.41 = bf16[144,1536]{1,0:T(8,128)(2,1)S(1)} collective-permute-done((bf16[144,1536]{1,0:T(8,128)(2,1)S(1)}, bf16[144,1536]{1,0:T(8,128)(2,1)S(1)}, u32[]{:S(2)}, u32[]{:S(2)}) %collective-permute-start.41) | collective-permute-done | bytes 442400 | tf_op jit(solution)/shard_map/ppermute | solution.py:423
  380.9 12.1 %collective-permute-done.44 = bf16[192,192]{1,0:T(8,128)(2,1)S(1)} collective-permute-done((bf16[192,192]{1,0:T(8,128)(2,1)S(1)}, bf16[192,192]{1,0:T(8,128)(2,1)S(1)}, u32[]{:S(2)}, u32[]{:S(2)}) %collective-permute-start.44) | collective-permute-done | bytes 73760 | tf_op jit(solution)/shard_map/ppermute | solution.py:480
  429.3 17.3 %collective-permute-done.52 = bf16[256,1536]{1,0:T(8,128)(2,1)S(1)} collective-permute-done((bf16[256,1536]{1,0:T(8,128)(2,1)S(1)}, bf16[256,1536]{1,0:T(8,128)(2,1)S(1)}, u32[]{:S(2)}, u32[]{:S(2)}) %collective-permute-start.52) | collective-permute-done | bytes 786464 | tf_op jit(solution)/shard_map/ppermute | solution.py:423
  450.8 18.0 %feed_back.1 = (bf16[1024,1536]{1,0:T(8,128)(2,1)}, bf16[1024,2048]{1,0:T(8,128)(2,1)}, bf16[1024,1024]{1,0:T(8,128)(2,1)S(1)}) custom-call(f32[1024,1024]{1,0:T(8,128)} %get-tuple-element.225.gate_ref, f32[1024,1024]{1,0:T(8,128)} %get-tuple-element.226.up_ref, bf16[1024,1536]{1,0:T(8,128)(2,1)} %pad_maximum_fusion.6.ga_ref.refs_0_, ...), custom_call_target="tpu_custom_call" | custom-call | tf_op jit(solution)/shard_map/feed_back/pallas_call | solution.py:403
  470.1 9.0 %token_product.6 = bf16[2,4,192,1024]{3,2,1,0:T(8,128)(2,1)} custom-call(s32[1]{0:T(128)} %bitcast.63.role_ref, bf16[1024,1536]{1,0:T(8,128)(2,1)} %copy-done.6, bf16[1024,2048]{1,0:T(8,128)(2,1)} %get-tuple-element.229.refs_1_, bf16[576,1536]{1,0:T(8,128)(2,1)} %pad_maximum_fusion.8.tok_ref.refs_2_, bf16[576,2048]{1,0:T(8,128)(2,1)} %get-tuple-element.231.refs_3_), custom_call_target="tpu_custom_call" | custom-call | tf_op jit(solution)/shard_map/token_product/pallas_call | solution.py:314
  489.3 9.1 %token_product.7 = bf16[2,4,192,1024]{3,2,1,0:T(8,128)(2,1)} custom-call(s32[1]{0:T(128)} %bitcast.63.role_ref, bf16[1024,1536]{1,0:T(8,128)(2,1)} %copy-done.6, bf16[1024,2048]{1,0:T(8,128)(2,1)} %get-tuple-element.229.refs_1_, bf16[576,1536]{1,0:T(8,128)(2,1)} %pad_maximum_fusion.8.tok_ref.refs_2_, bf16[576,2048]{1,0:T(8,128)(2,1)} %get-tuple-element.231.refs_3_), custom_call_target="tpu_custom_call" | custom-call | tf_op jit(solution)/shard_map/token_product/pallas_call | solution.py:314
  499.9 9.1 %token_product.8 = bf16[2,4,192,1024]{3,2,1,0:T(8,128)(2,1)} custom-call(s32[1]{0:T(128)} %bitcast.63.role_ref, bf16[1024,1536]{1,0:T(8,128)(2,1)} %pad_maximum_fusion.6.ga_ref.refs_0_, bf16[1024,1024]{1,0:T(8,128)(2,1)} %copy-done.2, bf16[576,1536]{1,0:T(8,128)(2,1)} %pad_maximum_fusion.7.refs_2_, bf16[576,1024]{1,0:T(8,128)(2,1)} %copy-done.3), custom_call_target="tpu_custom_call" | custom-call | tf_op jit(solution)/shard_map/token_product/pallas_call | solution.py:314
  520.7 8.7 %all-to-all-done.4 = bf16[4,192,384]{2,1,0:T(8,128)(2,1)} async-done(((bf16[4,192,384]{2,1,0:T(8,128)(2,1)}), bf16[4,192,384]{2,1,0:T(8,128)(2,1)}, u32[]{:S(2)}, u32[]{:S(2)}) %all-to-all-start.4) | async-done | bytes 589856 | tf_op jit(solution)/shard_map/all_to_all | solution.py:533
  540.8 17.9 %collective-permute-done.57 = bf16[256,1536]{1,0:T(8,128)(2,1)S(1)} collective-permute-done((bf16[256,1536]{1,0:T(8,128)(2,1)S(1)}, bf16[256,1536]{1,0:T(8,128)(2,1)S(1)}, u32[]{:S(2)}, u32[]{:S(2)}) %collective-permute-start.57) | collective-permute-done | bytes 786464 | tf_op jit(solution)/shard_map/ppermute | solution.py:423
  580.4 22.4 %conditional.4 = (bf16[1024,576]{1,0:T(8,128)(2,1)S(1)}, f32[3,81920]{1,0:T(4,128)S(1)}) conditional(s32[]{:T(128)} %convert_element_type.348, (s32[]{:T(128)}, bf16[1024,576]{0,1:T(8,128)(2,1)}, f32[8,3,128]{2,1,0:T(4,128)S(1)}, bf16[1024,192]{0,1:T(8,128)(2,1)S(1)}, s32[1]{0:T(128)}, /*index=5*/f32[576,192]{1,0:T(8,128)}, ...), branch_computations={%region_11.12_spmd, %region_12.13_spmd} | conditional | flops 16662647 | bytes 15073380 | solution.py:869
  584.2 17.3 %enc_backward.1 = (bf16[1024,192]{1,0:T(8,128)(2,1)S(1)}, bf16[1024,384]{1,0:T(8,128)(2,1)S(1)}, f32[3,5,128,128]{3,2,1,0:T(8,128)S(1)}) custom-call(s32[1]{0:T(128)} %get-tuple-element.87.tp_ref, bf16[1024,576]{1,0:T(8,128)(2,1)S(1)} %copy.141.q_ref.kv_ref, bf16[1024,576]{1,0:T(8,128)(2,1)S(1)} %copy.141.q_ref.kv_ref, f32[1024,128]{1,0:T(8,128)S(1)} %copy-done.38, ...), custom_call_target="tpu_custom_call" | custom-call | tf_op jit(solution)/shard_map/cond/branch_1_fun/enc_backward/pallas_call | solution.py:244
  602.8 10.7 %token_product.9 = bf16[2,4,192,768]{3,2,1,0:T(8,128)(2,1)} custom-call(s32[1]{0:T(128)} %bitcast.63.role_ref, bf16[1024,1536]{1,0:T(8,128)(2,1)} %copy-done.18, bf16[1024,576]{1,0:T(8,128)(2,1)S(1)} %get-tuple-element.245.refs_1_.refs_5_, bf16[1024,1536]{1,0:T(8,128)(2,1)} %copy-done.21, bf16[1024,192]{1,0:T(8,128)(2,1)} %copy-done.29, ...), custom_call_target="tpu_custom_call" | custom-call | tf_op jit(solution)/shard_map/token_product/pallas_call | solution.py:314
  656.0 11.4 %all-to-all-done.7 = bf16[4,192,1024]{2,1,0:T(8,128)(2,1)} async-done(((bf16[4,192,1024]{2,1,0:T(8,128)(2,1)}), bf16[4,192,1024]{2,1,0:T(8,128)(2,1)}, u32[]{:S(2)}, u32[]{:S(2)}) %all-to-all-start.7) | async-done | bytes 1572896 | tf_op jit(solution)/shard_map/all_to_all | solution.py:533
  689.1 9.2 %collective-permute-done.69 = f32[40,128]{1,0:T(8,128)S(1)} collective-permute-done((f32[40,128]{1,0:T(8,128)S(1)}, f32[40,128]{1,0:T(8,128)S(1)}, u32[]{:S(2)}, u32[]{:S(2)}) %collective-permute-start.69) | collective-permute-done | bytes 20512 | tf_op jit(solution)/shard_map/ppermute | solution.py:474
  698.3 10.2 %collective-permute-done.68 = f32[40,128]{1,0:T(8,128)S(1)} collective-permute-done((f32[40,128]{1,0:T(8,128)S(1)}, f32[40,128]{1,0:T(8,128)S(1)}, u32[]{:S(2)}, u32[]{:S(2)}) %collective-permute-start.68) | collective-permute-done | bytes 20512 | tf_op jit(solution)/shard_map/ppermute | solution.py:474
  (541 shorter events, 449.3 us)
Async XLA Ops:
  7.2 86.7 %collective-permute-start.11 = (bf16[144,1536]{1,0:T(8,128)(2,1)}, bf16[144,1536]{1,0:T(8,128)(2,1)}, u32[]{:S(2)}, u32[]{:S(2)}) collective-permute-start(bf16[144,1536]{1,0:T(8,128)(2,1)} %bitcast.211), channel_id=1, source_target_pairs={{24,25},{25,24},{26,27},{27,26},{28,29},{29,28},{30,31},{31,30}} | collective-permute-start | bytes 1327112 | tf_op jit(solution)/shard_map/ppermute | solution.py:426
  8.7 68.1 %collective-permute-start.10 = (bf16[144,1536]{1,0:T(8,128)(2,1)}, bf16[144,1536]{1,0:T(8,128)(2,1)}, u32[]{:S(2)}, u32[]{:S(2)}) collective-permute-start(bf16[144,1536]{1,0:T(8,128)(2,1)} %bitcast.212), channel_id=1, source_target_pairs={{24,26},{26,24},{25,27},{27,25},{28,30},{30,28},{29,31},{31,29}} | collective-permute-start | bytes 1327112 | tf_op jit(solution)/shard_map/ppermute | solution.py:426
  19.9 31.6 %collective-permute-start.8 = (bf16[192,896]{1,0:T(8,128)(2,1)}, bf16[192,896]{1,0:T(8,128)(2,1)S(1)}, u32[]{:S(2)}, u32[]{:S(2)}) collective-permute-start(bf16[192,896]{1,0:T(8,128)(2,1)} %get-tuple-element.487), channel_id=1, source_target_pairs={{0,24},{4,28},{8,0},{12,4},{16,8},{20,12},{24,16},{28,20},{1,25},{... | collective-permute-start | bytes 1032200 | tf_op jit(solution)/shard_map/ppermute | solution.py:474
  27.5 27.0 %collective-permute-start.6 = (bf16[192,896]{1,0:T(8,128)(2,1)S(1)}, bf16[192,896]{1,0:T(8,128)(2,1)S(1)}, u32[]{:S(2)}, u32[]{:S(2)}) collective-permute-start(bf16[192,896]{1,0:T(8,128)(2,1)S(1)} %get-tuple-element.489), channel_id=1, source_target_pairs={{0,16},{4,20},{8,24},{12,28},{16,0},{20,4},{24,8},{28,12},{1,17},{... | collective-permute-start | bytes 1032200 | tf_op jit(solution)/shard_map/ppermute | solution.py:474
  44.1 52.5 %collective-permute-start.1 = (bf16[256,1536]{1,0:T(8,128)(2,1)S(1)}, bf16[256,1536]{1,0:T(8,128)(2,1)}, u32[]{:S(2)}, u32[]{:S(2)}) collective-permute-start(bf16[256,1536]{1,0:T(8,128)(2,1)S(1)} %get-tuple-element.441), channel_id=1, source_target_pairs={{0,1},{1,0},{2,3},{3,2},{4,5},{5,4},{6,7},{7,6},{8,9},{9,8},{10,11... | collective-permute-start | bytes 2359304 | tf_op jit(solution)/shard_map/ppermute | solution.py:423
  44.1 45.0 %all-to-all-start = ((bf16[4,192,1024]{2,1,0:T(8,128)(2,1)}), bf16[4,192,1024]{2,1,0:T(8,128)(2,1)}, u32[]{:S(2)}, u32[]{:S(2)}) async-start(bf16[4,192,1024]{2,1,0:T(8,128)(2,1)} %pad_maximum_fusion.10), calls=%async_computation | async-start | bytes 3145728 | tf_op jit(solution)/shard_map/all_to_all | solution.py:533
  51.4 35.2 %collective-permute-start = (bf16[256,1536]{1,0:T(8,128)(2,1)S(1)}, bf16[256,1536]{1,0:T(8,128)(2,1)}, u32[]{:S(2)}, u32[]{:S(2)}) collective-permute-start(bf16[256,1536]{1,0:T(8,128)(2,1)S(1)} %get-tuple-element.441), channel_id=1, source_target_pairs={{0,2},{2,0},{1,3},{3,1},{4,6},{6,4},{5,7},{7,5},{8,10},{10,8},{9,1... | collective-permute-start | bytes 2359304 | tf_op jit(solution)/shard_map/ppermute | solution.py:423
  89.2 40.3 %all-to-all-start.1 = ((bf16[4,192,1024]{2,1,0:T(8,128)(2,1)}), bf16[4,192,1024]{2,1,0:T(8,128)(2,1)S(1)}, u32[]{:S(2)}, u32[]{:S(2)}) async-start(bf16[4,192,1024]{2,1,0:T(8,128)(2,1)} %pad_maximum_fusion.11), calls=%async_computation.1 | async-start | bytes 3145728 | tf_op jit(solution)/shard_map/all_to_all | solution.py:533
  98.6 42.8 %collective-permute-start.18 = (bf16[4,192,1024]{2,1,0:T(8,128)(2,1)}, bf16[4,192,1024]{2,1,0:T(8,128)(2,1)}, u32[]{:S(2)}, u32[]{:S(2)}) collective-permute-start(bf16[4,192,1024]{2,1,0:T(8,128)(2,1)} %all-to-all-done), channel_id=1, source_target_pairs={{0,4},{4,0},{8,12},{12,8},{16,20},{20,16},{24,28},{28,24},{1,5},{5... | collective-permute-start | bytes 4718600 | tf_op jit(solution)/shard_map/ppermute | solution.py:524
  133.5 28.8 %collective-permute-start.13 = (bf16[512,1536]{1,0:T(8,128)(2,1)}, bf16[512,1536]{1,0:T(8,128)(2,1)S(1)}, u32[]{:S(2)}, u32[]{:S(2)}) collective-permute-start(bf16[512,1536]{1,0:T(8,128)(2,1)} %slice.464), channel_id=1, source_target_pairs={{0,1},{1,0},{2,3},{3,2},{4,5},{5,4},{6,7},{7,6},{8,9},{9,8},{10,11... | collective-permute-start | bytes 4718600 | tf_op jit(solution)/shard_map/ppermute | solution.py:423
  135.8 43.3 %all-to-all-start.2 = ((bf16[4,192,1024]{2,1,0:T(8,128)(2,1)}), bf16[4,192,1024]{2,1,0:T(8,128)(2,1)}, u32[]{:S(2)}, u32[]{:S(2)}) async-start(bf16[4,192,1024]{2,1,0:T(8,128)(2,1)} %pad_maximum_fusion.12), calls=%async_computation.2 | async-start | bytes 3145728 | tf_op jit(solution)/shard_map/all_to_all | solution.py:533
  165.1 24.4 %collective-permute-start.14 = (bf16[256,1536]{1,0:T(8,128)(2,1)}, bf16[256,1536]{1,0:T(8,128)(2,1)}, u32[]{:S(2)}, u32[]{:S(2)}) collective-permute-start(bf16[256,1536]{1,0:T(8,128)(2,1)} %add_convert_fusion.5), channel_id=1, source_target_pairs={{0,2},{2,0},{1,3},{3,1},{4,6},{6,4},{5,7},{7,5},{8,10},{10,8},{9,1... | collective-permute-start | bytes 2359304 | tf_op jit(solution)/shard_map/ppermute | solution.py:423
  179.2 34.5 %collective-permute-start.21 = (bf16[4,192,1024]{2,1,0:T(8,128)(2,1)}, bf16[4,192,1024]{2,1,0:T(8,128)(2,1)}, u32[]{:S(2)}, u32[]{:S(2)}) collective-permute-start(bf16[4,192,1024]{2,1,0:T(8,128)(2,1)} %all-to-all-done.2), channel_id=1, source_target_pairs={{0,4},{4,0},{8,12},{12,8},{16,20},{20,16},{24,28},{28,24},{1,5},{5... | collective-permute-start | bytes 4718600 | tf_op jit(solution)/shard_map/ppermute | solution.py:524
  200.7 308.3 %reduce-scatter.8.cloned.1.call-start = ((), (), s32[]{:S(2)}) async-start(), calls=%async_computation.15 | async-start | bytes 1769472 | tf_op jit(solution)/shard_map/reduce_scatter | solution.py:556
  240.4 25.8 %collective-permute-start.23 = (bf16[256,1536]{1,0:T(8,128)(2,1)S(1)}, bf16[256,1536]{1,0:T(8,128)(2,1)S(1)}, u32[]{:S(2)}, u32[]{:S(2)}) collective-permute-start(bf16[256,1536]{1,0:T(8,128)(2,1)S(1)} %add_convert_fusion.4), channel_id=1, source_target_pairs={{0,2},{2,0},{1,3},{3,1},{4,6},{6,4},{5,7},{7,5},{8,10},{10,8},{9,1... | collective-permute-start | bytes 2359304 | tf_op jit(solution)/shard_map/ppermute | solution.py:423
  419.4 112.0 %reduce-scatter.6.cloned.1.call-start = ((), (), s32[]{:S(2)}) async-start(), calls=%async_computation.14 | async-start | bytes 4718592 | tf_op jit(solution)/shard_map/reduce_scatter | solution.py:556
  479.1 96.6 %reduce-scatter.10.cloned.1.call-start = ((), (), s32[]{:S(2)}) async-start(), calls=%async_computation.16 | async-start | bytes 4718592 | tf_op jit(solution)/shard_map/reduce_scatter | solution.py:556
  513.2 111.7 %reduce-scatter.12.cloned.1.call-start = ((), (), s32[]{:S(2)}) async-start(), calls=%async_computation.17 | async-start | bytes 4718592 | tf_op jit(solution)/shard_map/reduce_scatter | solution.py:556
  531.4 41.1 %all-to-all-start.5 = ((bf16[4,192,1024]{2,1,0:T(8,128)(2,1)}), bf16[4,192,1024]{2,1,0:T(8,128)(2,1)}, u32[]{:S(2)}, u32[]{:S(2)}) async-start(bf16[4,192,1024]{2,1,0:T(8,128)(2,1)} %bitcast.216), calls=%async_computation.7 | async-start | bytes 3145728 | tf_op jit(solution)/shard_map/all_to_all | solution.py:533
  575.7 43.6 %all-to-all-start.6 = ((bf16[4,192,1024]{2,1,0:T(8,128)(2,1)}), bf16[4,192,1024]{2,1,0:T(8,128)(2,1)}, u32[]{:S(2)}, u32[]{:S(2)}) async-start(bf16[4,192,1024]{2,1,0:T(8,128)(2,1)} %bitcast.215), calls=%async_computation.9 | async-start | bytes 3145728 | tf_op jit(solution)/shard_map/all_to_all | solution.py:533
  580.3 94.5 %reduce-scatter.14.cloned.1.call-start = ((), (), s32[]{:S(2)}) async-start(), calls=%async_computation.18 | async-start | bytes 3538944 | tf_op jit(solution)/shard_map/reduce_scatter | solution.py:556
  624.8 42.5 %all-to-all-start.7 = ((bf16[4,192,1024]{2,1,0:T(8,128)(2,1)}), bf16[4,192,1024]{2,1,0:T(8,128)(2,1)}, u32[]{:S(2)}, u32[]{:S(2)}) async-start(bf16[4,192,1024]{2,1,0:T(8,128)(2,1)} %bitcast.214), calls=%async_computation.11 | async-start | bytes 3145728 | tf_op jit(solution)/shard_map/all_to_all | solution.py:533
  647.5 39.7 %collective-permute-start.61 = (bf16[288,1536]{1,0:T(8,128)(2,1)}, bf16[288,1536]{1,0:T(8,128)(2,1)}, u32[]{:S(2)}, u32[]{:S(2)}) collective-permute-start(bf16[288,1536]{1,0:T(8,128)(2,1)} %slice.512), channel_id=1, source_target_pairs={{24,25},{25,24},{26,27},{27,26},{28,29},{29,28},{30,31},{31,30}} | collective-permute-start | bytes 2654216 | tf_op jit(solution)/shard_map/ppermute | solution.py:426
  674.8 38.9 %all-to-all-start.8 = ((bf16[4,192,768]{2,1,0:T(8,128)(2,1)}), bf16[4,192,768]{2,1,0:T(8,128)(2,1)S(1)}, u32[]{:S(2)}, u32[]{:S(2)}) async-start(bf16[4,192,768]{2,1,0:T(8,128)(2,1)} %bitcast.217), calls=%async_computation.13 | async-start | bytes 2359296 | tf_op jit(solution)/shard_map/all_to_all | solution.py:533
  (146 other events, 1399.7 us)
Sparse Core Ops, SparseCore 0:
  419.5 28.1 reduce-scatter.7
  479.2 44.7 reduce-scatter.5
  526.3 43.3 reduce-scatter.9
  571.9 43.3 reduce-scatter.11
  624.9 34.3 reduce-scatter.13

commit v6 on v5

--- a/solution.py
+++ b/solution.py
@@ -287,7 +287,7 @@
 
 def token_product(groups, widths, *jobs):
     rows_count = jobs[0][1].shape[1]
-    tile = 256
+    tile = 512
     share = rows_count // groups.count
     step = math.gcd(share, 64)
     offsets, described, operands, specs = {}, [], [], []
@@ -748,7 +748,7 @@
     wide_units = w_gate.shape[1]
     width_all = x_own.shape[1]
     feed_out2, gate2, up2 = feed_call(
-        "feed_forward", feed_kernel, 256, (norm2_all,), feed_weights,
+        "feed_forward", feed_kernel, 512, (norm2_all,), feed_weights,
         ((width_all, BF16), (wide_units, F32), (wide_units, F32)),
     )
     queries = {}

time: 736 us -> 731 us (level)
  transfers between devices with their start and end apart: 84 -> 84, of which waited for: 45 -> 45; matrix products, arithmetic and copies ran while one was open for 23% -> 23% of each run, Pallas kernels for 13% -> 12%
where the time goes in v6:
time: 731 us; the launch traced here: 720 us
  waiting for transfers between devices  255 us (35%)
  starting transfers between devices  124 us (17%)
  Pallas kernels  122 us (17%)
  local copies, waits for them, and re-layouts  82.9 us (11%)
  other arithmetic  75.5 us (10%)
  matrix products  44.9 us (6%)
  between operations  16.1 us (2%)
    ppermute x37, waiting for transfers between devices, tp_swap(): return lax.ppermute(value, 'tp', pairs)  141 us
    dot_general x15, matrix products, dot(): lax.dot_general(left, right, (dims, ((), ())), preferred_element_type=F32)  44.9 us
    pallas_call x3, Pallas kernels, feed_call(): pl.pallas_call(kernel, out_shape=tuple((jax.ShapeDtypeStruct((count, cols...  43.9 us
    all_to_all x9, starting transfers between devices, to_quarters(): lax.all_to_all(blocks, 'grp', 0, 0, tiled=True, axis_index_groups=self.ro...  40.9 us
    pallas_call x5, Pallas kernels, token_product(): pl.pallas_call(partial(product_kernel, groups.quarter, share, step, descr...  39.9 us
    ppermute x37, starting transfers between devices, tp_swap(): return lax.ppermute(value, 'tp', pairs)  32.3 us
    ppermute x6, waiting for transfers between devices, shift(): lax.ppermute(value, 'grp', [(i, (i + hop) % self.count) for i in range(se...  29.8 us
    all_to_all x9, waiting for transfers between devices, to_quarters(): lax.all_to_all(blocks, 'grp', 0, 0, tiled=True, axis_index_groups=self.ro...  29.4 us
  transfers between devices with their start and end apart: 84, of which 45 were waited for; matrix products, arithmetic and copies ran while one was open for 23% of the time, Pallas kernels for 12%

profile of v6, /device:TPU:0, one launch (start us, length us, event | category | flops | bytes accessed | tf_op | source)
XLA Modules:
  0.0 720.2 jit_solution(5412042753532341927)
XLA Ops:
  111.3 16.3 %conditional.3 = ((bf16[1024,192]{1,0:T(8,128)(2,1)S(1)}, f32[8,3,128]{2,1,0:T(4,128)S(1)})) conditional(s32[]{:T(128)} %convert_element_type.348, (s32[]{:T(128)}, bf16[1024,576]{0,1:T(8,128)(2,1)}, s32[1]{0:T(128)}, f32[576,192]{1,0:T(8,128)}, f32[3,1,192]{2,1,0:T(1,128)S(1)}, /*index=5*/f32[3,192,192]{2,1,0:T(8,128)S(1)}) %tuple.229, (s32[1]{0:T(128)}, ...), branch_computations={%region_1.2_spmd, %region_2.3_spmd} | conditional | flops 6586487 | bytes 6129180 | solution.py:743
  113.3 14.3 %enc_forward.1 = (bf16[1024,192]{1,0:T(8,128)(2,1)S(1)}, f32[8,3,128]{2,1,0:T(4,128)S(1)}) custom-call(s32[1]{0:T(128)} %get-tuple-element.71.tp_ref, bf16[1024,576]{1,0:T(8,128)(2,1)S(1)} %copy.126.q_ref.kv_ref, bf16[1024,576]{1,0:T(8,128)(2,1)S(1)} %copy.126.q_ref.kv_ref, f32[1024,128]{1,0:T(8,128)} %get-tuple-element.73.idk_ref, ...), custom_call_target="tpu_custom_call" | custom-call | tf_op jit(solution)/shard_map/cond/branch_1_fun/enc_forward/pallas_call | solution.py:206
  147.2 13.6 %collective-permute-done.19 = bf16[2,192,1024]{2,1,0:T(8,128)(2,1)S(1)} collective-permute-done((bf16[2,192,1024]{2,1,0:T(8,128)(2,1)}, bf16[2,192,1024]{2,1,0:T(8,128)(2,1)S(1)}, u32[]{:S(2)}, u32[]{:S(2)}) %collective-permute-start.19) | collective-permute-done | bytes 786464 | tf_op jit(solution)/shard_map/ppermute | solution.py:524
  180.7 8.8 %collective-permute-done.14 = bf16[256,1536]{1,0:T(8,128)(2,1)} collective-permute-done((bf16[256,1536]{1,0:T(8,128)(2,1)}, bf16[256,1536]{1,0:T(8,128)(2,1)}, u32[]{:S(2)}, u32[]{:S(2)}) %collective-permute-start.14) | collective-permute-done | bytes 786464 | tf_op jit(solution)/shard_map/ppermute | solution.py:423
  219.3 14.5 %feed_forward.1 = (bf16[1024,1536]{1,0:T(8,128)(2,1)S(1)}, f32[1024,1024]{1,0:T(8,128)}, f32[1024,1024]{1,0:T(8,128)}) custom-call(bf16[1024,1536]{1,0:T(8,128)(2,1)} %copy-done.6, bf16[1536,1024]{1,0:T(8,128)(2,1)} %bitcast.202, bf16[1536,1024]{1,0:T(8,128)(2,1)} %bitcast.205, bf16[1536,1024]{1,0:T(8,128)(2,1)} %bitcast.51.wd_ref), custom_call_target="tpu_custom_call" | custom-call | tf_op jit(solution)/shard_map/feed_forward/pallas_call | solution.py:403
  257.3 8.7 %collective-permute-done.23 = bf16[256,1536]{1,0:T(8,128)(2,1)S(1)} collective-permute-done((bf16[256,1536]{1,0:T(8,128)(2,1)S(1)}, bf16[256,1536]{1,0:T(8,128)(2,1)S(1)}, u32[]{:S(2)}, u32[]{:S(2)}) %collective-permute-start.23) | collective-permute-done | bytes 786464 | tf_op jit(solution)/shard_map/ppermute | solution.py:423
  308.1 10.8 %collective-permute-done.35 = bf16[144,1536]{1,0:T(8,128)(2,1)S(1)} collective-permute-done((bf16[144,1536]{1,0:T(8,128)(2,1)S(1)}, bf16[144,1536]{1,0:T(8,128)(2,1)S(1)}, u32[]{:S(2)}, u32[]{:S(2)}) %collective-permute-start.35) | collective-permute-done | bytes 442400 | tf_op jit(solution)/shard_map/ppermute | solution.py:423
  320.9 10.0 %collective-permute-done.36 = bf16[144,1536]{1,0:T(8,128)(2,1)S(1)} collective-permute-done((bf16[144,1536]{1,0:T(8,128)(2,1)S(1)}, bf16[144,1536]{1,0:T(8,128)(2,1)S(1)}, u32[]{:S(2)}, u32[]{:S(2)}) %collective-permute-start.36) | collective-permute-done | bytes 442400 | tf_op jit(solution)/shard_map/ppermute | solution.py:423
  333.9 11.4 %feed_both.1 = (bf16[576,1536]{1,0:T(8,128)(2,1)S(1)}, bf16[576,2048]{1,0:T(8,128)(2,1)}, bf16[576,1024]{1,0:T(8,128)(2,1)S(1)}) custom-call(bf16[576,1536]{1,0:T(8,128)(2,1)} %pad_maximum_fusion.8.tok_ref.refs_2_, f32[576,1024]{1,0:T(8,128)} %fusion.100.gh_ref, bf16[1536,1024]{1,0:T(8,128)(2,1)} %bitcast.203, bf16[1536,1024]{1,0:T(8,128)(2,1)} %bitcast.206), custom_call_target="tpu_custom_call" | custom-call | tf_op jit(solution)/shard_map/feed_both/pallas_call | solution.py:403
  349.5 10.8 %collective-permute-done.40 = bf16[144,1536]{1,0:T(8,128)(2,1)S(1)} collective-permute-done((bf16[144,1536]{1,0:T(8,128)(2,1)S(1)}, bf16[144,1536]{1,0:T(8,128)(2,1)S(1)}, u32[]{:S(2)}, u32[]{:S(2)}) %collective-permute-start.40) | collective-permute-done | bytes 442400 | tf_op jit(solution)/shard_map/ppermute | solution.py:423
  363.5 10.0 %collective-permute-done.41 = bf16[144,1536]{1,0:T(8,128)(2,1)S(1)} collective-permute-done((bf16[144,1536]{1,0:T(8,128)(2,1)S(1)}, bf16[144,1536]{1,0:T(8,128)(2,1)S(1)}, u32[]{:S(2)}, u32[]{:S(2)}) %collective-permute-start.41) | collective-permute-done | bytes 442400 | tf_op jit(solution)/shard_map/ppermute | solution.py:423
  380.7 12.1 %collective-permute-done.44 = bf16[192,192]{1,0:T(8,128)(2,1)S(1)} collective-permute-done((bf16[192,192]{1,0:T(8,128)(2,1)S(1)}, bf16[192,192]{1,0:T(8,128)(2,1)S(1)}, u32[]{:S(2)}, u32[]{:S(2)}) %collective-permute-start.44) | collective-permute-done | bytes 73760 | tf_op jit(solution)/shard_map/ppermute | solution.py:480
  429.1 17.3 %collective-permute-done.52 = bf16[256,1536]{1,0:T(8,128)(2,1)S(1)} collective-permute-done((bf16[256,1536]{1,0:T(8,128)(2,1)S(1)}, bf16[256,1536]{1,0:T(8,128)(2,1)S(1)}, u32[]{:S(2)}, u32[]{:S(2)}) %collective-permute-start.52) | collective-permute-done | bytes 786464 | tf_op jit(solution)/shard_map/ppermute | solution.py:423
  450.6 18.0 %feed_back.1 = (bf16[1024,1536]{1,0:T(8,128)(2,1)}, bf16[1024,2048]{1,0:T(8,128)(2,1)}, bf16[1024,1024]{1,0:T(8,128)(2,1)S(1)}) custom-call(f32[1024,1024]{1,0:T(8,128)} %get-tuple-element.225.gate_ref, f32[1024,1024]{1,0:T(8,128)} %get-tuple-element.226.up_ref, bf16[1024,1536]{1,0:T(8,128)(2,1)} %pad_maximum_fusion.6.ga_ref.refs_0_, ...), custom_call_target="tpu_custom_call" | custom-call | tf_op jit(solution)/shard_map/feed_back/pallas_call | solution.py:403
  469.9 8.0 %token_product.6 = bf16[2,4,192,1024]{3,2,1,0:T(8,128)(2,1)} custom-call(s32[1]{0:T(128)} %bitcast.63.role_ref, bf16[1024,1536]{1,0:T(8,128)(2,1)} %copy-done.6, bf16[1024,2048]{1,0:T(8,128)(2,1)} %get-tuple-element.229.refs_1_, bf16[576,1536]{1,0:T(8,128)(2,1)} %pad_maximum_fusion.8.tok_ref.refs_2_, bf16[576,2048]{1,0:T(8,128)(2,1)} %get-tuple-element.231.refs_3_), custom_call_target="tpu_custom_call" | custom-call | tf_op jit(solution)/shard_map/token_product/pallas_call | solution.py:314
  488.0 8.1 %token_product.7 = bf16[2,4,192,1024]{3,2,1,0:T(8,128)(2,1)} custom-call(s32[1]{0:T(128)} %bitcast.63.role_ref, bf16[1024,1536]{1,0:T(8,128)(2,1)} %copy-done.6, bf16[1024,2048]{1,0:T(8,128)(2,1)} %get-tuple-element.229.refs_1_, bf16[576,1536]{1,0:T(8,128)(2,1)} %pad_maximum_fusion.8.tok_ref.refs_2_, bf16[576,2048]{1,0:T(8,128)(2,1)} %get-tuple-element.231.refs_3_), custom_call_target="tpu_custom_call" | custom-call | tf_op jit(solution)/shard_map/token_product/pallas_call | solution.py:314
  497.6 8.1 %token_product.8 = bf16[2,4,192,1024]{3,2,1,0:T(8,128)(2,1)} custom-call(s32[1]{0:T(128)} %bitcast.63.role_ref, bf16[1024,1536]{1,0:T(8,128)(2,1)} %pad_maximum_fusion.6.ga_ref.refs_0_, bf16[1024,1024]{1,0:T(8,128)(2,1)} %copy-done.2, bf16[576,1536]{1,0:T(8,128)(2,1)} %pad_maximum_fusion.7.refs_2_, bf16[576,1024]{1,0:T(8,128)(2,1)} %copy-done.3), custom_call_target="tpu_custom_call" | custom-call | tf_op jit(solution)/shard_map/token_product/pallas_call | solution.py:314
  537.5 18.0 %collective-permute-done.57 = bf16[256,1536]{1,0:T(8,128)(2,1)S(1)} collective-permute-done((bf16[256,1536]{1,0:T(8,128)(2,1)S(1)}, bf16[256,1536]{1,0:T(8,128)(2,1)S(1)}, u32[]{:S(2)}, u32[]{:S(2)}) %collective-permute-start.57) | collective-permute-done | bytes 786464 | tf_op jit(solution)/shard_map/ppermute | solution.py:423
  577.1 22.5 %conditional.4 = (bf16[1024,576]{1,0:T(8,128)(2,1)S(1)}, f32[3,81920]{1,0:T(4,128)S(1)}) conditional(s32[]{:T(128)} %convert_element_type.348, (s32[]{:T(128)}, bf16[1024,576]{0,1:T(8,128)(2,1)}, f32[8,3,128]{2,1,0:T(4,128)S(1)}, bf16[1024,192]{0,1:T(8,128)(2,1)S(1)}, s32[1]{0:T(128)}, /*index=5*/f32[576,192]{1,0:T(8,128)}, ...), branch_computations={%region_11.12_spmd, %region_12.13_spmd} | conditional | flops 16662647 | bytes 15073380 | solution.py:869
  580.7 17.3 %enc_backward.1 = (bf16[1024,192]{1,0:T(8,128)(2,1)S(1)}, bf16[1024,384]{1,0:T(8,128)(2,1)S(1)}, f32[3,5,128,128]{3,2,1,0:T(8,128)S(1)}) custom-call(s32[1]{0:T(128)} %get-tuple-element.87.tp_ref, bf16[1024,576]{1,0:T(8,128)(2,1)S(1)} %copy.141.q_ref.kv_ref, bf16[1024,576]{1,0:T(8,128)(2,1)S(1)} %copy.141.q_ref.kv_ref, f32[1024,128]{1,0:T(8,128)S(1)} %copy-done.38, ...), custom_call_target="tpu_custom_call" | custom-call | tf_op jit(solution)/shard_map/cond/branch_1_fun/enc_backward/pallas_call | solution.py:244
  599.6 9.7 %token_product.9 = bf16[2,4,192,768]{3,2,1,0:T(8,128)(2,1)} custom-call(s32[1]{0:T(128)} %bitcast.63.role_ref, bf16[1024,1536]{1,0:T(8,128)(2,1)} %copy-done.18, bf16[1024,576]{1,0:T(8,128)(2,1)S(1)} %get-tuple-element.245.refs_1_.refs_5_, bf16[1024,1536]{1,0:T(8,128)(2,1)} %copy-done.21, bf16[1024,192]{1,0:T(8,128)(2,1)} %copy-done.29, ...), custom_call_target="tpu_custom_call" | custom-call | tf_op jit(solution)/shard_map/token_product/pallas_call | solution.py:314
  651.7 11.4 %all-to-all-done.7 = bf16[4,192,1024]{2,1,0:T(8,128)(2,1)} async-done(((bf16[4,192,1024]{2,1,0:T(8,128)(2,1)}), bf16[4,192,1024]{2,1,0:T(8,128)(2,1)}, u32[]{:S(2)}, u32[]{:S(2)}) %all-to-all-start.7) | async-done | bytes 1572896 | tf_op jit(solution)/shard_map/all_to_all | solution.py:533
  685.0 9.1 %collective-permute-done.69 = f32[40,128]{1,0:T(8,128)S(1)} collective-permute-done((f32[40,128]{1,0:T(8,128)S(1)}, f32[40,128]{1,0:T(8,128)S(1)}, u32[]{:S(2)}, u32[]{:S(2)}) %collective-permute-start.69) | collective-permute-done | bytes 20512 | tf_op jit(solution)/shard_map/ppermute | solution.py:474
  694.2 10.2 %collective-permute-done.68 = f32[40,128]{1,0:T(8,128)S(1)} collective-permute-done((f32[40,128]{1,0:T(8,128)S(1)}, f32[40,128]{1,0:T(8,128)S(1)}, u32[]{:S(2)}, u32[]{:S(2)}) %collective-permute-start.68) | collective-permute-done | bytes 20512 | tf_op jit(solution)/shard_map/ppermute | solution.py:474
  (541 shorter events, 449.7 us)
Async XLA Ops:
  7.2 86.7 %collective-permute-start.11 = (bf16[144,1536]{1,0:T(8,128)(2,1)}, bf16[144,1536]{1,0:T(8,128)(2,1)}, u32[]{:S(2)}, u32[]{:S(2)}) collective-permute-start(bf16[144,1536]{1,0:T(8,128)(2,1)} %bitcast.211), channel_id=1, source_target_pairs={{24,25},{25,24},{26,27},{27,26},{28,29},{29,28},{30,31},{31,30}} | collective-permute-start | bytes 1327112 | tf_op jit(solution)/shard_map/ppermute | solution.py:426
  8.7 68.1 %collective-permute-start.10 = (bf16[144,1536]{1,0:T(8,128)(2,1)}, bf16[144,1536]{1,0:T(8,128)(2,1)}, u32[]{:S(2)}, u32[]{:S(2)}) collective-permute-start(bf16[144,1536]{1,0:T(8,128)(2,1)} %bitcast.212), channel_id=1, source_target_pairs={{24,26},{26,24},{25,27},{27,25},{28,30},{30,28},{29,31},{31,29}} | collective-permute-start | bytes 1327112 | tf_op jit(solution)/shard_map/ppermute | solution.py:426
  19.9 31.6 %collective-permute-start.8 = (bf16[192,896]{1,0:T(8,128)(2,1)}, bf16[192,896]{1,0:T(8,128)(2,1)S(1)}, u32[]{:S(2)}, u32[]{:S(2)}) collective-permute-start(bf16[192,896]{1,0:T(8,128)(2,1)} %get-tuple-element.487), channel_id=1, source_target_pairs={{0,24},{4,28},{8,0},{12,4},{16,8},{20,12},{24,16},{28,20},{1,25},{... | collective-permute-start | bytes 1032200 | tf_op jit(solution)/shard_map/ppermute | solution.py:474
  27.5 27.0 %collective-permute-start.6 = (bf16[192,896]{1,0:T(8,128)(2,1)S(1)}, bf16[192,896]{1,0:T(8,128)(2,1)S(1)}, u32[]{:S(2)}, u32[]{:S(2)}) collective-permute-start(bf16[192,896]{1,0:T(8,128)(2,1)S(1)} %get-tuple-element.489), channel_id=1, source_target_pairs={{0,16},{4,20},{8,24},{12,28},{16,0},{20,4},{24,8},{28,12},{1,17},{... | collective-permute-start | bytes 1032200 | tf_op jit(solution)/shard_map/ppermute | solution.py:474
  44.1 52.5 %collective-permute-start.1 = (bf16[256,1536]{1,0:T(8,128)(2,1)S(1)}, bf16[256,1536]{1,0:T(8,128)(2,1)}, u32[]{:S(2)}, u32[]{:S(2)}) collective-permute-start(bf16[256,1536]{1,0:T(8,128)(2,1)S(1)} %get-tuple-element.441), channel_id=1, source_target_pairs={{0,1},{1,0},{2,3},{3,2},{4,5},{5,4},{6,7},{7,6},{8,9},{9,8},{10,11... | collective-permute-start | bytes 2359304 | tf_op jit(solution)/shard_map/ppermute | solution.py:423
  44.1 45.0 %all-to-all-start = ((bf16[4,192,1024]{2,1,0:T(8,128)(2,1)}), bf16[4,192,1024]{2,1,0:T(8,128)(2,1)}, u32[]{:S(2)}, u32[]{:S(2)}) async-start(bf16[4,192,1024]{2,1,0:T(8,128)(2,1)} %pad_maximum_fusion.10), calls=%async_computation | async-start | bytes 3145728 | tf_op jit(solution)/shard_map/all_to_all | solution.py:533
  51.4 35.2 %collective-permute-start = (bf16[256,1536]{1,0:T(8,128)(2,1)S(1)}, bf16[256,1536]{1,0:T(8,128)(2,1)}, u32[]{:S(2)}, u32[]{:S(2)}) collective-permute-start(bf16[256,1536]{1,0:T(8,128)(2,1)S(1)} %get-tuple-element.441), channel_id=1, source_target_pairs={{0,2},{2,0},{1,3},{3,1},{4,6},{6,4},{5,7},{7,5},{8,10},{10,8},{9,1... | collective-permute-start | bytes 2359304 | tf_op jit(solution)/shard_map/ppermute | solution.py:423
  89.2 40.3 %all-to-all-start.1 = ((bf16[4,192,1024]{2,1,0:T(8,128)(2,1)}), bf16[4,192,1024]{2,1,0:T(8,128)(2,1)S(1)}, u32[]{:S(2)}, u32[]{:S(2)}) async-start(bf16[4,192,1024]{2,1,0:T(8,128)(2,1)} %pad_maximum_fusion.11), calls=%async_computation.1 | async-start | bytes 3145728 | tf_op jit(solution)/shard_map/all_to_all | solution.py:533
  98.6 42.9 %collective-permute-start.18 = (bf16[4,192,1024]{2,1,0:T(8,128)(2,1)}, bf16[4,192,1024]{2,1,0:T(8,128)(2,1)}, u32[]{:S(2)}, u32[]{:S(2)}) collective-permute-start(bf16[4,192,1024]{2,1,0:T(8,128)(2,1)} %all-to-all-done), channel_id=1, source_target_pairs={{0,4},{4,0},{8,12},{12,8},{16,20},{20,16},{24,28},{28,24},{1,5},{5... | collective-permute-start | bytes 4718600 | tf_op jit(solution)/shard_map/ppermute | solution.py:524
  133.5 28.7 %collective-permute-start.13 = (bf16[512,1536]{1,0:T(8,128)(2,1)}, bf16[512,1536]{1,0:T(8,128)(2,1)S(1)}, u32[]{:S(2)}, u32[]{:S(2)}) collective-permute-start(bf16[512,1536]{1,0:T(8,128)(2,1)} %slice.464), channel_id=1, source_target_pairs={{0,1},{1,0},{2,3},{3,2},{4,5},{5,4},{6,7},{7,6},{8,9},{9,8},{10,11... | collective-permute-start | bytes 4718600 | tf_op jit(solution)/shard_map/ppermute | solution.py:423
  135.8 43.3 %all-to-all-start.2 = ((bf16[4,192,1024]{2,1,0:T(8,128)(2,1)}), bf16[4,192,1024]{2,1,0:T(8,128)(2,1)}, u32[]{:S(2)}, u32[]{:S(2)}) async-start(bf16[4,192,1024]{2,1,0:T(8,128)(2,1)} %pad_maximum_fusion.12), calls=%async_computation.2 | async-start | bytes 3145728 | tf_op jit(solution)/shard_map/all_to_all | solution.py:533
  165.1 24.4 %collective-permute-start.14 = (bf16[256,1536]{1,0:T(8,128)(2,1)}, bf16[256,1536]{1,0:T(8,128)(2,1)}, u32[]{:S(2)}, u32[]{:S(2)}) collective-permute-start(bf16[256,1536]{1,0:T(8,128)(2,1)} %add_convert_fusion.5), channel_id=1, source_target_pairs={{0,2},{2,0},{1,3},{3,1},{4,6},{6,4},{5,7},{7,5},{8,10},{10,8},{9,1... | collective-permute-start | bytes 2359304 | tf_op jit(solution)/shard_map/ppermute | solution.py:423
  179.2 34.5 %collective-permute-start.21 = (bf16[4,192,1024]{2,1,0:T(8,128)(2,1)}, bf16[4,192,1024]{2,1,0:T(8,128)(2,1)}, u32[]{:S(2)}, u32[]{:S(2)}) collective-permute-start(bf16[4,192,1024]{2,1,0:T(8,128)(2,1)} %all-to-all-done.2), channel_id=1, source_target_pairs={{0,4},{4,0},{8,12},{12,8},{16,20},{20,16},{24,28},{28,24},{1,5},{5... | collective-permute-start | bytes 4718600 | tf_op jit(solution)/shard_map/ppermute | solution.py:524
  200.7 305.0 %reduce-scatter.8.cloned.1.call-start = ((), (), s32[]{:S(2)}) async-start(), calls=%async_computation.15 | async-start | bytes 1769472 | tf_op jit(solution)/shard_map/reduce_scatter | solution.py:556
  240.2 25.8 %collective-permute-start.23 = (bf16[256,1536]{1,0:T(8,128)(2,1)S(1)}, bf16[256,1536]{1,0:T(8,128)(2,1)S(1)}, u32[]{:S(2)}, u32[]{:S(2)}) collective-permute-start(bf16[256,1536]{1,0:T(8,128)(2,1)S(1)} %add_convert_fusion.4), channel_id=1, source_target_pairs={{0,2},{2,0},{1,3},{3,1},{4,6},{6,4},{5,7},{7,5},{8,10},{10,8},{9,1... | collective-permute-start | bytes 2359304 | tf_op jit(solution)/shard_map/ppermute | solution.py:423
  418.2 109.9 %reduce-scatter.6.cloned.1.call-start = ((), (), s32[]{:S(2)}) async-start(), calls=%async_computation.14 | async-start | bytes 4718592 | tf_op jit(solution)/shard_map/reduce_scatter | solution.py:556
  477.9 94.6 %reduce-scatter.10.cloned.1.call-start = ((), (), s32[]{:S(2)}) async-start(), calls=%async_computation.16 | async-start | bytes 4718592 | tf_op jit(solution)/shard_map/reduce_scatter | solution.py:556
  509.8 110.7 %reduce-scatter.12.cloned.1.call-start = ((), (), s32[]{:S(2)}) async-start(), calls=%async_computation.17 | async-start | bytes 4718592 | tf_op jit(solution)/shard_map/reduce_scatter | solution.py:556
  528.1 41.1 %all-to-all-start.5 = ((bf16[4,192,1024]{2,1,0:T(8,128)(2,1)}), bf16[4,192,1024]{2,1,0:T(8,128)(2,1)}, u32[]{:S(2)}, u32[]{:S(2)}) async-start(bf16[4,192,1024]{2,1,0:T(8,128)(2,1)} %bitcast.216), calls=%async_computation.7 | async-start | bytes 3145728 | tf_op jit(solution)/shard_map/all_to_all | solution.py:533
  572.4 42.5 %all-to-all-start.6 = ((bf16[4,192,1024]{2,1,0:T(8,128)(2,1)}), bf16[4,192,1024]{2,1,0:T(8,128)(2,1)}, u32[]{:S(2)}, u32[]{:S(2)}) async-start(bf16[4,192,1024]{2,1,0:T(8,128)(2,1)} %bitcast.215), calls=%async_computation.9 | async-start | bytes 3145728 | tf_op jit(solution)/shard_map/all_to_all | solution.py:533
  577.0 93.7 %reduce-scatter.14.cloned.1.call-start = ((), (), s32[]{:S(2)}) async-start(), calls=%async_computation.18 | async-start | bytes 3538944 | tf_op jit(solution)/shard_map/reduce_scatter | solution.py:556
  620.5 42.5 %all-to-all-start.7 = ((bf16[4,192,1024]{2,1,0:T(8,128)(2,1)}), bf16[4,192,1024]{2,1,0:T(8,128)(2,1)}, u32[]{:S(2)}, u32[]{:S(2)}) async-start(bf16[4,192,1024]{2,1,0:T(8,128)(2,1)} %bitcast.214), calls=%async_computation.11 | async-start | bytes 3145728 | tf_op jit(solution)/shard_map/all_to_all | solution.py:533
  643.6 39.5 %collective-permute-start.61 = (bf16[288,1536]{1,0:T(8,128)(2,1)}, bf16[288,1536]{1,0:T(8,128)(2,1)}, u32[]{:S(2)}, u32[]{:S(2)}) collective-permute-start(bf16[288,1536]{1,0:T(8,128)(2,1)} %slice.512), channel_id=1, source_target_pairs={{24,25},{25,24},{26,27},{27,26},{28,29},{29,28},{30,31},{31,30}} | collective-permute-start | bytes 2654216 | tf_op jit(solution)/shard_map/ppermute | solution.py:426
  670.7 38.8 %all-to-all-start.8 = ((bf16[4,192,768]{2,1,0:T(8,128)(2,1)}), bf16[4,192,768]{2,1,0:T(8,128)(2,1)S(1)}, u32[]{:S(2)}, u32[]{:S(2)}) async-start(bf16[4,192,768]{2,1,0:T(8,128)(2,1)} %bitcast.217), calls=%async_computation.13 | async-start | bytes 2359296 | tf_op jit(solution)/shard_map/all_to_all | solution.py:533
  (146 other events, 1399.3 us)
Sparse Core Ops, SparseCore 0:
  418.3 27.7 reduce-scatter.7
  478.0 43.6 reduce-scatter.5
  524.0 43.3 reduce-scatter.9
  569.6 43.3 reduce-scatter.11
  620.6 34.3 reduce-scatter.13
